TPU v7x, 32 devices: a whole 2x2x4 slice. The times are simulated.
32 devices in a mesh: branch: 2 (over core), seq: 4 (over z), head: 4 (over y, x).
Axes of the slice: x: 2, y: 2, z: 4, core: 2. Of those that a mesh axis runs over, the one named last changes fastest.
Arguments:
- tokens: bfloat16 [1024, 3072], P('seq', 'head'), may hold values from -10 to 10
- valid_counts: int32 [4], P('seq'), may hold values from 1 to 256, 768 in all
- shared_qkv: bfloat16 [3072, 3, 1536], P('branch', None, 'head'), may hold values from -0.08479832 to 0.08479832
- shared_out: bfloat16 [1536, 3072], P('head', 'branch'), may hold values from -0.15625 to 0.15625
- skipped_qkv: bfloat16 [3072, 3, 1536], P('branch', None, 'head'), may hold values from -0.08479832 to 0.08479832
- skipped_out: bfloat16 [1536, 3072], P('head', 'branch'), may hold values from -0.15625 to 0.15625
- modulation: float32 [2, 3, 3072], replicated, may hold values from -3 to 3
- qk_gains: float32 [2, 2, 128], replicated, may hold values from 1.2 to 5.5
Outputs:
- branches: bfloat16 [2, 1024, 3072], P('branch', 'seq', 'head')
Inputs may be any that keep to these rules, and one draw needn't show every extreme that they name: `valid_counts`: each entry counts the leading real tokens of one shard of 256 slots; the rest are padding. The entries sum to 768 and one of them equals 256.
All inputs are finite; a program needn't handle non-finite values.
Results may differ from a plain program's by a relative error of at most 0.01.
Values may be sent and summed in bfloat16 or wider, within the bound.
No kernel may reach another device: no remote copies, remote signals or barrier semaphores. Data moves between devices by JAX's collectives and lax.ppermute only.
A program may use at most 128 MiB of HBM per device.

v0:
```python
import jax
import jax.numpy as jnp
from jax import lax
from jax.sharding import PartitionSpec as P

HEAD_DIM = 128


def modulate(x_rows, mod):
    whole = lax.all_gather(x_rows, "head", axis=1, tiled=True)
    xf = whole.astype(jnp.float32)
    mean = jnp.mean(xf, axis=1, keepdims=True)
    centered = xf - mean
    var = jnp.mean(centered * centered, axis=1, keepdims=True)
    normed = centered * lax.rsqrt(var + 1e-06)
    return (normed * (1.0 + mod[1]) + mod[0]).astype(jnp.bfloat16)


def attend_block(x_full, keep_full, qkv_weight, out_weight, mod, gains):
    rows, quarter = x_full.shape
    width = qkv_weight.shape[2]
    group = width // HEAD_DIM
    moded = modulate(x_full, mod)
    qkv = jnp.einsum(
        "rd,dsc->rsc",
        moded,
        lax.all_gather(qkv_weight, "branch", axis=0, tiled=True),
        preferred_element_type=jnp.float32,
    )
    qpart = qkv[:, 0].reshape(rows, group, HEAD_DIM)
    kpart = qkv[:, 1].reshape(rows, group, HEAD_DIM)
    query = (
        qpart * lax.rsqrt(jnp.mean(qpart * qpart, axis=2, keepdims=True) + 1e-06) * gains[0]
    ).astype(jnp.bfloat16)
    key = (
        kpart * lax.rsqrt(jnp.mean(kpart * kpart, axis=2, keepdims=True) + 1e-06) * gains[1]
    ).astype(jnp.bfloat16)
    key = key.reshape(rows, width)
    value = qkv[:, 2].astype(jnp.bfloat16)
    scale = 1.0 / HEAD_DIM**0.5
    keep_wire = keep_full.astype(jnp.bfloat16)
    peak = jnp.full((group, rows), -1e30, jnp.float32)
    key_piece = lax.all_gather(key, "seq", axis=0, tiled=True)
    value_piece = lax.all_gather(value, "seq", axis=0, tiled=True)
    keep_piece = lax.all_gather(keep_wire, "seq", axis=0, tiled=True)
    length = key_piece.shape[0]
    key_heads = key_piece.reshape(length, group, HEAD_DIM)
    value_heads = value_piece.reshape(length, group, HEAD_DIM)
    scores = (
        jnp.einsum("rhd,nhd->hrn", query, key_heads, preferred_element_type=jnp.float32) * scale
    )
    valid = keep_piece[None, None, :] > 0.5
    scores = jnp.where(valid, scores, -1e30)
    new_peak = jnp.maximum(peak, jnp.max(scores, axis=2))
    weights = jnp.where(valid, jnp.exp(scores - new_peak[:, :, None]), 0.0)
    total = jnp.sum(weights, axis=2)
    mixed = jnp.einsum(
        "hrn,nhd->hrd",
        weights.astype(jnp.bfloat16),
        value_heads,
        preferred_element_type=jnp.float32,
    )
    attended = (mixed / total[:, :, None]).astype(jnp.bfloat16)
    attended = attended.transpose(1, 0, 2).reshape(rows, width)
    projected = jnp.dot(
        attended,
        lax.all_gather(out_weight, "branch", axis=1, tiled=True),
        preferred_element_type=jnp.float32,
    )
    mine = lax.psum_scatter(projected, "head", scatter_dimension=1, tiled=True)
    gate = lax.dynamic_slice_in_dim(mod[2], lax.axis_index("head") * quarter, quarter, 0)
    return (x_full.astype(jnp.float32) + gate[None, :] * mine).astype(jnp.bfloat16)


def full_block(x_full, keep_full, qkv_weight, out_weight, mod, gains):
    updated = attend_block(x_full, keep_full, qkv_weight, out_weight, mod, gains)
    return updated


def per_device(
    tokens, valid_counts, shared_qkv, shared_out, skipped_qkv, skipped_out, modulation, qk_gains
):
    rows = tokens.shape[0]
    positions = jnp.arange(rows, dtype=jnp.int32)
    keep_all = (positions < valid_counts[0]).astype(jnp.float32)
    forked = full_block(tokens, keep_all, shared_qkv, shared_out, modulation[0], qk_gains[0])
    strong = full_block(forked, keep_all, skipped_qkv, skipped_out, modulation[1], qk_gains[1])
    result = jnp.where(lax.axis_index("branch") == 0, strong, forked)
    return result[None]


def solution(mesh):
    in_specs = (
        P("seq", "head"),
        P("seq"),
        P("branch", None, "head"),
        P("head", "branch"),
        P("branch", None, "head"),
        P("head", "branch"),
        P(),
        P(),
    )
    out_specs = P("branch", "seq", "head")
    return jax.shard_map(
        per_device, mesh=mesh, in_specs=in_specs, out_specs=out_specs, check_vma=False
    )
```

profile of v0, /device:TPU:0, one launch (start us, length us, event | category | flops | bytes accessed | tf_op | source)
XLA Modules:
  0.0 313.8 jit_solution(11347913517500845164)
XLA Ops:
  6.5 0.7 all-gather.10.cloned.1.call-update
  7.3 0.7 all-gather.12.cloned.1.call-update
  8.1 0.7 all-gather.14.cloned.1.call-update
  9.6 12.7 %all-gather.2 = bf16[4,1,256]{2,1,0:T(2,128)(2,1)S(1)} all-gather(bf16[1,1,256]{2,1,0:T(2,128)(2,1)S(1)} %reshape.146), channel_id=1, replica_groups=mesh['branch'=2,'seq'=4,'head'=4] {'seq'}, dimensions={0}, use_global_device_ids=true | all-gather | bytes 2560 | tf_op jit(solution)/shard_map/all_gather | solution.py:45
  22.3 20.5 %all-gather.10.cloned.1.call-done = bf16[256,3072]{1,0:T(8,128)(2,1)} async-done(((bf16[256,768]{1,0:T(8,128)(2,1)}), bf16[256,3072]{1,0:T(8,128)(2,1)}) %all-gather.10.cloned.1.call-update) | async-done | bytes 1572880 | tf_op jit(solution)/shard_map/all_gather | solution.py:10
  42.8 1.8 convert_reduce_fusion.1
  44.6 2.0 fusion.8
  46.6 15.7 %all-gather.12.cloned.1.call-done = bf16[3072,3,384]{2,0,1:T(8,128)(2,1)} async-done(((bf16[1536,3,384]{2,0,1:T(8,128)(2,1)}), bf16[3072,3,384]{2,0,1:T(8,128)(2,1)}) %all-gather.12.cloned.1.call-update) | async-done | bytes 7077904 | tf_op jit(solution)/shard_map/all_gather | solution.py:27
  62.3 5.3 %fusion.19 = f32[256,3,384]{2,0,1:T(8,128)S(1)} fusion(bf16[3072,3,384]{2,0,1:T(8,128)(2,1)} %all-gather.12.cloned.1.call-done, bf16[256,3072]{1,0:T(8,128)(2,1)S(1)} %copy-done, f32[3072]{0:T(1024)S(1)} %bitcast.90, f32[3072]{0:T(1024)S(1)} %bitcast.91, f32[256]{0:T(256)S(1)} %add_rsqrt_fusion.5, f32[256]{0:T(256)S(1)} %broadcast_multiply_fusion.1), kind=kOutput, calls=%fused_computation.27 | convolution fusion | flops 1816657920 | bytes 9857024 | tf_op jit(solution)/shard_map/rd,dsc->rsc/dot_general | solution.py:24
  68.1 19.8 %all_gather.37 = bf16[1024,384]{1,0:T(8,128)(2,1)S(1)} all-gather(bf16[256,384]{1,0:T(8,128)(2,1)S(1)} %fusion.61), channel_id=1, replica_groups=mesh['branch'=2,'seq'=4,'head'=4] {'seq'}, dimensions={0}, use_global_device_ids=true | all-gather | bytes 983040 | tf_op jit(solution)/shard_map/all_gather | solution.py:43
  88.4 18.0 %all-gather = bf16[1024,1,384]{2,0,1:T(8,128)(2,1)S(1)} all-gather(bf16[256,1,384]{2,0,1:T(8,128)(2,1)S(1)} %slice.109), channel_id=2, replica_groups=mesh['branch'=2,'seq'=4,'head'=4] {'seq'}, dimensions={0}, use_global_device_ids=true | all-gather | bytes 983040 | tf_op jit(solution)/shard_map/all_gather | solution.py:44
  106.8 0.8 fusion.12
  107.6 0.9 fusion.14
  108.5 0.9 fusion.53
  109.5 4.4 %fusion.78 = f32[256,3072]{1,0:T(8,128)} fusion(bf16[256,384]{0,1:T(8,128)(2,1)S(1)} %bitcast.87, bf16[384,3072]{1,0:T(8,128)(2,1)} %all-gather.14.cloned.1.call-done), kind=kOutput, calls=%fused_computation.104 | convolution fusion | flops 603979776 | bytes 5701632 | tf_op jit(solution)/shard_map/dot_general | solution.py:65
  114.0 43.3 %reduce-scatter.3.cloned.1.call-done = f32[256,768]{1,0:T(8,128)} async-done(((f32[256,3072]{1,0:T(8,128)}), f32[256,768]{1,0:T(8,128)}) %reduce-scatter.3.cloned.1.call-update) | async-done | bytes 786448 | tf_op jit(solution)/shard_map/reduce_scatter | solution.py:70
  157.3 2.0 add_convert_fusion.1
  159.4 0.5 all-gather.18.cloned.1.call-update
  159.9 0.7 all-gather.20.cloned.1.call-update
  160.7 29.6 %all-gather.16.cloned.1.call-done = bf16[256,3072]{1,0:T(8,128)(2,1)} async-done(((bf16[256,768]{1,0:T(8,128)(2,1)}), bf16[256,3072]{1,0:T(8,128)(2,1)}) %all-gather.16.cloned.1.call-update) | async-done | bytes 1572880 | tf_op jit(solution)/shard_map/all_gather | solution.py:10
  190.3 1.8 convert_reduce_fusion
  192.2 2.0 fusion.4
  194.1 15.5 %all-gather.18.cloned.1.call-done = bf16[3072,3,384]{2,0,1:T(8,128)(2,1)} async-done(((bf16[1536,3,384]{2,0,1:T(8,128)(2,1)}), bf16[3072,3,384]{2,0,1:T(8,128)(2,1)}) %all-gather.18.cloned.1.call-update) | async-done | bytes 7077904 | tf_op jit(solution)/shard_map/all_gather | solution.py:27
  209.7 5.3 %fusion.22 = f32[256,3,384]{2,0,1:T(8,128)S(1)} fusion(bf16[3072,3,384]{2,0,1:T(8,128)(2,1)} %all-gather.18.cloned.1.call-done, bf16[256,3072]{1,0:T(8,128)(2,1)S(1)} %copy-done.1, f32[3072]{0:T(1024)S(1)} %bitcast.88, f32[3072]{0:T(1024)S(1)} %bitcast.89, f32[256]{0:T(256)S(1)} %add_rsqrt_fusion.4, f32[256]{0:T(256)S(1)} %broadcast_multiply_fusion), kind=kOutput, calls=%fused_computation.29 | convolution fusion | flops 1816657920 | bytes 9857024 | tf_op jit(solution)/shard_map/rd,dsc->rsc/dot_general | solution.py:24
  215.5 19.8 %all_gather.42 = bf16[1024,384]{1,0:T(8,128)(2,1)S(1)} all-gather(bf16[256,384]{1,0:T(8,128)(2,1)S(1)} %fusion.59), channel_id=1, replica_groups=mesh['branch'=2,'seq'=4,'head'=4] {'seq'}, dimensions={0}, use_global_device_ids=true | all-gather | bytes 983040 | tf_op jit(solution)/shard_map/all_gather | solution.py:43
  235.8 18.2 %all-gather.1 = bf16[1024,1,384]{2,0,1:T(8,128)(2,1)S(1)} all-gather(bf16[256,1,384]{2,0,1:T(8,128)(2,1)S(1)} %slice.108), channel_id=3, replica_groups=mesh['branch'=2,'seq'=4,'head'=4] {'seq'}, dimensions={0}, use_global_device_ids=true | all-gather | bytes 983040 | tf_op jit(solution)/shard_map/all_gather | solution.py:44
  254.4 0.8 fusion.13
  255.2 0.9 fusion.16
  256.1 0.9 fusion.47
  257.1 4.4 %fusion.79 = f32[256,3072]{1,0:T(8,128)} fusion(bf16[256,384]{0,1:T(8,128)(2,1)S(1)} %bitcast.86, bf16[384,3072]{1,0:T(8,128)(2,1)} %all-gather.20.cloned.1.call-done), kind=kOutput, calls=%fused_computation.105 | convolution fusion | flops 603979776 | bytes 5701632 | tf_op jit(solution)/shard_map/dot_general | solution.py:65
  261.5 43.4 %reduce-scatter.5.cloned.1.call-done = f32[256,768]{1,0:T(8,128)} async-done(((f32[256,3072]{1,0:T(8,128)}), f32[256,768]{1,0:T(8,128)}) %reduce-scatter.5.cloned.1.call-update) | async-done | bytes 786448 | tf_op jit(solution)/shard_map/reduce_scatter | solution.py:70
  304.9 2.0 fusion.57
  (67 shorter events, 3.2 us)
Async XLA Ops:
  6.5 2.3 copy-start.4
  6.5 2.3 copy-start.5
  6.5 36.2 %all-gather.10.cloned.1.call-start = ((), (), s32[]{:S(2)}) async-start(), calls=%async_computation.2 | async-start | bytes 1966080 | tf_op jit(solution)/shard_map/all_gather | solution.py:10
  7.3 55.0 %all-gather.12.cloned.1.call-start = ((), (), s32[]{:S(2)}) async-start(), calls=%async_computation.3 | async-start | bytes 10616832 | tf_op jit(solution)/shard_map/all_gather | solution.py:27
  8.0 101.5 %all-gather.14.cloned.1.call-start = ((), (), s32[]{:S(2)}) async-start(), calls=%async_computation.4 | async-start | bytes 3538944 | tf_op jit(solution)/shard_map/all_gather | solution.py:67
  8.7 148.6 %reduce-scatter.3.cloned.1.call-start = ((), (), s32[]{:S(2)}) async-start(), calls=%async_computation.5 | async-start | bytes 3932160 | tf_op jit(solution)/shard_map/reduce_scatter | solution.py:70
  42.8 19.5 %copy-start = (bf16[256,3072]{1,0:T(8,128)(2,1)S(1)}, bf16[256,3072]{1,0:T(8,128)(2,1)}, u32[]{:S(2)}) copy-start(bf16[256,3072]{1,0:T(8,128)(2,1)} %all-gather.10.cloned.1.call-done) | copy-start | bytes 4718596
  109.5 47.8 %copy-start.3 = (bf16[256,768]{1,0:T(8,128)(2,1)S(1)}, bf16[256,768]{1,0:T(8,128)(2,1)}, u32[]{:S(2)}) copy-start(bf16[256,768]{1,0:T(8,128)(2,1)} %param.8) | copy-start | bytes 1179652
  113.9 76.4 %all-gather.16.cloned.1.call-start = ((), (), s32[]{:S(2)}) async-start(), calls=%async_computation.6 | async-start | bytes 1966080 | tf_op jit(solution)/shard_map/all_gather | solution.py:10
  159.3 50.4 %all-gather.18.cloned.1.call-start = ((), (), s32[]{:S(2)}) async-start(), calls=%async_computation.7 | async-start | bytes 10616832 | tf_op jit(solution)/shard_map/all_gather | solution.py:27
  159.9 97.1 %all-gather.20.cloned.1.call-start = ((), (), s32[]{:S(2)}) async-start(), calls=%async_computation.8 | async-start | bytes 3538944 | tf_op jit(solution)/shard_map/all_gather | solution.py:67
  160.6 144.3 %reduce-scatter.5.cloned.1.call-start = ((), (), s32[]{:S(2)}) async-start(), calls=%async_computation.9 | async-start | bytes 3932160 | tf_op jit(solution)/shard_map/reduce_scatter | solution.py:70
  190.3 19.3 %copy-start.1 = (bf16[256,3072]{1,0:T(8,128)(2,1)S(1)}, bf16[256,3072]{1,0:T(8,128)(2,1)}, u32[]{:S(2)}) copy-start(bf16[256,3072]{1,0:T(8,128)(2,1)} %all-gather.16.cloned.1.call-done) | copy-start | bytes 4718596
  257.0 47.9 %copy-start.2 = (bf16[256,768]{1,0:T(8,128)(2,1)S(1)}, bf16[256,768]{1,0:T(8,128)(2,1)}, u32[]{:S(2)}) copy-start(bf16[256,768]{1,0:T(8,128)(2,1)} %add_convert_fusion.1) | copy-start | bytes 1179652
Sparse Core Ops, SparseCore 0:
  9.2 33.5 all-gather.9
  44.3 17.9 all-gather.11
  63.8 12.1 all-gather.13
  114.0 43.2 reduce-scatter.2
  159.4 30.8 all-gather.15
  191.7 17.9 all-gather.17
  211.2 12.1 all-gather.19
  261.6 43.2 reduce-scatter.4
where the time goes:
time: 314 us
  waiting for transfers between devices  172 us (55%)
  blocking collectives  88.5 us (28%)
  matrix products  22.8 us (7%)
  between operations  14.5 us (5%)
  other arithmetic  13.9 us (4%)
    reduce_scatter x2, waiting for transfers between devices, attend_block(): mine = lax.psum_scatter(projected, 'head', scatter_dimension=1, tiled=True)  86.7 us
    all_gather x2, waiting for transfers between devices, modulate(): whole = lax.all_gather(x_rows, 'head', axis=1, tiled=True)  50.1 us
    all_gather x2, blocking collectives, attend_block(): key_piece = lax.all_gather(key, 'seq', axis=0, tiled=True)  39.7 us
    all_gather x2, blocking collectives, attend_block(): value_piece = lax.all_gather(value, 'seq', axis=0, tiled=True)  36.2 us
    all_gather x2, waiting for transfers between devices, attend_block(): lax.all_gather(qkv_weight, 'branch', axis=0, tiled=True)  31.2 us
    all_gather x1, blocking collectives, attend_block(): keep_piece = lax.all_gather(keep_wire, 'seq', axis=0, tiled=True)  12.7 us
    dot_general x2, matrix products, attend_block(): jnp.einsum('rd,dsc->rsc', moded, lax.all_gather(qkv_weight, 'branch', axi...  10.5 us
    dot_general x2, matrix products, attend_block(): jnp.dot(attended, lax.all_gather(out_weight, 'branch', axis=1, tiled=True...  8.77 us
  transfers between devices with their start and end apart: 8, of which 6 were waited for; matrix products, arithmetic and copies ran while one was open for 8% of the time, Pallas kernels for 0%

commit v1 on v0

v1 whole, which is shorter than its diff:
```python
import jax
import jax.numpy as jnp
from jax import lax
from jax.sharding import PartitionSpec as P

HEAD_DIM = 128
EPS = 1e-06


def swap(x, axis, k, n):
    return lax.ppermute(x, axis, [(i, (i + k) % n) for i in range(n)])


def cross(x, axis, k, n):
    return lax.ppermute(x, axis, [(i, i ^ k) for i in range(n)])


def modulate(x, mod):
    xf = x.astype(jnp.float32)
    mean = jnp.mean(xf, axis=1, keepdims=True)
    centered = xf - mean
    var = jnp.mean(centered * centered, axis=1, keepdims=True)
    normed = centered * lax.rsqrt(var + EPS)
    return (normed * (1.0 + mod[1]) + mod[0]).astype(jnp.bfloat16)


def head_norm(part, gain):
    return (
        part * lax.rsqrt(jnp.mean(part * part, axis=2, keepdims=True) + EPS) * gain
    ).astype(jnp.bfloat16)


def block(x, counts, weights, outs, mod, gains, sizes):
    n_branch, n_seq, n_head = sizes
    b = lax.axis_index("branch")
    h = lax.axis_index("head")
    rows, quarter = x.shape
    width = weights[0].shape[2]
    group = width // HEAD_DIM
    pieces = [x] + [cross(x, "head", k, n_head) for k in range(1, n_head)]
    stacked = jnp.stack(pieces)
    whole = jnp.concatenate(
        [lax.dynamic_index_in_dim(stacked, j ^ h, 0, keepdims=False) for j in range(n_head)], axis=1
    )
    moded = modulate(whole, mod)
    depth = moded.shape[1] // 2
    mine = jnp.where(b == 0, moded[:, :depth], moded[:, depth:])
    other = jnp.where(b == 0, moded[:, depth:], moded[:, :depth])

    def project(lo, hi):
        n = (hi - lo) * width
        return jnp.dot(
            mine, weights[0][:, lo:hi].reshape(depth, n), preferred_element_type=jnp.float32
        ) + jnp.dot(
            other, weights[1][:, lo:hi].reshape(depth, n), preferred_element_type=jnp.float32
        )

    kv = project(1, 3)
    key = head_norm(kv[:, :width].reshape(rows, group, HEAD_DIM), gains[1]).reshape(rows, width)
    packed = jnp.concatenate([key, kv[:, width:].astype(jnp.bfloat16)], axis=1)
    query = head_norm(project(0, 1).reshape(rows, group, HEAD_DIM), gains[0])
    blocks = [packed] + [swap(packed, "seq", k, n_seq) for k in range(1, n_seq)]
    partner = [cross(p, "branch", 1, n_branch) for p in blocks]
    keys = jnp.concatenate(blocks + partner, axis=0)
    pos = jnp.arange(rows, dtype=jnp.int32)
    valid = jnp.concatenate(
        [b * rows + pos < c for c in counts] + [(1 - b) * rows + pos < c for c in counts]
    )[None, None, :]
    length = keys.shape[0]
    key_heads = keys[:, :width].reshape(length, group, HEAD_DIM)
    value_heads = keys[:, width:].reshape(length, group, HEAD_DIM)
    scale = 1.0 / HEAD_DIM**0.5
    scores = (
        jnp.einsum("rhd,nhd->hrn", query, key_heads, preferred_element_type=jnp.float32) * scale
    )
    scores = jnp.where(valid, scores, -1e30)
    peak = jnp.max(scores, axis=2, keepdims=True)
    weight = jnp.where(valid, jnp.exp(scores - peak), 0.0)
    total = jnp.sum(weight, axis=2)
    mixed = jnp.einsum(
        "hrn,nhd->hrd",
        weight.astype(jnp.bfloat16),
        value_heads,
        preferred_element_type=jnp.float32,
    )
    attended = (mixed / total[:, :, None]).astype(jnp.bfloat16)
    attended = attended.transpose(1, 0, 2).reshape(rows, width)
    left = jnp.dot(attended, outs[0], preferred_element_type=jnp.float32)
    right = jnp.dot(attended, outs[1], preferred_element_type=jnp.float32)
    projected = jnp.concatenate(
        [jnp.where(b == 0, left, right), jnp.where(b == 0, right, left)], axis=1
    )
    total_out = lax.dynamic_slice_in_dim(projected, h * quarter, quarter, 1)
    for k in range(1, n_head):
        part = lax.dynamic_slice_in_dim(projected, (h ^ k) * quarter, quarter, 1)
        total_out = total_out + cross(part.astype(jnp.bfloat16), "head", k, n_head).astype(
            jnp.float32
        )
    gate = lax.dynamic_slice_in_dim(mod[2], h * quarter, quarter, 0)
    return (x.astype(jnp.float32) + gate[None, :] * total_out).astype(jnp.bfloat16)


def solution(mesh):
    n_branch, n_seq, n_head = (mesh.shape[a] for a in ("branch", "seq", "head"))
    sizes = (n_branch, n_seq, n_head)

    def per_device(
        tokens, valid_counts, shared_qkv, shared_out, skipped_qkv, skipped_out, modulation, qk_gains
    ):
        b = lax.axis_index("branch")
        rows = tokens.shape[0] // n_branch
        x = lax.dynamic_slice_in_dim(tokens, b * rows, rows, 0)
        count = valid_counts.astype(jnp.float32)
        counts = [valid_counts[0]] + [
            swap(count, "seq", k, n_seq)[0].astype(jnp.int32) for k in range(1, n_seq)
        ]
        both = lambda w: (w, cross(w, "branch", 1, n_branch))
        w0, o0, w1, o1 = both(shared_qkv), both(shared_out), both(skipped_qkv), both(skipped_out)
        forked = block(x, counts, w0, o0, modulation[0], qk_gains[0], sizes)
        strong = block(forked, counts, w1, o1, modulation[1], qk_gains[1], sizes)
        got = cross(jnp.where(b == 0, forked, strong), "branch", 1, n_branch)
        low = jnp.where(b == 0, strong, got)
        high = jnp.where(b == 0, got, forked)
        return jnp.concatenate([low, high], axis=0)[None]

    in_specs = (
        P("seq", "head"),
        P("seq"),
        P("branch", None, "head"),
        P("head", "branch"),
        P("branch", None, "head"),
        P("head", "branch"),
        P(),
        P(),
    )
    return jax.shard_map(
        per_device,
        mesh=mesh,
        in_specs=in_specs,
        out_specs=P("branch", "seq", "head"),
        check_vma=False,
    )
```

time: 314 us -> 188 us (0.60)
  waiting for transfers between devices: 172 us -> 41.1 us
  blocking collectives: 88.5 us -> 0 us
  local copies, waits for them, and re-layouts: 2.33 us -> 56.8 us
  starting transfers between devices: 0.28 us -> 35 us
  between operations: 14.5 us -> 3.09 us
  matrix products: 22.8 us -> 29.7 us
  other arithmetic: 13.9 us -> 19.3 us
    all_gather x5 -> x0, blocking collectives: 88.5 us -> none  [the longest x2 39.7 us: attend_block(): key_piece = lax.all_gather(key, 'seq', axis=0, tiled=True)]
    reduce_scatter x2 -> x0, waiting for transfers between devices: 86.7 us -> none  [attend_block(): mine = lax.psum_scatter(projected, 'head', scatter_dimension=1, tiled=True)]
    all_gather x6 -> x0, waiting for transfers between devices: 81.4 us -> none  [the longest x2 50.1 us: modulate(): whole = lax.all_gather(x_rows, 'head', axis=1, tiled=True)]
    ppermute x0 -> x34, waiting for transfers between devices: none -> 41.1 us  [the longest x25 25.8 us: cross(): return lax.ppermute(x, axis, [(i, i ^ k) for i in range(n)])]
    ppermute x0 -> x34, starting transfers between devices: none -> 35 us  [the longest x9 18.2 us: swap(): return lax.ppermute(x, axis, [(i, (i + k) % n) for i in range(n)])]
    unnamed x13 -> x51, local copies, waits for them, and re-layouts: 0.03 us -> 27 us
    slice x4 -> x12, local copies, waits for them, and re-layouts: 0.37 us -> 15.8 us  [the longest x4 5.44 us: block(): key_heads = keys[:, :width].reshape(length, group, HEAD_DIM)]
    mul x9 -> x8, local copies, waits for them, and re-layouts: 0.72 us -> 5.52 us  [the longest x6 3.67 us: head_norm(): part * lax.rsqrt(jnp.mean(part * part, axis=2, keepdims=True) + EPS) * gain]
  transfers between devices with their start and end apart: 8 -> 34, of which waited for: 6 -> 16; matrix products, arithmetic and copies ran while one was open for 8% -> 54% of each run, Pallas kernels for 0% -> 0%
where the time goes in v1:
time: 188 us; the launch traced here: 185 us
  local copies, waits for them, and re-layouts  56.8 us (30%)
  waiting for transfers between devices  41.1 us (22%)
  starting transfers between devices  35 us (19%)
  matrix products  29.7 us (16%)
  other arithmetic  19.3 us (10%)
  between operations  3.09 us (2%)
    unnamed x51, local copies, waits for them, and re-layouts  27 us
    ppermute x25, waiting for transfers between devices, cross(): return lax.ppermute(x, axis, [(i, i ^ k) for i in range(n)])  25.8 us
    ppermute x9, starting transfers between devices, swap(): return lax.ppermute(x, axis, [(i, (i + k) % n) for i in range(n)])  18.2 us
    ppermute x25, starting transfers between devices, cross(): return lax.ppermute(x, axis, [(i, i ^ k) for i in range(n)])  16.8 us
    ppermute x9, waiting for transfers between devices, swap(): return lax.ppermute(x, axis, [(i, (i + k) % n) for i in range(n)])  15.3 us
    dot_general x4, matrix products, project(): jnp.dot(other, weights[1][:, lo:hi].reshape(depth, n), preferred_element_...  6.26 us
    dot_general x4, matrix products, project(): jnp.dot(mine, weights[0][:, lo:hi].reshape(depth, n), preferred_element_t...  6.04 us
    slice x4, local copies, waits for them, and re-layouts, block(): key_heads = keys[:, :width].reshape(length, group, HEAD_DIM)  5.44 us
  transfers between devices with their start and end apart: 34, of which 16 were waited for; matrix products, arithmetic and copies ran while one was open for 54% of the time, Pallas kernels for 0%

profile of v1, /device:TPU:0, one launch (start us, length us, event | category | flops | bytes accessed | tf_op | source)
XLA Modules:
  0.0 185.0 jit_solution(4164504133416033619)
XLA Ops:
  1.6 3.9 %collective-permute-start.5 = (bf16[128,768]{1,0:T(8,128)(2,1)}, bf16[128,768]{1,0:T(8,128)(2,1)}, u32[]{:S(2)}, u32[]{:S(2)}) collective-permute-start(bf16[128,768]{1,0:T(8,128)(2,1)} %constant_dynamic-slice_fusion.2), channel_id=1, source_target_pairs={{0,3},{1,2},{2,1},{3,0},{4,7},{5,6},{6,5},{7,4},{8,11},{9,10},{10,... | collective-permute-start | bytes 589832 | tf_op jit(solution)/shard_map/ppermute | solution.py:15
  6.1 6.1 %copy.17 = bf16[1536,3,384]{0,2,1:T(8,128)(2,1)} copy(bf16[1536,3,384]{2,0,1:T(8,128)(2,1)} %param.10) | data formatting | bytes 7077888 | tf_op args[2]
  12.9 3.4 %collective-permute-start = (f32[1]{0:T(128)}, f32[1]{0:T(128)}, u32[]{:S(2)}, u32[]{:S(2)}) collective-permute-start(f32[1]{0:T(128)} %convert_element_type.112), channel_id=1, source_target_pairs={{0,4},{4,8},{8,12},{12,0},{1,5},{5,9},{9,13},{13,1},{2,6},{6,10},{... | collective-permute-start | bytes 20 | tf_op jit(solution)/shard_map/ppermute | solution.py:11
  17.9 3.3 %slice.153 = bf16[1536,2,384]{0,2,1:T(8,128)(2,1)} slice(bf16[1536,3,384]{0,2,1:T(8,128)(2,1)} %copy.17), slice={[0:1536], [1:3], [0:384]} | slice | bytes 4718592 | tf_op jit(solution)/shard_map/slice | solution.py:53
  21.2 4.3 %copy.26 = bf16[1536,3,384]{0,2,1:T(8,128)(2,1)S(1)} copy(bf16[1536,3,384]{2,0,1:T(8,128)(2,1)} %param.12) | data formatting | bytes 7077888 | tf_op args[4]
  29.4 3.9 %collective-permute-start.1 = (f32[1]{0:T(128)}, f32[1]{0:T(128)}, u32[]{:S(2)}, u32[]{:S(2)}) collective-permute-start(f32[1]{0:T(128)} %convert_element_type.112), channel_id=1, source_target_pairs={{0,8},{4,12},{8,0},{12,4},{1,9},{5,13},{9,1},{13,5},{2,10},{6,14},... | collective-permute-start | bytes 20 | tf_op jit(solution)/shard_map/ppermute | solution.py:11
  35.8 2.6 %collective-permute-start.2 = (f32[1]{0:T(128)}, f32[1]{0:T(128)}, u32[]{:S(2)}, u32[]{:S(2)}) collective-permute-start(f32[1]{0:T(128)} %convert_element_type.112), channel_id=1, source_target_pairs={{0,12},{4,0},{8,4},{12,8},{1,13},{5,1},{9,5},{13,9},{2,14},{6,2},{... | collective-permute-start | bytes 20 | tf_op jit(solution)/shard_map/ppermute | solution.py:11
  52.0 2.7 %fusion.20 = f32[128,384]{1,0:T(8,128)} fusion(bf16[1536,3,384]{2,0,1:T(8,128)(2,1)} %param.10, pred[]{:T(512)S(6)} %eq.2, bf16[128,3072]{1,0:T(8,128)(2,1)S(1)} %fusion.15), kind=kOutput, calls=%fused_computation.48 | convolution fusion | flops 151191552 | bytes 2162689 | tf_op jit(solution)/shard_map/dot_general | solution.py:52
  55.6 1.8 slice.154
  70.8 1.8 collective-permute-start.9
  72.6 2.7 %fusion.24 = f32[128,384]{1,0:T(8,128)} fusion(f32[128,384]{1,0:T(8,128)} %fusion.20, bf16[1536,3,384]{0,2,1:T(8,128)(2,1)} %collective-permute-done.6, pred[]{:T(512)S(6)} %eq.2, bf16[128,3072]{1,0:T(8,128)(2,1)} %copy-done.6), kind=kOutput, calls=%fused_computation.52 | convolution fusion | flops 151240704 | bytes 2359297 | tf_op jit(solution)/shard_map/dot_general | solution.py:54
  80.4 5.9 %collective-permute-done.8 = bf16[128,768]{1,0:T(8,128)(2,1)} collective-permute-done((bf16[128,768]{1,0:T(8,128)(2,1)}, bf16[128,768]{1,0:T(8,128)(2,1)}, u32[]{:S(2)}, u32[]{:S(2)}) %collective-permute-start.8) | collective-permute-done | bytes 196640 | tf_op jit(solution)/shard_map/ppermute | solution.py:11
  92.8 2.7 %fusion.84 = (bf16[1024,384]{1,0:T(8,128)(2,1)}, bf16[1024,384]{1,0:T(8,128)(2,1)}) fusion(bf16[1024,768]{1,0:T(8,128)(2,1)} %constant_dynamic-update-slice_fusion), kind=kLoop, calls=%fused_computation.186 | loop fusion | bytes 3145728 | tf_op jit(solution)/shard_map/slice | solution.py:70
  95.6 2.3 %copy.25 = bf16[1024,384]{0,1:T(8,128)(2,1)} copy(bf16[1024,384]{1,0:T(8,128)(2,1)} %get-tuple-element.20) | data formatting | bytes 1572864 | tf_op jit(solution)/shard_map/slice | solution.py:71
  97.8 2.3 %copy.22 = bf16[1024,384]{0,1:T(8,128)(2,1)} copy(bf16[1024,384]{1,0:T(8,128)(2,1)} %get-tuple-element.19) | data formatting | bytes 1572864 | tf_op jit(solution)/shard_map/slice | solution.py:70
  100.1 2.6 %fusion.86 = f32[3,128]{1,0:T(4,128)} fusion(bf16[1024,3,128]{0,2,1:T(8,128)(2,1)} %bitcast.119, pred[1024]{0:T(1024)(128)(4,1)} %dynamic-update-slice.23, f32[128,3,128]{0,2,1:T(8,128)} %bitcast.124, f32[128]{0:T(128)} %get-tuple-element.43, f32[128,3]{0,1:T(4,128)} %add_rsqrt_fusion.3), kind=kOutput, calls=%fused_computation.188 | convolution fusion | flops 102777856 | bytes 987648 | tf_op jit(solution)/shard_map/sub | solution.py:78
  102.7 2.8 %multiply_select_fusion.1 = f32[3,128,1024]{2,1,0:T(8,128)} fusion(bf16[1024,3,128]{0,2,1:T(8,128)(2,1)} %bitcast.120, pred[1024]{0:T(1024)(128)(4,1)} %dynamic-update-slice.23, f32[128,3,128]{0,2,1:T(8,128)} %bitcast.125, f32[128]{0:T(128)} %get-tuple-element.43, f32[128,3]{0,1:T(4,128)} %add_rsqrt_fusion.3), kind=kOutput, calls=%fused_computation.39 | convolution fusion | flops 101597184 | bytes 2558976 | tf_op jit(solution)/shard_map/rhd,nhd->hrn/dot_general | solution.py:74
  105.6 3.3 %fusion.28 = bf16[128,3,128]{0,2,1:T(8,128)(2,1)} fusion(bf16[1024,3,128]{0,2,1:T(8,128)(2,1)} %bitcast.130, f32[3,128,1024]{2,1,0:T(8,128)} %multiply_select_fusion.1, pred[1024]{0:T(1024)(128)(4,1)} %dynamic-update-slice.23, f32[128,3]{0,1:T(4,128)} %bitcast.147), kind=kOutput, calls=%fused_computation.58 | convolution fusion | flops 101942656 | bytes 2460160 | tf_op jit(solution)/shard_map/hrn,nhd->hrd/dot_general | solution.py:80
  114.2 2.5 %collective-permute-start.17 = (bf16[128,768]{1,0:T(8,128)(2,1)}, bf16[128,768]{1,0:T(8,128)(2,1)}, u32[]{:S(2)}, u32[]{:S(2)}) collective-permute-start(bf16[128,768]{1,0:T(8,128)(2,1)} %get-tuple-element.16), channel_id=1, source_target_pairs={{0,3},{1,2},{2,1},{3,0},{4,7},{5,6},{6,5},{7,4},{8,11},{9,10},{10,... | collective-permute-start | bytes 589832 | tf_op jit(solution)/shard_map/ppermute | solution.py:15
  118.4 4.9 %collective-permute-done.17 = bf16[128,768]{1,0:T(8,128)(2,1)} collective-permute-done((bf16[128,768]{1,0:T(8,128)(2,1)}, bf16[128,768]{1,0:T(8,128)(2,1)}, u32[]{:S(2)}, u32[]{:S(2)}) %collective-permute-start.17) | collective-permute-done | bytes 196640 | tf_op jit(solution)/shard_map/ppermute | solution.py:15
  123.3 3.7 %collective-permute-done.16 = bf16[128,768]{1,0:T(8,128)(2,1)} collective-permute-done((bf16[128,768]{1,0:T(8,128)(2,1)}, bf16[128,768]{1,0:T(8,128)(2,1)}, u32[]{:S(2)}, u32[]{:S(2)}) %collective-permute-start.16) | collective-permute-done | bytes 196640 | tf_op jit(solution)/shard_map/ppermute | solution.py:15
  132.2 1.8 slice.163
  134.0 3.2 %collective-permute-done.20 = bf16[128,768]{1,0:T(8,128)(2,1)S(1)} collective-permute-done((bf16[128,768]{1,0:T(8,128)(2,1)S(1)}, bf16[128,768]{1,0:T(8,128)(2,1)S(1)}, u32[]{:S(2)}, u32[]{:S(2)}) %collective-permute-start.20) | collective-permute-done | bytes 196640 | tf_op jit(solution)/shard_map/ppermute | solution.py:15
  137.3 3.2 %collective-permute-done.19 = bf16[128,768]{1,0:T(8,128)(2,1)S(1)} collective-permute-done((bf16[128,768]{1,0:T(8,128)(2,1)S(1)}, bf16[128,768]{1,0:T(8,128)(2,1)S(1)}, u32[]{:S(2)}, u32[]{:S(2)}) %collective-permute-start.19) | collective-permute-done | bytes 196640 | tf_op jit(solution)/shard_map/ppermute | solution.py:15
  144.6 2.0 %collective-permute-start.22 = (bf16[128,768]{1,0:T(8,128)(2,1)}, bf16[128,768]{1,0:T(8,128)(2,1)S(1)}, u32[]{:S(2)}, u32[]{:S(2)}) collective-permute-start(bf16[128,768]{1,0:T(8,128)(2,1)} %get-tuple-element.31), channel_id=1, source_target_pairs={{0,4},{4,8},{8,12},{12,0},{1,5},{5,9},{9,13},{13,1},{2,6},{6,10},{... | collective-permute-start | bytes 589832 | tf_op jit(solution)/shard_map/ppermute | solution.py:11
  146.7 2.1 %collective-permute-start.23 = (bf16[128,768]{1,0:T(8,128)(2,1)}, bf16[128,768]{1,0:T(8,128)(2,1)S(1)}, u32[]{:S(2)}, u32[]{:S(2)}) collective-permute-start(bf16[128,768]{1,0:T(8,128)(2,1)} %get-tuple-element.31), channel_id=1, source_target_pairs={{0,8},{4,12},{8,0},{12,4},{1,9},{5,13},{9,1},{13,5},{2,10},{6,14},... | collective-permute-start | bytes 589832 | tf_op jit(solution)/shard_map/ppermute | solution.py:11
  150.7 1.8 fusion.25
  152.6 1.9 %collective-permute-done.22 = bf16[128,768]{1,0:T(8,128)(2,1)S(1)} collective-permute-done((bf16[128,768]{1,0:T(8,128)(2,1)}, bf16[128,768]{1,0:T(8,128)(2,1)S(1)}, u32[]{:S(2)}, u32[]{:S(2)}) %collective-permute-start.22) | collective-permute-done | bytes 196640 | tf_op jit(solution)/shard_map/ppermute | solution.py:11
  154.5 7.4 %collective-permute-done.23 = bf16[128,768]{1,0:T(8,128)(2,1)S(1)} collective-permute-done((bf16[128,768]{1,0:T(8,128)(2,1)}, bf16[128,768]{1,0:T(8,128)(2,1)S(1)}, u32[]{:S(2)}, u32[]{:S(2)}) %collective-permute-start.23) | collective-permute-done | bytes 196640 | tf_op jit(solution)/shard_map/ppermute | solution.py:11
  171.2 1.8 collective-permute-start.31
  174.3 4.5 %collective-permute-done.32 = bf16[128,768]{1,0:T(8,128)(2,1)S(1)} collective-permute-done((bf16[128,768]{1,0:T(8,128)(2,1)S(1)}, bf16[128,768]{1,0:T(8,128)(2,1)S(1)}, u32[]{:S(2)}, u32[]{:S(2)}) %collective-permute-start.32) | collective-permute-done | bytes 196640 | tf_op jit(solution)/shard_map/ppermute | solution.py:15
  178.8 3.5 %collective-permute-done.31 = bf16[128,768]{1,0:T(8,128)(2,1)S(1)} collective-permute-done((bf16[128,768]{1,0:T(8,128)(2,1)S(1)}, bf16[128,768]{1,0:T(8,128)(2,1)S(1)}, u32[]{:S(2)}, u32[]{:S(2)}) %collective-permute-start.31) | collective-permute-done | bytes 196640 | tf_op jit(solution)/shard_map/ppermute | solution.py:15
  (175 shorter events, 79.1 us)
Async XLA Ops:
  1.6 47.4 %collective-permute-start.5 = (bf16[128,768]{1,0:T(8,128)(2,1)}, bf16[128,768]{1,0:T(8,128)(2,1)}, u32[]{:S(2)}, u32[]{:S(2)}) collective-permute-start(bf16[128,768]{1,0:T(8,128)(2,1)} %constant_dynamic-slice_fusion.2), channel_id=1, source_target_pairs={{0,3},{1,2},{2,1},{3,0},{4,7},{5,6},{6,5},{7,4},{8,11},{9,10},{10,... | collective-permute-start | bytes 589832 | tf_op jit(solution)/shard_map/ppermute | solution.py:15
  5.5 44.0 %collective-permute-start.4 = (bf16[128,768]{1,0:T(8,128)(2,1)}, bf16[128,768]{1,0:T(8,128)(2,1)}, u32[]{:S(2)}, u32[]{:S(2)}) collective-permute-start(bf16[128,768]{1,0:T(8,128)(2,1)} %constant_dynamic-slice_fusion.2), channel_id=1, source_target_pairs={{0,2},{1,3},{2,0},{3,1},{4,6},{5,7},{6,4},{7,5},{8,10},{9,11},{10,... | collective-permute-start | bytes 589832 | tf_op jit(solution)/shard_map/ppermute | solution.py:15
  6.0 43.5 %collective-permute-start.3 = (bf16[128,768]{1,0:T(8,128)(2,1)}, bf16[128,768]{1,0:T(8,128)(2,1)}, u32[]{:S(2)}, u32[]{:S(2)}) collective-permute-start(bf16[128,768]{1,0:T(8,128)(2,1)} %constant_dynamic-slice_fusion.2), channel_id=1, source_target_pairs={{0,1},{1,0},{2,3},{3,2},{4,5},{5,4},{6,7},{7,6},{8,9},{9,8},{10,11... | collective-permute-start | bytes 589832 | tf_op jit(solution)/shard_map/ppermute | solution.py:15
  12.2 43.3 %collective-permute-start.6 = (bf16[1536,3,384]{0,2,1:T(8,128)(2,1)}, bf16[1536,3,384]{0,2,1:T(8,128)(2,1)}, u32[]{:S(2)}, u32[]{:S(2)}) collective-permute-start(bf16[1536,3,384]{0,2,1:T(8,128)(2,1)} %copy.17), channel_id=1, source_target_pairs={{0,16},{16,0},{1,17},{17,1},{2,18},{18,2},{3,19},{19,3},{4,20},{20... | collective-permute-start | bytes 10616840 | tf_op jit(solution)/shard_map/ppermute | solution.py:15
  12.9 16.5 %collective-permute-start = (f32[1]{0:T(128)}, f32[1]{0:T(128)}, u32[]{:S(2)}, u32[]{:S(2)}) collective-permute-start(f32[1]{0:T(128)} %convert_element_type.112), channel_id=1, source_target_pairs={{0,4},{4,8},{8,12},{12,0},{1,5},{5,9},{9,13},{13,1},{2,6},{6,10},{... | collective-permute-start | bytes 20 | tf_op jit(solution)/shard_map/ppermute | solution.py:11
  29.4 6.4 %collective-permute-start.1 = (f32[1]{0:T(128)}, f32[1]{0:T(128)}, u32[]{:S(2)}, u32[]{:S(2)}) collective-permute-start(f32[1]{0:T(128)} %convert_element_type.112), channel_id=1, source_target_pairs={{0,8},{4,12},{8,0},{12,4},{1,9},{5,13},{9,1},{13,5},{2,10},{6,14},... | collective-permute-start | bytes 20 | tf_op jit(solution)/shard_map/ppermute | solution.py:11
  35.8 5.2 %collective-permute-start.2 = (f32[1]{0:T(128)}, f32[1]{0:T(128)}, u32[]{:S(2)}, u32[]{:S(2)}) collective-permute-start(f32[1]{0:T(128)} %convert_element_type.112), channel_id=1, source_target_pairs={{0,12},{4,0},{8,4},{12,8},{1,13},{5,1},{9,5},{13,9},{2,14},{6,2},{... | collective-permute-start | bytes 20 | tf_op jit(solution)/shard_map/ppermute | solution.py:11
  41.0 69.6 %collective-permute-start.14 = (bf16[384,1536]{1,0:T(8,128)(2,1)}, bf16[384,1536]{1,0:T(8,128)(2,1)}, u32[]{:S(2)}, u32[]{:S(2)}) collective-permute-start(bf16[384,1536]{1,0:T(8,128)(2,1)} %param.11), channel_id=1, source_target_pairs={{0,16},{16,0},{1,17},{17,1},{2,18},{18,2},{3,19},{19,3},{4,20},{20... | collective-permute-start | bytes 3538952 | tf_op jit(solution)/shard_map/ppermute | solution.py:15
  49.0 83.2 %collective-permute-start.21 = (bf16[1536,3,384]{0,2,1:T(8,128)(2,1)S(1)}, bf16[1536,3,384]{0,2,1:T(8,128)(2,1)}, u32[]{:S(2)}, u32[]{:S(2)}) collective-permute-start(bf16[1536,3,384]{0,2,1:T(8,128)(2,1)S(1)} %copy.26), channel_id=1, source_target_pairs={{0,16},{16,0},{1,17},{17,1},{2,18},{18,2},{3,19},{19,3},{4,20},{20... | collective-permute-start | bytes 10616840 | tf_op jit(solution)/shard_map/ppermute | solution.py:15
  68.8 10.0 %collective-permute-start.7 = (bf16[128,768]{1,0:T(8,128)(2,1)}, bf16[128,768]{1,0:T(8,128)(2,1)}, u32[]{:S(2)}, u32[]{:S(2)}) collective-permute-start(bf16[128,768]{1,0:T(8,128)(2,1)} %get-tuple-element.33), channel_id=1, source_target_pairs={{0,4},{4,8},{8,12},{12,0},{1,5},{5,9},{9,13},{13,1},{2,6},{6,10},{... | collective-permute-start | bytes 589832 | tf_op jit(solution)/shard_map/ppermute | solution.py:11
  69.5 16.8 %collective-permute-start.8 = (bf16[128,768]{1,0:T(8,128)(2,1)}, bf16[128,768]{1,0:T(8,128)(2,1)}, u32[]{:S(2)}, u32[]{:S(2)}) collective-permute-start(bf16[128,768]{1,0:T(8,128)(2,1)} %get-tuple-element.33), channel_id=1, source_target_pairs={{0,8},{4,12},{8,0},{12,4},{1,9},{5,13},{9,1},{13,5},{2,10},{6,14},... | collective-permute-start | bytes 589832 | tf_op jit(solution)/shard_map/ppermute | solution.py:11
  70.8 17.1 %collective-permute-start.9 = (bf16[128,768]{1,0:T(8,128)(2,1)}, bf16[128,768]{1,0:T(8,128)(2,1)}, u32[]{:S(2)}, u32[]{:S(2)}) collective-permute-start(bf16[128,768]{1,0:T(8,128)(2,1)} %get-tuple-element.33), channel_id=1, source_target_pairs={{0,12},{4,0},{8,4},{12,8},{1,13},{5,1},{9,5},{13,9},{2,14},{6,2},{... | collective-permute-start | bytes 589832 | tf_op jit(solution)/shard_map/ppermute | solution.py:11
  78.8 11.2 %collective-permute-start.10 = (bf16[128,768]{1,0:T(8,128)(2,1)}, bf16[128,768]{1,0:T(8,128)(2,1)S(1)}, u32[]{:S(2)}, u32[]{:S(2)}) collective-permute-start(bf16[128,768]{1,0:T(8,128)(2,1)} %get-tuple-element.33), channel_id=1, source_target_pairs={{0,16},{16,0},{1,17},{17,1},{2,18},{18,2},{3,19},{19,3},{4,20},{20... | collective-permute-start | bytes 589832 | tf_op jit(solution)/shard_map/ppermute | solution.py:15
  86.3 4.5 %collective-permute-start.11 = (bf16[128,768]{1,0:T(8,128)(2,1)}, bf16[128,768]{1,0:T(8,128)(2,1)S(1)}, u32[]{:S(2)}, u32[]{:S(2)}) collective-permute-start(bf16[128,768]{1,0:T(8,128)(2,1)} %collective-permute-done.7), channel_id=1, source_target_pairs={{0,16},{16,0},{1,17},{17,1},{2,18},{18,2},{3,19},{19,3},{4,20},{20... | collective-permute-start | bytes 589832 | tf_op jit(solution)/shard_map/ppermute | solution.py:15
  87.9 3.5 %collective-permute-start.12 = (bf16[128,768]{1,0:T(8,128)(2,1)}, bf16[128,768]{1,0:T(8,128)(2,1)S(1)}, u32[]{:S(2)}, u32[]{:S(2)}) collective-permute-start(bf16[128,768]{1,0:T(8,128)(2,1)} %collective-permute-done.8), channel_id=1, source_target_pairs={{0,16},{16,0},{1,17},{17,1},{2,18},{18,2},{3,19},{19,3},{4,20},{20... | collective-permute-start | bytes 589832 | tf_op jit(solution)/shard_map/ppermute | solution.py:15
  90.0 2.1 %collective-permute-start.13 = (bf16[128,768]{1,0:T(8,128)(2,1)}, bf16[128,768]{1,0:T(8,128)(2,1)S(1)}, u32[]{:S(2)}, u32[]{:S(2)}) collective-permute-start(bf16[128,768]{1,0:T(8,128)(2,1)} %collective-permute-done.9), channel_id=1, source_target_pairs={{0,16},{16,0},{1,17},{17,1},{2,18},{18,2},{3,19},{19,3},{4,20},{20... | collective-permute-start | bytes 589832 | tf_op jit(solution)/shard_map/ppermute | solution.py:15
  114.2 9.0 %collective-permute-start.17 = (bf16[128,768]{1,0:T(8,128)(2,1)}, bf16[128,768]{1,0:T(8,128)(2,1)}, u32[]{:S(2)}, u32[]{:S(2)}) collective-permute-start(bf16[128,768]{1,0:T(8,128)(2,1)} %get-tuple-element.16), channel_id=1, source_target_pairs={{0,3},{1,2},{2,1},{3,0},{4,7},{5,6},{6,5},{7,4},{8,11},{9,10},{10,... | collective-permute-start | bytes 589832 | tf_op jit(solution)/shard_map/ppermute | solution.py:15
  116.7 10.3 %collective-permute-start.16 = (bf16[128,768]{1,0:T(8,128)(2,1)}, bf16[128,768]{1,0:T(8,128)(2,1)}, u32[]{:S(2)}, u32[]{:S(2)}) collective-permute-start(bf16[128,768]{1,0:T(8,128)(2,1)} %get-tuple-element.15), channel_id=1, source_target_pairs={{0,2},{1,3},{2,0},{3,1},{4,6},{5,7},{6,4},{7,5},{8,10},{9,11},{10,... | collective-permute-start | bytes 589832 | tf_op jit(solution)/shard_map/ppermute | solution.py:15
  117.2 9.9 %collective-permute-start.15 = (bf16[128,768]{1,0:T(8,128)(2,1)}, bf16[128,768]{1,0:T(8,128)(2,1)}, u32[]{:S(2)}, u32[]{:S(2)}) collective-permute-start(bf16[128,768]{1,0:T(8,128)(2,1)} %get-tuple-element.14), channel_id=1, source_target_pairs={{0,1},{1,0},{2,3},{3,2},{4,5},{5,4},{6,7},{7,6},{8,9},{9,8},{10,11... | collective-permute-start | bytes 589832 | tf_op jit(solution)/shard_map/ppermute | solution.py:15
  128.5 8.8 %collective-permute-start.20 = (bf16[128,768]{1,0:T(8,128)(2,1)S(1)}, bf16[128,768]{1,0:T(8,128)(2,1)S(1)}, u32[]{:S(2)}, u32[]{:S(2)}) collective-permute-start(bf16[128,768]{1,0:T(8,128)(2,1)S(1)} %fusion.53), channel_id=1, source_target_pairs={{0,3},{1,2},{2,1},{3,0},{4,7},{5,6},{6,5},{7,4},{8,11},{9,10},{10,... | collective-permute-start | bytes 589832 | tf_op jit(solution)/shard_map/ppermute | solution.py:15
  130.2 10.2 %collective-permute-start.19 = (bf16[128,768]{1,0:T(8,128)(2,1)S(1)}, bf16[128,768]{1,0:T(8,128)(2,1)S(1)}, u32[]{:S(2)}, u32[]{:S(2)}) collective-permute-start(bf16[128,768]{1,0:T(8,128)(2,1)S(1)} %fusion.53), channel_id=1, source_target_pairs={{0,2},{1,3},{2,0},{3,1},{4,6},{5,7},{6,4},{7,5},{8,10},{9,11},{10,... | collective-permute-start | bytes 589832 | tf_op jit(solution)/shard_map/ppermute | solution.py:15
  131.5 9.0 %collective-permute-start.18 = (bf16[128,768]{1,0:T(8,128)(2,1)S(1)}, bf16[128,768]{1,0:T(8,128)(2,1)S(1)}, u32[]{:S(2)}, u32[]{:S(2)}) collective-permute-start(bf16[128,768]{1,0:T(8,128)(2,1)S(1)} %fusion.53), channel_id=1, source_target_pairs={{0,1},{1,0},{2,3},{3,2},{4,5},{5,4},{6,7},{7,6},{8,9},{9,8},{10,11... | collective-permute-start | bytes 589832 | tf_op jit(solution)/shard_map/ppermute | solution.py:15
  132.1 35.9 %collective-permute-start.29 = (bf16[384,1536]{1,0:T(8,128)(2,1)}, bf16[384,1536]{1,0:T(8,128)(2,1)}, u32[]{:S(2)}, u32[]{:S(2)}) collective-permute-start(bf16[384,1536]{1,0:T(8,128)(2,1)} %param.13), channel_id=1, source_target_pairs={{0,16},{16,0},{1,17},{17,1},{2,18},{18,2},{3,19},{19,3},{4,20},{20... | collective-permute-start | bytes 3538952 | tf_op jit(solution)/shard_map/ppermute | solution.py:15
  144.6 9.9 %collective-permute-start.22 = (bf16[128,768]{1,0:T(8,128)(2,1)}, bf16[128,768]{1,0:T(8,128)(2,1)S(1)}, u32[]{:S(2)}, u32[]{:S(2)}) collective-permute-start(bf16[128,768]{1,0:T(8,128)(2,1)} %get-tuple-element.31), channel_id=1, source_target_pairs={{0,4},{4,8},{8,12},{12,0},{1,5},{5,9},{9,13},{13,1},{2,6},{6,10},{... | collective-permute-start | bytes 589832 | tf_op jit(solution)/shard_map/ppermute | solution.py:11
  146.7 15.2 %collective-permute-start.23 = (bf16[128,768]{1,0:T(8,128)(2,1)}, bf16[128,768]{1,0:T(8,128)(2,1)S(1)}, u32[]{:S(2)}, u32[]{:S(2)}) collective-permute-start(bf16[128,768]{1,0:T(8,128)(2,1)} %get-tuple-element.31), channel_id=1, source_target_pairs={{0,8},{4,12},{8,0},{12,4},{1,9},{5,13},{9,1},{13,5},{2,10},{6,14},... | collective-permute-start | bytes 589832 | tf_op jit(solution)/shard_map/ppermute | solution.py:11
  148.8 13.2 %collective-permute-start.24 = (bf16[128,768]{1,0:T(8,128)(2,1)}, bf16[128,768]{1,0:T(8,128)(2,1)S(1)}, u32[]{:S(2)}, u32[]{:S(2)}) collective-permute-start(bf16[128,768]{1,0:T(8,128)(2,1)} %get-tuple-element.31), channel_id=1, source_target_pairs={{0,12},{4,0},{8,4},{12,8},{1,13},{5,1},{9,5},{13,9},{2,14},{6,2},{... | collective-permute-start | bytes 589832 | tf_op jit(solution)/shard_map/ppermute | solution.py:11
  149.0 13.5 %collective-permute-start.25 = (bf16[128,768]{1,0:T(8,128)(2,1)}, bf16[128,768]{1,0:T(8,128)(2,1)S(1)}, u32[]{:S(2)}, u32[]{:S(2)}) collective-permute-start(bf16[128,768]{1,0:T(8,128)(2,1)} %get-tuple-element.31), channel_id=1, source_target_pairs={{0,16},{16,0},{1,17},{17,1},{2,18},{18,2},{3,19},{19,3},{4,20},{20... | collective-permute-start | bytes 589832 | tf_op jit(solution)/shard_map/ppermute | solution.py:15
  154.5 8.1 %collective-permute-start.26 = (bf16[128,768]{1,0:T(8,128)(2,1)S(1)}, bf16[128,768]{1,0:T(8,128)(2,1)S(1)}, u32[]{:S(2)}, u32[]{:S(2)}) collective-permute-start(bf16[128,768]{1,0:T(8,128)(2,1)S(1)} %collective-permute-done.22), channel_id=1, source_target_pairs={{0,16},{16,0},{1,17},{17,1},{2,18},{18,2},{3,19},{19,3},{4,20},{20... | collective-permute-start | bytes 589832 | tf_op jit(solution)/shard_map/ppermute | solution.py:15
  161.9 1.7 collective-permute-start.28
  170.0 8.8 %collective-permute-start.32 = (bf16[128,768]{1,0:T(8,128)(2,1)S(1)}, bf16[128,768]{1,0:T(8,128)(2,1)S(1)}, u32[]{:S(2)}, u32[]{:S(2)}) collective-permute-start(bf16[128,768]{1,0:T(8,128)(2,1)S(1)} %get-tuple-element.9), channel_id=1, source_target_pairs={{0,3},{1,2},{2,1},{3,0},{4,7},{5,6},{6,5},{7,4},{8,11},{9,10},{10,... | collective-permute-start | bytes 589832 | tf_op jit(solution)/shard_map/ppermute | solution.py:15
  171.2 11.1 %collective-permute-start.31 = (bf16[128,768]{1,0:T(8,128)(2,1)S(1)}, bf16[128,768]{1,0:T(8,128)(2,1)S(1)}, u32[]{:S(2)}, u32[]{:S(2)}) collective-permute-start(bf16[128,768]{1,0:T(8,128)(2,1)S(1)} %get-tuple-element.8), channel_id=1, source_target_pairs={{0,2},{1,3},{2,0},{3,1},{4,6},{5,7},{6,4},{7,5},{8,10},{9,11},{10,... | collective-permute-start | bytes 589832 | tf_op jit(solution)/shard_map/ppermute | solution.py:15
  173.1 9.4 %collective-permute-start.30 = (bf16[128,768]{1,0:T(8,128)(2,1)S(1)}, bf16[128,768]{1,0:T(8,128)(2,1)S(1)}, u32[]{:S(2)}, u32[]{:S(2)}) collective-permute-start(bf16[128,768]{1,0:T(8,128)(2,1)S(1)} %get-tuple-element.7), channel_id=1, source_target_pairs={{0,1},{1,0},{2,3},{3,2},{4,5},{5,4},{6,7},{7,6},{8,9},{9,8},{10,11... | collective-permute-start | bytes 589832 | tf_op jit(solution)/shard_map/ppermute | solution.py:15
  (17 other events, 59.7 us)

commit v2 on v1

v2 whole, which is shorter than its diff:
```python
import functools

import jax
import jax.numpy as jnp
from jax import lax
from jax.experimental import pallas as pl
from jax.experimental.pallas import tpu as pltpu
from jax.sharding import PartitionSpec as P

HEAD_DIM = 128
EPS = 1e-06
F32 = jnp.float32
BF16 = jnp.bfloat16
VMEM = pl.BlockSpec(memory_space=pltpu.VMEM)
SMEM = pl.BlockSpec(memory_space=pltpu.SMEM)
ANY = pl.BlockSpec(memory_space=pl.ANY)
MIB = 1 << 20


def turn(x, axis, k, n):
    return lax.ppermute(x, axis, [(i, (i + k) % n) for i in range(n)])


def cross(x, axis, k, n):
    return lax.ppermute(x, axis, [(i, i ^ k) for i in range(n)])


def params(mib):
    return pltpu.CompilerParams(vmem_limit_bytes=mib * MIB)


def half_kernel(tok_ref, out_ref, sem):
    rows = out_ref.shape[0]
    start = pl.multiple_of(lax.axis_index("branch") * rows, rows)
    copy = pltpu.make_async_copy(tok_ref.at[pl.ds(start, rows)], out_ref, sem)
    copy.start()
    copy.wait()


def take_half(tokens, n_branch):
    rows, cols = tokens.shape
    return pl.pallas_call(
        half_kernel,
        out_shape=jax.ShapeDtypeStruct((rows // n_branch, cols), tokens.dtype),
        in_specs=[ANY],
        out_specs=VMEM,
        scratch_shapes=[pltpu.SemaphoreType.DMA],
        compiler_params=params(4),
        name="take_half",
    )(tokens)


def contract(moded_ref, own_ref, other_ref, which, n_head):
    b = lax.axis_index("branch")
    h = lax.axis_index("head")
    quarter = moded_ref.shape[2]
    per_core = n_head // 2
    total = None
    for ref, core in ((own_ref, b), (other_ref, 1 - b)):
        for i in range(per_core):
            piece = moded_ref[(core * per_core + i) ^ h]
            term = jnp.dot(
                piece,
                ref[which, i * quarter : (i + 1) * quarter, :],
                preferred_element_type=F32,
            )
            total = term if total is None else total + term
    return total


def norm_heads(part, gain, width):
    outs = []
    for lo in range(0, width, HEAD_DIM):
        one = part[:, lo : lo + HEAD_DIM]
        scale = lax.rsqrt(jnp.mean(one * one, axis=1, keepdims=True) + EPS)
        outs.append((one * scale * gain).astype(BF16))
    return outs


def kv_kernel(blk, n_head, *refs):
    xs = refs[:n_head]
    own_ref, other_ref, mod_ref, gain_ref, packed_ref, moded_ref = refs[n_head:]
    h = lax.axis_index("head")
    quarter = xs[0].shape[1]
    width = own_ref.shape[2]
    total = sum(jnp.sum(x[...].astype(F32), axis=1, keepdims=True) for x in xs)
    mean = total / (n_head * quarter)
    square = 0.0
    for x in xs:
        centered = x[...].astype(F32) - mean
        square = square + jnp.sum(centered * centered, axis=1, keepdims=True)
    scale = lax.rsqrt(square / (n_head * quarter) + EPS)
    for k, x in enumerate(xs):
        at = pl.ds(pl.multiple_of((h ^ k) * quarter, quarter), quarter)
        shift = mod_ref[0, blk : blk + 1, at]
        gain = mod_ref[1, blk : blk + 1, at] + 1.0
        normed = (x[...].astype(F32) - mean) * scale
        moded_ref[k] = (normed * gain + shift).astype(BF16)
    key = contract(moded_ref, own_ref, other_ref, 1, n_head)
    for i, out in enumerate(norm_heads(key, gain_ref[blk, 1:2, :], width)):
        packed_ref[:, i * HEAD_DIM : (i + 1) * HEAD_DIM] = out
    packed_ref[:, width:] = contract(moded_ref, own_ref, other_ref, 2, n_head).astype(BF16)


def q_kernel(blk, n_head, moded_ref, own_ref, other_ref, gain_ref, query_ref):
    width = own_ref.shape[2]
    query = contract(moded_ref, own_ref, other_ref, 0, n_head)
    for i, out in enumerate(norm_heads(query, gain_ref[blk, 0:1, :], width)):
        query_ref[:, i * HEAD_DIM : (i + 1) * HEAD_DIM] = out


def attend_kernel(n_seq, n_head, *refs):
    query_ref = refs[0]
    blocks = refs[1 : 1 + 2 * n_seq]
    counts = refs[1 + 2 * n_seq : 1 + 3 * n_seq]
    own_ref, other_ref = refs[1 + 3 * n_seq : 3 + 3 * n_seq]
    outs = refs[3 + 3 * n_seq : 3 + 3 * n_seq + n_head]
    attended, spread = refs[3 + 3 * n_seq + n_head :]
    b = lax.axis_index("branch")
    h = lax.axis_index("head")
    rows, width = query_ref.shape
    scale = 1.0 / HEAD_DIM**0.5
    lane = lax.broadcasted_iota(jnp.int32, (1, rows), 1)
    valid = []
    for i in range(2 * n_seq):
        core = b if i < n_seq else 1 - b
        valid.append(lane + core * rows < counts[i % n_seq][0])
    for lo in range(0, width, HEAD_DIM):
        at = slice(lo, lo + HEAD_DIM)
        query = query_ref[:, at]
        scores = []
        for block, ok in zip(blocks, valid):
            one = lax.dot_general(
                query, block[:, at], (((1,), (1,)), ((), ())), preferred_element_type=F32
            )
            scores.append(jnp.where(ok, one * scale, -1e30))
        peak = functools.reduce(jnp.maximum, scores)
        peak = jnp.max(peak, axis=1, keepdims=True)
        mixed = None
        total = None
        for block, ok, one in zip(blocks, valid, scores):
            weight = jnp.where(ok, jnp.exp(one - peak), 0.0)
            total = weight if total is None else total + weight
            term = jnp.dot(
                weight.astype(BF16),
                block[:, width + lo : width + lo + HEAD_DIM],
                preferred_element_type=F32,
            )
            mixed = term if mixed is None else mixed + term
        total = jnp.sum(total, axis=1, keepdims=True)
        attended[:, at] = (mixed / total).astype(BF16)
    quarter = outs[0].shape[1]
    per_core = n_head // 2
    value = attended[...]
    for ref, core in ((own_ref, b), (other_ref, 1 - b)):
        for i in range(per_core):
            spread[(core * per_core + i) ^ h] = jnp.dot(
                value, ref[:, i * quarter : (i + 1) * quarter], preferred_element_type=F32
            )
    for k, out in enumerate(outs):
        out[...] = spread[k].astype(out.dtype)


def join_kernel(blk, n_head, *refs):
    x_ref, kept_ref = refs[:2]
    parts = refs[2 : 1 + n_head]
    mod_ref, out_ref = refs[1 + n_head :]
    h = lax.axis_index("head")
    quarter = x_ref.shape[1]
    gate = mod_ref[2, blk : blk + 1, pl.ds(pl.multiple_of(h * quarter, quarter), quarter)]
    total = kept_ref[...]
    for part in parts:
        total = total + part[...].astype(F32)
    out_ref[...] = (x_ref[...].astype(F32) + gate * total).astype(BF16)


def block(x, counts, weights, outs, mod, gains, blk, sizes):
    n_branch, n_seq, n_head = sizes
    rows, quarter = x.shape
    width = weights[0].shape[2]
    shape = jax.ShapeDtypeStruct
    pieces = [x] + [cross(x, "head", k, n_head) for k in range(1, n_head)]
    packed, moded = pl.pallas_call(
        functools.partial(kv_kernel, blk, n_head),
        out_shape=(shape((rows, 2 * width), BF16), shape((n_head, rows, quarter), BF16)),
        in_specs=[VMEM] * (n_head + 4),
        out_specs=(VMEM, VMEM),
        compiler_params=params(24),
        name=f"kv_{blk}",
    )(*pieces, *weights, mod, gains)
    blocks = [packed] + [turn(packed, "seq", k, n_seq) for k in range(1, n_seq)]
    query = pl.pallas_call(
        functools.partial(q_kernel, blk, n_head),
        out_shape=shape((rows, width), BF16),
        in_specs=[VMEM] * 4,
        out_specs=VMEM,
        compiler_params=params(24),
        name=f"q_{blk}",
    )(moded, *weights, gains)
    partner = [cross(p, "branch", 1, n_branch) for p in blocks]
    sent = pl.pallas_call(
        functools.partial(attend_kernel, n_seq, n_head),
        out_shape=tuple(
            shape((rows, quarter), F32 if k == 0 else BF16) for k in range(n_head)
        ),
        in_specs=[VMEM] * (1 + 2 * n_seq) + [SMEM] * n_seq + [VMEM] * 2,
        out_specs=tuple([VMEM] * n_head),
        scratch_shapes=[
            pltpu.VMEM((rows, width), BF16),
            pltpu.VMEM((n_head, rows, quarter), F32),
        ],
        compiler_params=params(24),
        name=f"attend_{blk}",
    )(query, *blocks, *partner, *counts, *outs)
    parts = [cross(sent[k], "head", k, n_head) for k in range(1, n_head)]
    return pl.pallas_call(
        functools.partial(join_kernel, blk, n_head),
        out_shape=shape((rows, quarter), BF16),
        in_specs=[VMEM] * (n_head + 2),
        out_specs=VMEM,
        compiler_params=params(8),
        name=f"join_{blk}",
    )(x, sent[0], *parts, mod)


def solution(mesh):
    n_branch, n_seq, n_head = (mesh.shape[a] for a in ("branch", "seq", "head"))
    sizes = (n_branch, n_seq, n_head)

    def per_device(
        tokens, valid_counts, shared_qkv, shared_out, skipped_qkv, skipped_out, modulation, qk_gains
    ):
        b = lax.axis_index("branch")
        x = take_half(tokens, n_branch)
        counts = [valid_counts] + [turn(valid_counts, "seq", k, n_seq) for k in range(1, n_seq)]
        both = lambda w: (w, cross(w, "branch", 1, n_branch))
        first = both(shared_qkv.transpose(1, 0, 2))
        second = both(skipped_qkv.transpose(1, 0, 2))
        mod = modulation.transpose(1, 0, 2)
        forked = block(x, counts, first, both(shared_out), mod, qk_gains, 0, sizes)
        strong = block(forked, counts, second, both(skipped_out), mod, qk_gains, 1, sizes)
        got = cross(jnp.where(b == 0, forked, strong), "branch", 1, n_branch)
        low = jnp.where(b == 0, strong, got)
        high = jnp.where(b == 0, got, forked)
        return jnp.concatenate([low, high], axis=0)[None]

    in_specs = (
        P("seq", "head"),
        P("seq"),
        P("branch", None, "head"),
        P("head", "branch"),
        P("branch", None, "head"),
        P("head", "branch"),
        P(),
        P(),
    )
    return jax.shard_map(
        per_device,
        mesh=mesh,
        in_specs=in_specs,
        out_specs=P("branch", "seq", "head"),
        check_vma=False,
    )
```

time: 188 us -> 114 us (0.61)
  local copies, waits for them, and re-layouts: 56.8 us -> 5.1 us
  matrix products: 29.7 us -> 0 us
  other arithmetic: 19.3 us -> 0.84 us
  waiting for transfers between devices: 41.1 us -> 56.9 us
  Pallas kernels: 0 us -> 14 us
  between operations: 3.09 us -> 0.84 us
    dot_general x16 -> x0, matrix products: 26.2 us -> none  [the longest x4 6.26 us: project(): jnp.dot(other, weights[1][:, lo:hi].reshape(depth, n), preferred_element_...]
    unnamed x51 -> x18, local copies, waits for them, and re-layouts: 27 us -> 5.1 us
    slice x12 -> x0, local copies, waits for them, and re-layouts: 15.8 us -> none  [the longest x4 5.44 us: block(): key_heads = keys[:, :width].reshape(length, group, HEAD_DIM)]
    pallas_call x0 -> x9, Pallas kernels: none -> 14 us  [the longest x2 8.38 us: block(): pl.pallas_call(functools.partial(attend_kernel, n_seq, n_head), out_shape...]
    ppermute x25, waiting for transfers between devices: 25.8 us -> 36.1 us  [cross(): return lax.ppermute(x, axis, [(i, i ^ k) for i in range(n)])]
    mul x8 -> x0, local copies, waits for them, and re-layouts: 5.52 us -> none  [the longest x6 3.67 us: head_norm(): part * lax.rsqrt(jnp.mean(part * part, axis=2, keepdims=True) + EPS) * gain]
    ppermute x9, waiting for transfers between devices: 15.3 us -> 20.8 us  [turn(): return lax.ppermute(x, axis, [(i, (i + k) % n) for i in range(n)])]
    convert_element_type x7 -> x0, other arithmetic: 4.55 us -> none  [the longest x1 1.43 us: block(): (x.astype(jnp.float32) + gate[None, :] * total_out).astype(jnp.bfloat16)]
  transfers between devices with their start and end apart: 34 -> 34, of which waited for: 16 -> 16; matrix products, arithmetic and copies ran while one was open for 54% -> 0% of each run, Pallas kernels for 0% -> 9%
where the time goes in v2:
time: 114 us; the launch traced here: 112 us
  waiting for transfers between devices  56.9 us (50%)
  starting transfers between devices  34.2 us (30%)
  Pallas kernels  14 us (12%)
  local copies, waits for them, and re-layouts  5.1 us (4%)
    ppermute x25, waiting for transfers between devices, cross(): return lax.ppermute(x, axis, [(i, i ^ k) for i in range(n)])  36.1 us
    ppermute x9, waiting for transfers between devices, turn(): return lax.ppermute(x, axis, [(i, (i + k) % n) for i in range(n)])  20.8 us
    ppermute x25, starting transfers between devices, cross(): return lax.ppermute(x, axis, [(i, i ^ k) for i in range(n)])  20.1 us
    ppermute x9, starting transfers between devices, turn(): return lax.ppermute(x, axis, [(i, (i + k) % n) for i in range(n)])  14.2 us
    pallas_call x2, Pallas kernels, block(): pl.pallas_call(functools.partial(attend_kernel, n_seq, n_head), out_shape...  8.38 us
    unnamed x18, local copies, waits for them, and re-layouts  5.1 us
    pallas_call x2, Pallas kernels, block(): pl.pallas_call(functools.partial(kv_kernel, blk, n_head), out_shape=(shap...  3.77 us
  transfers between devices with their start and end apart: 34, of which 16 were waited for; matrix products, arithmetic and copies ran while one was open for 0% of the time, Pallas kernels for 9%

profile of v2, /device:TPU:0, one launch (start us, length us, event | category | flops | bytes accessed | tf_op | source)
XLA Modules:
  0.0 112.0 jit_solution(10587974953527517540)
XLA Ops:
  2.2 2.5 %collective-permute-start = (bf16[128,768]{1,0:T(8,128)(2,1)S(1)}, bf16[128,768]{1,0:T(8,128)(2,1)S(1)}, u32[]{:S(2)}, u32[]{:S(2)}) collective-permute-start(bf16[128,768]{1,0:T(8,128)(2,1)S(1)} %take_half.1.refs_0_), channel_id=1, source_target_pairs={{0,1},{1,0},{2,3},{3,2},{4,5},{5,4},{6,7},{7,6},{8,9},{9,8},{10,11... | collective-permute-start | bytes 589832 | tf_op jit(solution)/shard_map/ppermute | solution.py:25
  4.8 1.5 %collective-permute-start.1 = (bf16[128,768]{1,0:T(8,128)(2,1)S(1)}, bf16[128,768]{1,0:T(8,128)(2,1)S(1)}, u32[]{:S(2)}, u32[]{:S(2)}) collective-permute-start(bf16[128,768]{1,0:T(8,128)(2,1)S(1)} %take_half.1.refs_0_), channel_id=1, source_target_pairs={{0,2},{1,3},{2,0},{3,1},{4,6},{5,7},{6,4},{7,5},{8,10},{9,11},{10,... | collective-permute-start | bytes 589832 | tf_op jit(solution)/shard_map/ppermute | solution.py:25
  6.3 4.1 %collective-permute-done.refs_1_ = bf16[128,768]{1,0:T(8,128)(2,1)S(1)} collective-permute-done((bf16[128,768]{1,0:T(8,128)(2,1)S(1)}, bf16[128,768]{1,0:T(8,128)(2,1)S(1)}, u32[]{:S(2)}, u32[]{:S(2)}) %collective-permute-start) | collective-permute-done | bytes 196640 | tf_op jit(solution)/shard_map/ppermute | solution.py:25
  10.4 2.7 %collective-permute-start.2 = (bf16[128,768]{1,0:T(8,128)(2,1)S(1)}, bf16[128,768]{1,0:T(8,128)(2,1)S(1)}, u32[]{:S(2)}, u32[]{:S(2)}) collective-permute-start(bf16[128,768]{1,0:T(8,128)(2,1)S(1)} %take_half.1.refs_0_), channel_id=1, source_target_pairs={{0,3},{1,2},{2,1},{3,0},{4,7},{5,6},{6,5},{7,4},{8,11},{9,10},{10,... | collective-permute-start | bytes 589832 | tf_op jit(solution)/shard_map/ppermute | solution.py:25
  13.1 4.9 %collective-permute-done.2.refs_3_ = bf16[128,768]{1,0:T(8,128)(2,1)S(1)} collective-permute-done((bf16[128,768]{1,0:T(8,128)(2,1)S(1)}, bf16[128,768]{1,0:T(8,128)(2,1)S(1)}, u32[]{:S(2)}, u32[]{:S(2)}) %collective-permute-start.2) | collective-permute-done | bytes 196640 | tf_op jit(solution)/shard_map/ppermute | solution.py:25
  18.0 2.0 %copy-done = bf16[1536,3,384]{2,0,1:T(8,128)(2,1)S(1)} copy-done((bf16[1536,3,384]{2,0,1:T(8,128)(2,1)S(1)}, bf16[1536,3,384]{2,0,1:T(8,128)(2,1)}, u32[]{:S(2)}) %copy-start) | copy-done | bytes 3538968
  21.6 1.9 %kv_0.1 = (bf16[128,768]{1,0:T(8,128)(2,1)S(1)}, bf16[4,128,768]{2,1,0:T(8,128)(2,1)S(1)}) custom-call(bf16[128,768]{1,0:T(8,128)(2,1)S(1)} %take_half.1.refs_0_, bf16[128,768]{1,0:T(8,128)(2,1)S(1)} %collective-permute-done.refs_1_, bf16[128,768]{1,0:T(8,128)(2,1)S(1)} %collective-permute-done.1.refs_2_, ...), custom_call_target="tpu_custom_call" | custom-call | tf_op jit(solution)/shard_map/kv_0/pallas_call | solution.py:183
  23.5 1.6 %collective-permute-start.4 = (bf16[128,768]{1,0:T(8,128)(2,1)S(1)}, bf16[128,768]{1,0:T(8,128)(2,1)S(1)}, u32[]{:S(2)}, u32[]{:S(2)}) collective-permute-start(bf16[128,768]{1,0:T(8,128)(2,1)S(1)} %get-tuple-element.18.refs_1_), channel_id=1, source_target_pairs={{0,4},{4,8},{8,12},{12,0},{1,5},{5,9},{9,13},{13,1},{2,6},{6,10},{... | collective-permute-start | bytes 589832 | tf_op jit(solution)/shard_map/ppermute | solution.py:21
  25.1 1.6 %collective-permute-start.11 = (s32[1]{0:T(128)}, s32[1]{0:T(128)}, u32[]{:S(2)}, u32[]{:S(2)}) collective-permute-start(s32[1]{0:T(128)} %param.9), channel_id=1, source_target_pairs={{0,4},{4,8},{8,12},{12,0},{1,5},{5,9},{9,13},{13,1},{2,6},{6,10},{... | collective-permute-start | bytes 20 | tf_op jit(solution)/shard_map/ppermute | solution.py:21
  27.9 3.4 %collective-permute-done.11.refs_10_ = s32[1]{0:T(128)} collective-permute-done((s32[1]{0:T(128)}, s32[1]{0:T(128)}, u32[]{:S(2)}, u32[]{:S(2)}) %collective-permute-start.11) | collective-permute-done | bytes 36 | tf_op jit(solution)/shard_map/ppermute | solution.py:21
  31.3 1.5 %collective-permute-start.13 = (s32[1]{0:T(128)}, s32[1]{0:T(128)}, u32[]{:S(2)}, u32[]{:S(2)}) collective-permute-start(s32[1]{0:T(128)} %param.9), channel_id=1, source_target_pairs={{0,12},{4,0},{8,4},{12,8},{1,13},{5,1},{9,5},{13,9},{2,14},{6,2},{... | collective-permute-start | bytes 20 | tf_op jit(solution)/shard_map/ppermute | solution.py:21
  32.8 2.3 %collective-permute-done.13.refs_12_ = s32[1]{0:T(128)} collective-permute-done((s32[1]{0:T(128)}, s32[1]{0:T(128)}, u32[]{:S(2)}, u32[]{:S(2)}) %collective-permute-start.13) | collective-permute-done | bytes 36 | tf_op jit(solution)/shard_map/ppermute | solution.py:21
  35.1 3.3 %collective-permute-start.6 = (bf16[128,768]{1,0:T(8,128)(2,1)S(1)}, bf16[128,768]{1,0:T(8,128)(2,1)S(1)}, u32[]{:S(2)}, u32[]{:S(2)}) collective-permute-start(bf16[128,768]{1,0:T(8,128)(2,1)S(1)} %get-tuple-element.18.refs_1_), channel_id=1, source_target_pairs={{0,12},{4,0},{8,4},{12,8},{1,13},{5,1},{9,5},{13,9},{2,14},{6,2},{... | collective-permute-start | bytes 589832 | tf_op jit(solution)/shard_map/ppermute | solution.py:21
  38.9 4.6 %collective-permute-done.5.refs_3_ = bf16[128,768]{1,0:T(8,128)(2,1)S(1)} collective-permute-done((bf16[128,768]{1,0:T(8,128)(2,1)S(1)}, bf16[128,768]{1,0:T(8,128)(2,1)S(1)}, u32[]{:S(2)}, u32[]{:S(2)}) %collective-permute-start.5) | collective-permute-done | bytes 196640 | tf_op jit(solution)/shard_map/ppermute | solution.py:21
  46.1 4.3 %attend_0.1 = (f32[128,768]{1,0:T(8,128)S(1)}, bf16[128,768]{1,0:T(8,128)(2,1)S(1)}, bf16[128,768]{1,0:T(8,128)(2,1)S(1)}, bf16[128,768]{1,0:T(8,128)(2,1)S(1)}) custom-call(bf16[128,384]{1,0:T(8,128)(2,1)S(1)} %q_0.1.refs_0_, bf16[128,768]{1,0:T(8,128)(2,1)S(1)} %get-tuple-element.18.refs_1_, bf16[128,768]{1,0:T(8,128)(2,1)S(1)} %collective-permute-done.4.refs_2_, ...), custom_call_target="tpu_custom_call" | custom-call | tf_op jit(solution)/shard_map/attend_0/pallas_call | solution.py:201
  50.4 1.4 %collective-permute-start.15 = (bf16[128,768]{1,0:T(8,128)(2,1)S(1)}, bf16[128,768]{1,0:T(8,128)(2,1)S(1)}, u32[]{:S(2)}, u32[]{:S(2)}) collective-permute-start(bf16[128,768]{1,0:T(8,128)(2,1)S(1)} %get-tuple-element.20), channel_id=1, source_target_pairs={{0,1},{1,0},{2,3},{3,2},{4,5},{5,4},{6,7},{7,6},{8,9},{9,8},{10,11... | collective-permute-start | bytes 589832 | tf_op jit(solution)/shard_map/ppermute | solution.py:25
  51.8 1.5 %collective-permute-start.16 = (bf16[128,768]{1,0:T(8,128)(2,1)S(1)}, bf16[128,768]{1,0:T(8,128)(2,1)S(1)}, u32[]{:S(2)}, u32[]{:S(2)}) collective-permute-start(bf16[128,768]{1,0:T(8,128)(2,1)S(1)} %get-tuple-element.21), channel_id=1, source_target_pairs={{0,2},{1,3},{2,0},{3,1},{4,6},{5,7},{6,4},{7,5},{8,10},{9,11},{10,... | collective-permute-start | bytes 589832 | tf_op jit(solution)/shard_map/ppermute | solution.py:25
  54.0 4.3 %collective-permute-done.15.refs_2_ = bf16[128,768]{1,0:T(8,128)(2,1)S(1)} collective-permute-done((bf16[128,768]{1,0:T(8,128)(2,1)S(1)}, bf16[128,768]{1,0:T(8,128)(2,1)S(1)}, u32[]{:S(2)}, u32[]{:S(2)}) %collective-permute-start.15) | collective-permute-done | bytes 196640 | tf_op jit(solution)/shard_map/ppermute | solution.py:25
  58.2 4.8 %collective-permute-done.16.refs_3_ = bf16[128,768]{1,0:T(8,128)(2,1)S(1)} collective-permute-done((bf16[128,768]{1,0:T(8,128)(2,1)S(1)}, bf16[128,768]{1,0:T(8,128)(2,1)S(1)}, u32[]{:S(2)}, u32[]{:S(2)}) %collective-permute-start.16) | collective-permute-done | bytes 196640 | tf_op jit(solution)/shard_map/ppermute | solution.py:25
  65.3 1.4 %collective-permute-start.20 = (bf16[128,768]{1,0:T(8,128)(2,1)S(1)}, bf16[128,768]{1,0:T(8,128)(2,1)S(1)}, u32[]{:S(2)}, u32[]{:S(2)}) collective-permute-start(bf16[128,768]{1,0:T(8,128)(2,1)S(1)} %join_0.1.refs_0_), channel_id=1, source_target_pairs={{0,3},{1,2},{2,1},{3,0},{4,7},{5,6},{6,5},{7,4},{8,11},{9,10},{10,... | collective-permute-start | bytes 589832 | tf_op jit(solution)/shard_map/ppermute | solution.py:25
  66.7 4.3 %collective-permute-done.18.refs_1_ = bf16[128,768]{1,0:T(8,128)(2,1)S(1)} collective-permute-done((bf16[128,768]{1,0:T(8,128)(2,1)S(1)}, bf16[128,768]{1,0:T(8,128)(2,1)S(1)}, u32[]{:S(2)}, u32[]{:S(2)}) %collective-permute-start.18) | collective-permute-done | bytes 196640 | tf_op jit(solution)/shard_map/ppermute | solution.py:25
  71.0 3.8 %collective-permute-done.19.refs_2_ = bf16[128,768]{1,0:T(8,128)(2,1)S(1)} collective-permute-done((bf16[128,768]{1,0:T(8,128)(2,1)S(1)}, bf16[128,768]{1,0:T(8,128)(2,1)S(1)}, u32[]{:S(2)}, u32[]{:S(2)}) %collective-permute-start.19) | collective-permute-done | bytes 196640 | tf_op jit(solution)/shard_map/ppermute | solution.py:25
  74.8 1.9 %kv_1.1 = (bf16[128,768]{1,0:T(8,128)(2,1)S(1)}, bf16[4,128,768]{2,1,0:T(8,128)(2,1)S(1)}) custom-call(bf16[128,768]{1,0:T(8,128)(2,1)S(1)} %join_0.1.refs_0_, bf16[128,768]{1,0:T(8,128)(2,1)S(1)} %collective-permute-done.18.refs_1_, bf16[128,768]{1,0:T(8,128)(2,1)S(1)} %collective-permute-done.19.refs_2_, ...), custom_call_target="tpu_custom_call" | custom-call | tf_op jit(solution)/shard_map/kv_1/pallas_call | solution.py:183
  76.7 2.4 %collective-permute-start.22 = (bf16[128,768]{1,0:T(8,128)(2,1)S(1)}, bf16[128,768]{1,0:T(8,128)(2,1)S(1)}, u32[]{:S(2)}, u32[]{:S(2)}) collective-permute-start(bf16[128,768]{1,0:T(8,128)(2,1)S(1)} %get-tuple-element.24.refs_1_), channel_id=1, source_target_pairs={{0,4},{4,8},{8,12},{12,0},{1,5},{5,9},{9,13},{13,1},{2,6},{6,10},{... | collective-permute-start | bytes 589832 | tf_op jit(solution)/shard_map/ppermute | solution.py:21
  79.1 1.6 %collective-permute-start.23 = (bf16[128,768]{1,0:T(8,128)(2,1)S(1)}, bf16[128,768]{1,0:T(8,128)(2,1)S(1)}, u32[]{:S(2)}, u32[]{:S(2)}) collective-permute-start(bf16[128,768]{1,0:T(8,128)(2,1)S(1)} %get-tuple-element.24.refs_1_), channel_id=1, source_target_pairs={{0,8},{4,12},{8,0},{12,4},{1,9},{5,13},{9,1},{13,5},{2,10},{6,14},... | collective-permute-start | bytes 589832 | tf_op jit(solution)/shard_map/ppermute | solution.py:21
  81.5 4.9 %collective-permute-done.22.refs_2_ = bf16[128,768]{1,0:T(8,128)(2,1)S(1)} collective-permute-done((bf16[128,768]{1,0:T(8,128)(2,1)S(1)}, bf16[128,768]{1,0:T(8,128)(2,1)S(1)}, u32[]{:S(2)}, u32[]{:S(2)}) %collective-permute-start.22) | collective-permute-done | bytes 196640 | tf_op jit(solution)/shard_map/ppermute | solution.py:21
  86.4 5.7 %collective-permute-done.23.refs_3_ = bf16[128,768]{1,0:T(8,128)(2,1)S(1)} collective-permute-done((bf16[128,768]{1,0:T(8,128)(2,1)S(1)}, bf16[128,768]{1,0:T(8,128)(2,1)S(1)}, u32[]{:S(2)}, u32[]{:S(2)}) %collective-permute-start.23) | collective-permute-done | bytes 196640 | tf_op jit(solution)/shard_map/ppermute | solution.py:21
  93.8 4.1 %attend_1.1 = (f32[128,768]{1,0:T(8,128)S(1)}, bf16[128,768]{1,0:T(8,128)(2,1)S(1)}, bf16[128,768]{1,0:T(8,128)(2,1)S(1)}, bf16[128,768]{1,0:T(8,128)(2,1)S(1)}) custom-call(bf16[128,384]{1,0:T(8,128)(2,1)S(1)} %q_1.1.refs_0_, bf16[128,768]{1,0:T(8,128)(2,1)S(1)} %get-tuple-element.24.refs_1_, bf16[128,768]{1,0:T(8,128)(2,1)S(1)} %collective-permute-done.22.refs_2_, ...), custom_call_target="tpu_custom_call" | custom-call | tf_op jit(solution)/shard_map/attend_1/pallas_call | solution.py:201
  98.5 1.7 %collective-permute-start.31 = (bf16[128,768]{1,0:T(8,128)(2,1)S(1)}, bf16[128,768]{1,0:T(8,128)(2,1)S(1)}, u32[]{:S(2)}, u32[]{:S(2)}) collective-permute-start(bf16[128,768]{1,0:T(8,128)(2,1)S(1)} %get-tuple-element.27), channel_id=1, source_target_pairs={{0,2},{1,3},{2,0},{3,1},{4,6},{5,7},{6,4},{7,5},{8,10},{9,11},{10,... | collective-permute-start | bytes 589832 | tf_op jit(solution)/shard_map/ppermute | solution.py:25
  101.4 4.3 %collective-permute-done.30.refs_2_ = bf16[128,768]{1,0:T(8,128)(2,1)S(1)} collective-permute-done((bf16[128,768]{1,0:T(8,128)(2,1)S(1)}, bf16[128,768]{1,0:T(8,128)(2,1)S(1)}, u32[]{:S(2)}, u32[]{:S(2)}) %collective-permute-start.30) | collective-permute-done | bytes 196640 | tf_op jit(solution)/shard_map/ppermute | solution.py:25
  105.7 3.8 %collective-permute-done.31.refs_3_ = bf16[128,768]{1,0:T(8,128)(2,1)S(1)} collective-permute-done((bf16[128,768]{1,0:T(8,128)(2,1)S(1)}, bf16[128,768]{1,0:T(8,128)(2,1)S(1)}, u32[]{:S(2)}, u32[]{:S(2)}) %collective-permute-start.31) | collective-permute-done | bytes 196640 | tf_op jit(solution)/shard_map/ppermute | solution.py:25
  109.7 1.4 %collective-permute-done.33 = bf16[128,768]{1,0:T(8,128)(2,1)S(1)} collective-permute-done((bf16[128,768]{1,0:T(8,128)(2,1)S(1)}, bf16[128,768]{1,0:T(8,128)(2,1)S(1)}, u32[]{:S(2)}, u32[]{:S(2)}) %collective-permute-start.33) | collective-permute-done | bytes 196640 | tf_op jit(solution)/shard_map/ppermute | solution.py:25
  (66 shorter events, 15.6 us)
Async XLA Ops:
  0.0 18.0 %collective-permute-start.3 = (bf16[3,1536,384]{2,1,0:T(8,128)(2,1)}, bf16[3,1536,384]{2,1,0:T(8,128)(2,1)S(1)}, u32[]{:S(2)}, u32[]{:S(2)}) collective-permute-start(bf16[3,1536,384]{2,1,0:T(8,128)(2,1)} %bitcast.5), channel_id=1, source_target_pairs={{0,16},{16,0},{1,17},{17,1},{2,18},{18,2},{3,19},{19,3},{4,20},{20... | collective-permute-start | bytes 10616840 | tf_op jit(solution)/shard_map/ppermute | solution.py:25
  0.5 66.2 %collective-permute-start.21 = (bf16[3,1536,384]{2,1,0:T(8,128)(2,1)}, bf16[3,1536,384]{2,1,0:T(8,128)(2,1)S(1)}, u32[]{:S(2)}, u32[]{:S(2)}) collective-permute-start(bf16[3,1536,384]{2,1,0:T(8,128)(2,1)} %bitcast.8), channel_id=1, source_target_pairs={{0,16},{16,0},{1,17},{17,1},{2,18},{18,2},{3,19},{19,3},{4,20},{20... | collective-permute-start | bytes 10616840 | tf_op jit(solution)/shard_map/ppermute | solution.py:25
  0.5 37.9 %collective-permute-start.14 = (bf16[384,1536]{1,0:T(8,128)(2,1)}, bf16[384,1536]{1,0:T(8,128)(2,1)S(1)}, u32[]{:S(2)}, u32[]{:S(2)}) collective-permute-start(bf16[384,1536]{1,0:T(8,128)(2,1)} %refs_13_.2), channel_id=1, source_target_pairs={{0,16},{16,0},{1,17},{17,1},{2,18},{18,2},{3,19},{19,3},{4,20},{20... | collective-permute-start | bytes 3538952 | tf_op jit(solution)/shard_map/ppermute | solution.py:25
  2.2 8.1 %collective-permute-start = (bf16[128,768]{1,0:T(8,128)(2,1)S(1)}, bf16[128,768]{1,0:T(8,128)(2,1)S(1)}, u32[]{:S(2)}, u32[]{:S(2)}) collective-permute-start(bf16[128,768]{1,0:T(8,128)(2,1)S(1)} %take_half.1.refs_0_), channel_id=1, source_target_pairs={{0,1},{1,0},{2,3},{3,2},{4,5},{5,4},{6,7},{7,6},{8,9},{9,8},{10,11... | collective-permute-start | bytes 589832 | tf_op jit(solution)/shard_map/ppermute | solution.py:25
  4.8 8.3 %collective-permute-start.1 = (bf16[128,768]{1,0:T(8,128)(2,1)S(1)}, bf16[128,768]{1,0:T(8,128)(2,1)S(1)}, u32[]{:S(2)}, u32[]{:S(2)}) collective-permute-start(bf16[128,768]{1,0:T(8,128)(2,1)S(1)} %take_half.1.refs_0_), channel_id=1, source_target_pairs={{0,2},{1,3},{2,0},{3,1},{4,6},{5,7},{6,4},{7,5},{8,10},{9,11},{10,... | collective-permute-start | bytes 589832 | tf_op jit(solution)/shard_map/ppermute | solution.py:25
  10.4 7.6 %collective-permute-start.2 = (bf16[128,768]{1,0:T(8,128)(2,1)S(1)}, bf16[128,768]{1,0:T(8,128)(2,1)S(1)}, u32[]{:S(2)}, u32[]{:S(2)}) collective-permute-start(bf16[128,768]{1,0:T(8,128)(2,1)S(1)} %take_half.1.refs_0_), channel_id=1, source_target_pairs={{0,3},{1,2},{2,1},{3,0},{4,7},{5,6},{6,5},{7,4},{8,11},{9,10},{10,... | collective-permute-start | bytes 589832 | tf_op jit(solution)/shard_map/ppermute | solution.py:25
  23.5 15.0 %collective-permute-start.4 = (bf16[128,768]{1,0:T(8,128)(2,1)S(1)}, bf16[128,768]{1,0:T(8,128)(2,1)S(1)}, u32[]{:S(2)}, u32[]{:S(2)}) collective-permute-start(bf16[128,768]{1,0:T(8,128)(2,1)S(1)} %get-tuple-element.18.refs_1_), channel_id=1, source_target_pairs={{0,4},{4,8},{8,12},{12,0},{1,5},{5,9},{9,13},{13,1},{2,6},{6,10},{... | collective-permute-start | bytes 589832 | tf_op jit(solution)/shard_map/ppermute | solution.py:21
  25.1 6.2 %collective-permute-start.11 = (s32[1]{0:T(128)}, s32[1]{0:T(128)}, u32[]{:S(2)}, u32[]{:S(2)}) collective-permute-start(s32[1]{0:T(128)} %param.9), channel_id=1, source_target_pairs={{0,4},{4,8},{8,12},{12,0},{1,5},{5,9},{9,13},{13,1},{2,6},{6,10},{... | collective-permute-start | bytes 20 | tf_op jit(solution)/shard_map/ppermute | solution.py:21
  26.6 6.2 %collective-permute-start.12 = (s32[1]{0:T(128)}, s32[1]{0:T(128)}, u32[]{:S(2)}, u32[]{:S(2)}) collective-permute-start(s32[1]{0:T(128)} %param.9), channel_id=1, source_target_pairs={{0,8},{4,12},{8,0},{12,4},{1,9},{5,13},{9,1},{13,5},{2,10},{6,14},... | collective-permute-start | bytes 20 | tf_op jit(solution)/shard_map/ppermute | solution.py:21
  31.3 3.8 %collective-permute-start.13 = (s32[1]{0:T(128)}, s32[1]{0:T(128)}, u32[]{:S(2)}, u32[]{:S(2)}) collective-permute-start(s32[1]{0:T(128)} %param.9), channel_id=1, source_target_pairs={{0,12},{4,0},{8,4},{12,8},{1,13},{5,1},{9,5},{13,9},{2,14},{6,2},{... | collective-permute-start | bytes 20 | tf_op jit(solution)/shard_map/ppermute | solution.py:21
  32.8 10.7 %collective-permute-start.5 = (bf16[128,768]{1,0:T(8,128)(2,1)S(1)}, bf16[128,768]{1,0:T(8,128)(2,1)S(1)}, u32[]{:S(2)}, u32[]{:S(2)}) collective-permute-start(bf16[128,768]{1,0:T(8,128)(2,1)S(1)} %get-tuple-element.18.refs_1_), channel_id=1, source_target_pairs={{0,8},{4,12},{8,0},{12,4},{1,9},{5,13},{9,1},{13,5},{2,10},{6,14},... | collective-permute-start | bytes 589832 | tf_op jit(solution)/shard_map/ppermute | solution.py:21
  35.1 8.5 %collective-permute-start.6 = (bf16[128,768]{1,0:T(8,128)(2,1)S(1)}, bf16[128,768]{1,0:T(8,128)(2,1)S(1)}, u32[]{:S(2)}, u32[]{:S(2)}) collective-permute-start(bf16[128,768]{1,0:T(8,128)(2,1)S(1)} %get-tuple-element.18.refs_1_), channel_id=1, source_target_pairs={{0,12},{4,0},{8,4},{12,8},{1,13},{5,1},{9,5},{13,9},{2,14},{6,2},{... | collective-permute-start | bytes 589832 | tf_op jit(solution)/shard_map/ppermute | solution.py:21
  38.4 5.6 %collective-permute-start.7 = (bf16[128,768]{1,0:T(8,128)(2,1)S(1)}, bf16[128,768]{1,0:T(8,128)(2,1)S(1)}, u32[]{:S(2)}, u32[]{:S(2)}) collective-permute-start(bf16[128,768]{1,0:T(8,128)(2,1)S(1)} %get-tuple-element.18.refs_1_), channel_id=1, source_target_pairs={{0,16},{16,0},{1,17},{17,1},{2,18},{18,2},{3,19},{19,3},{4,20},{20... | collective-permute-start | bytes 589832 | tf_op jit(solution)/shard_map/ppermute | solution.py:25
  38.4 54.8 %collective-permute-start.29 = (bf16[384,1536]{1,0:T(8,128)(2,1)S(1)}, bf16[384,1536]{1,0:T(8,128)(2,1)S(1)}, u32[]{:S(2)}, u32[]{:S(2)}) collective-permute-start(bf16[384,1536]{1,0:T(8,128)(2,1)S(1)} %copy-done.6), channel_id=1, source_target_pairs={{0,16},{16,0},{1,17},{17,1},{2,18},{18,2},{3,19},{19,3},{4,20},{20... | collective-permute-start | bytes 3538952 | tf_op jit(solution)/shard_map/ppermute | solution.py:25
  43.6 2.0 %collective-permute-start.8 = (bf16[128,768]{1,0:T(8,128)(2,1)S(1)}, bf16[128,768]{1,0:T(8,128)(2,1)S(1)}, u32[]{:S(2)}, u32[]{:S(2)}) collective-permute-start(bf16[128,768]{1,0:T(8,128)(2,1)S(1)} %collective-permute-done.4.refs_2_), channel_id=1, source_target_pairs={{0,16},{16,0},{1,17},{17,1},{2,18},{18,2},{3,19},{19,3},{4,20},{20... | collective-permute-start | bytes 589832 | tf_op jit(solution)/shard_map/ppermute | solution.py:25
  43.6 2.0 %collective-permute-start.9 = (bf16[128,768]{1,0:T(8,128)(2,1)S(1)}, bf16[128,768]{1,0:T(8,128)(2,1)S(1)}, u32[]{:S(2)}, u32[]{:S(2)}) collective-permute-start(bf16[128,768]{1,0:T(8,128)(2,1)S(1)} %collective-permute-done.5.refs_3_), channel_id=1, source_target_pairs={{0,16},{16,0},{1,17},{17,1},{2,18},{18,2},{3,19},{19,3},{4,20},{20... | collective-permute-start | bytes 589832 | tf_op jit(solution)/shard_map/ppermute | solution.py:25
  50.4 7.8 %collective-permute-start.15 = (bf16[128,768]{1,0:T(8,128)(2,1)S(1)}, bf16[128,768]{1,0:T(8,128)(2,1)S(1)}, u32[]{:S(2)}, u32[]{:S(2)}) collective-permute-start(bf16[128,768]{1,0:T(8,128)(2,1)S(1)} %get-tuple-element.20), channel_id=1, source_target_pairs={{0,1},{1,0},{2,3},{3,2},{4,5},{5,4},{6,7},{7,6},{8,9},{9,8},{10,11... | collective-permute-start | bytes 589832 | tf_op jit(solution)/shard_map/ppermute | solution.py:25
  51.8 11.2 %collective-permute-start.16 = (bf16[128,768]{1,0:T(8,128)(2,1)S(1)}, bf16[128,768]{1,0:T(8,128)(2,1)S(1)}, u32[]{:S(2)}, u32[]{:S(2)}) collective-permute-start(bf16[128,768]{1,0:T(8,128)(2,1)S(1)} %get-tuple-element.21), channel_id=1, source_target_pairs={{0,2},{1,3},{2,0},{3,1},{4,6},{5,7},{6,4},{7,5},{8,10},{9,11},{10,... | collective-permute-start | bytes 589832 | tf_op jit(solution)/shard_map/ppermute | solution.py:25
  53.4 9.7 %collective-permute-start.17 = (bf16[128,768]{1,0:T(8,128)(2,1)S(1)}, bf16[128,768]{1,0:T(8,128)(2,1)S(1)}, u32[]{:S(2)}, u32[]{:S(2)}) collective-permute-start(bf16[128,768]{1,0:T(8,128)(2,1)S(1)} %get-tuple-element.22), channel_id=1, source_target_pairs={{0,3},{1,2},{2,1},{3,0},{4,7},{5,6},{6,5},{7,4},{8,11},{9,10},{10,... | collective-permute-start | bytes 589832 | tf_op jit(solution)/shard_map/ppermute | solution.py:25
  63.2 7.8 %collective-permute-start.18 = (bf16[128,768]{1,0:T(8,128)(2,1)S(1)}, bf16[128,768]{1,0:T(8,128)(2,1)S(1)}, u32[]{:S(2)}, u32[]{:S(2)}) collective-permute-start(bf16[128,768]{1,0:T(8,128)(2,1)S(1)} %join_0.1.refs_0_), channel_id=1, source_target_pairs={{0,1},{1,0},{2,3},{3,2},{4,5},{5,4},{6,7},{7,6},{8,9},{9,8},{10,11... | collective-permute-start | bytes 589832 | tf_op jit(solution)/shard_map/ppermute | solution.py:25
  64.5 10.3 %collective-permute-start.19 = (bf16[128,768]{1,0:T(8,128)(2,1)S(1)}, bf16[128,768]{1,0:T(8,128)(2,1)S(1)}, u32[]{:S(2)}, u32[]{:S(2)}) collective-permute-start(bf16[128,768]{1,0:T(8,128)(2,1)S(1)} %join_0.1.refs_0_), channel_id=1, source_target_pairs={{0,2},{1,3},{2,0},{3,1},{4,6},{5,7},{6,4},{7,5},{8,10},{9,11},{10,... | collective-permute-start | bytes 589832 | tf_op jit(solution)/shard_map/ppermute | solution.py:25
  65.3 9.5 %collective-permute-start.20 = (bf16[128,768]{1,0:T(8,128)(2,1)S(1)}, bf16[128,768]{1,0:T(8,128)(2,1)S(1)}, u32[]{:S(2)}, u32[]{:S(2)}) collective-permute-start(bf16[128,768]{1,0:T(8,128)(2,1)S(1)} %join_0.1.refs_0_), channel_id=1, source_target_pairs={{0,3},{1,2},{2,1},{3,0},{4,7},{5,6},{6,5},{7,4},{8,11},{9,10},{10,... | collective-permute-start | bytes 589832 | tf_op jit(solution)/shard_map/ppermute | solution.py:25
  76.7 9.7 %collective-permute-start.22 = (bf16[128,768]{1,0:T(8,128)(2,1)S(1)}, bf16[128,768]{1,0:T(8,128)(2,1)S(1)}, u32[]{:S(2)}, u32[]{:S(2)}) collective-permute-start(bf16[128,768]{1,0:T(8,128)(2,1)S(1)} %get-tuple-element.24.refs_1_), channel_id=1, source_target_pairs={{0,4},{4,8},{8,12},{12,0},{1,5},{5,9},{9,13},{13,1},{2,6},{6,10},{... | collective-permute-start | bytes 589832 | tf_op jit(solution)/shard_map/ppermute | solution.py:21
  79.1 13.0 %collective-permute-start.23 = (bf16[128,768]{1,0:T(8,128)(2,1)S(1)}, bf16[128,768]{1,0:T(8,128)(2,1)S(1)}, u32[]{:S(2)}, u32[]{:S(2)}) collective-permute-start(bf16[128,768]{1,0:T(8,128)(2,1)S(1)} %get-tuple-element.24.refs_1_), channel_id=1, source_target_pairs={{0,8},{4,12},{8,0},{12,4},{1,9},{5,13},{9,1},{13,5},{2,10},{6,14},... | collective-permute-start | bytes 589832 | tf_op jit(solution)/shard_map/ppermute | solution.py:21
  80.7 11.4 %collective-permute-start.24 = (bf16[128,768]{1,0:T(8,128)(2,1)S(1)}, bf16[128,768]{1,0:T(8,128)(2,1)S(1)}, u32[]{:S(2)}, u32[]{:S(2)}) collective-permute-start(bf16[128,768]{1,0:T(8,128)(2,1)S(1)} %get-tuple-element.24.refs_1_), channel_id=1, source_target_pairs={{0,12},{4,0},{8,4},{12,8},{1,13},{5,1},{9,5},{13,9},{2,14},{6,2},{... | collective-permute-start | bytes 589832 | tf_op jit(solution)/shard_map/ppermute | solution.py:21
  81.5 11.8 %collective-permute-start.25 = (bf16[128,768]{1,0:T(8,128)(2,1)S(1)}, bf16[128,768]{1,0:T(8,128)(2,1)S(1)}, u32[]{:S(2)}, u32[]{:S(2)}) collective-permute-start(bf16[128,768]{1,0:T(8,128)(2,1)S(1)} %get-tuple-element.24.refs_1_), channel_id=1, source_target_pairs={{0,16},{16,0},{1,17},{17,1},{2,18},{18,2},{3,19},{19,3},{4,20},{20... | collective-permute-start | bytes 589832 | tf_op jit(solution)/shard_map/ppermute | solution.py:25
  86.4 6.9 %collective-permute-start.26 = (bf16[128,768]{1,0:T(8,128)(2,1)S(1)}, bf16[128,768]{1,0:T(8,128)(2,1)S(1)}, u32[]{:S(2)}, u32[]{:S(2)}) collective-permute-start(bf16[128,768]{1,0:T(8,128)(2,1)S(1)} %collective-permute-done.22.refs_2_), channel_id=1, source_target_pairs={{0,16},{16,0},{1,17},{17,1},{2,18},{18,2},{3,19},{19,3},{4,20},{20... | collective-permute-start | bytes 589832 | tf_op jit(solution)/shard_map/ppermute | solution.py:25
  92.1 1.7 %collective-permute-start.28 = (bf16[128,768]{1,0:T(8,128)(2,1)S(1)}, bf16[128,768]{1,0:T(8,128)(2,1)S(1)}, u32[]{:S(2)}, u32[]{:S(2)}) collective-permute-start(bf16[128,768]{1,0:T(8,128)(2,1)S(1)} %collective-permute-done.24.refs_4_), channel_id=1, source_target_pairs={{0,16},{16,0},{1,17},{17,1},{2,18},{18,2},{3,19},{19,3},{4,20},{20... | collective-permute-start | bytes 589832 | tf_op jit(solution)/shard_map/ppermute | solution.py:25
  97.9 7.8 %collective-permute-start.30 = (bf16[128,768]{1,0:T(8,128)(2,1)S(1)}, bf16[128,768]{1,0:T(8,128)(2,1)S(1)}, u32[]{:S(2)}, u32[]{:S(2)}) collective-permute-start(bf16[128,768]{1,0:T(8,128)(2,1)S(1)} %get-tuple-element.26), channel_id=1, source_target_pairs={{0,1},{1,0},{2,3},{3,2},{4,5},{5,4},{6,7},{7,6},{8,9},{9,8},{10,11... | collective-permute-start | bytes 589832 | tf_op jit(solution)/shard_map/ppermute | solution.py:25
  98.5 11.0 %collective-permute-start.31 = (bf16[128,768]{1,0:T(8,128)(2,1)S(1)}, bf16[128,768]{1,0:T(8,128)(2,1)S(1)}, u32[]{:S(2)}, u32[]{:S(2)}) collective-permute-start(bf16[128,768]{1,0:T(8,128)(2,1)S(1)} %get-tuple-element.27), channel_id=1, source_target_pairs={{0,2},{1,3},{2,0},{3,1},{4,6},{5,7},{6,4},{7,5},{8,10},{9,11},{10,... | collective-permute-start | bytes 589832 | tf_op jit(solution)/shard_map/ppermute | solution.py:25
  100.2 9.2 %collective-permute-start.32 = (bf16[128,768]{1,0:T(8,128)(2,1)S(1)}, bf16[128,768]{1,0:T(8,128)(2,1)S(1)}, u32[]{:S(2)}, u32[]{:S(2)}) collective-permute-start(bf16[128,768]{1,0:T(8,128)(2,1)S(1)} %get-tuple-element.28), channel_id=1, source_target_pairs={{0,3},{1,2},{2,1},{3,0},{4,7},{5,6},{6,5},{7,4},{8,11},{9,10},{10,... | collective-permute-start | bytes 589832 | tf_op jit(solution)/shard_map/ppermute | solution.py:25
  109.6 1.5 %collective-permute-start.33 = (bf16[128,768]{1,0:T(8,128)(2,1)S(1)}, bf16[128,768]{1,0:T(8,128)(2,1)S(1)}, u32[]{:S(2)}, u32[]{:S(2)}) collective-permute-start(bf16[128,768]{1,0:T(8,128)(2,1)S(1)} %broadcast_select_fusion.2), channel_id=1, source_target_pairs={{0,16},{16,0},{1,17},{17,1},{2,18},{18,2},{3,19},{19,3},{4,20},{20... | collective-permute-start | bytes 589832 | tf_op jit(solution)/shard_map/ppermute | solution.py:25
  (11 other events, 95.7 us)

commit v3 on v2

v3 whole, which is shorter than its diff:
```python
import functools
import math

import jax
import jax.numpy as jnp
from jax import lax
from jax.experimental import pallas as pl
from jax.experimental.pallas import tpu as pltpu
from jax.sharding import PartitionSpec as P


HEAD_DIM = 128
EPS = 1e-06
F32 = jnp.float32
BF16 = jnp.bfloat16
VMEM = pl.BlockSpec(memory_space=pltpu.VMEM)
SMEM = pl.BlockSpec(memory_space=pltpu.SMEM)
FAR = pl.BlockSpec(memory_space=pl.ANY)
MIB = 1 << 20
SHAPE = jax.ShapeDtypeStruct


def turn(x, axis, k, n):
    return lax.ppermute(x, axis, [(i, (i + k) % n) for i in range(n)])


def cross(x, axis, k, n):
    return lax.ppermute(x, axis, [(i, i ^ k) for i in range(n)])


def swap(x):
    return lax.ppermute(x, "branch", [(0, 1), (1, 0)])


def far(x):
    return pltpu.with_memory_space_constraint(x, pltpu.HBM)


def params(mib):
    return pltpu.CompilerParams(vmem_limit_bytes=mib * MIB)


def half_kernel(tok_ref, out_ref, sem):
    rows = out_ref.shape[0]
    start = pl.multiple_of(lax.axis_index("branch") * rows, rows)
    copy = pltpu.make_async_copy(tok_ref.at[pl.ds(start, rows)], out_ref, sem)
    copy.start()
    copy.wait()


def take_half(tokens, n_branch):
    rows, cols = tokens.shape
    return pl.pallas_call(
        half_kernel,
        out_shape=SHAPE((rows // n_branch, cols), tokens.dtype),
        in_specs=[FAR],
        out_specs=VMEM,
        scratch_shapes=[pltpu.SemaphoreType.DMA],
        compiler_params=params(4),
        name="take_half",
    )(far(tokens))


def prep_kernel(n_head, *refs):
    far_qkv, near_ref, across_ref, far_mod, far_gain = refs[:5]
    qkv_ref, mod_ref, gain_ref = refs[5:8]
    pieces = refs[8 : 9 + n_head]
    sems = refs[9 + n_head]
    copies = [
        pltpu.make_async_copy(src, dst, sems.at[i])
        for i, (src, dst) in enumerate(
            ((far_qkv, qkv_ref), (far_mod, mod_ref), (far_gain, gain_ref))
        )
    ]
    for copy in copies:
        copy.start()
    b = lax.axis_index("branch")
    h = lax.axis_index("head")
    per_core = n_head // 2
    part = pieces[0].shape[1]
    for k in range(n_head + 1):
        j = h ^ (k % n_head)
        half = b if k < n_head else 1 - b
        at = pl.ds(pl.multiple_of(lax.rem(j, per_core) * 2 * part + half * part, part), part)
        mine = lax.div(j, per_core) == b
        piece = pieces[k]

        @pl.when(mine)
        def _():
            piece[...] = near_ref[:, at]

        @pl.when(jnp.logical_not(mine))
        def _():
            piece[...] = across_ref[:, at]

    for copy in copies:
        copy.wait()


def contract(moded_ref, own_ref, other_ref, which, n_head):
    b = lax.axis_index("branch")
    h = lax.axis_index("head")
    quarter = moded_ref.shape[2]
    per_core = n_head // 2
    total = None
    for ref, core in ((own_ref, b), (other_ref, 1 - b)):
        for i in range(per_core):
            piece = moded_ref[(core * per_core + i) ^ h]
            term = jnp.dot(
                piece,
                ref[which, i * quarter : (i + 1) * quarter, :],
                preferred_element_type=F32,
            )
            total = term if total is None else total + term
    return total


def norm_heads(part, gain, width):
    outs = []
    for lo in range(0, width, HEAD_DIM):
        one = part[:, lo : lo + HEAD_DIM]
        scale = lax.rsqrt(jnp.mean(one * one, axis=1, keepdims=True) + EPS)
        outs.append((one * scale * gain).astype(BF16))
    return outs


def kv_kernel(blk, n_head, *refs):
    xs = refs[:n_head]
    own_ref, other_ref, mod_ref, gain_ref, packed_ref, moded_ref = refs[n_head:]
    h = lax.axis_index("head")
    quarter = xs[0].shape[1]
    width = own_ref.shape[2]
    total = sum(jnp.sum(x[...].astype(F32), axis=1, keepdims=True) for x in xs)
    mean = total / (n_head * quarter)
    square = 0.0
    for x in xs:
        centered = x[...].astype(F32) - mean
        square = square + jnp.sum(centered * centered, axis=1, keepdims=True)
    scale = lax.rsqrt(square / (n_head * quarter) + EPS)
    for k, x in enumerate(xs):
        at = pl.ds(pl.multiple_of((h ^ k) * quarter, quarter), quarter)
        shift = mod_ref[0, blk : blk + 1, at]
        gain = mod_ref[1, blk : blk + 1, at] + 1.0
        normed = (x[...].astype(F32) - mean) * scale
        moded_ref[k] = (normed * gain + shift).astype(BF16)
    key = contract(moded_ref, own_ref, other_ref, 1, n_head)
    for i, out in enumerate(norm_heads(key, gain_ref[blk, 1:2, :], width)):
        packed_ref[:, i * HEAD_DIM : (i + 1) * HEAD_DIM] = out
    packed_ref[:, width:] = contract(moded_ref, own_ref, other_ref, 2, n_head).astype(BF16)


def q_kernel(blk, n_head, moded_ref, own_ref, other_ref, gain_ref, query_ref):
    width = own_ref.shape[2]
    query = contract(moded_ref, own_ref, other_ref, 0, n_head)
    for i, out in enumerate(norm_heads(query, gain_ref[blk, 0:1, :], width)):
        query_ref[:, i * HEAD_DIM : (i + 1) * HEAD_DIM] = out


def drop_kernel(n_seq, *refs):
    counts, out_ref = refs[:n_seq], refs[n_seq]
    b = lax.axis_index("branch")
    rows = out_ref.shape[1]
    lane = lax.broadcasted_iota(jnp.int32, (1, rows), 1)
    for i in range(2 * n_seq):
        core = b if i < n_seq else 1 - b
        out_ref[i : i + 1, :] = jnp.where(
            lane + core * rows < counts[i % n_seq][0], 0.0, -1e30
        ).astype(F32)


def scan_keys(query, at, pairs, drop_ref):
    scale = math.log2(math.e) / HEAD_DIM**0.5
    scores = []
    for ref, i in pairs:
        one = lax.dot_general(
            query, ref[:, at], (((1,), (1,)), ((), ())), preferred_element_type=F32
        )
        scores.append(one * scale + drop_ref[i : i + 1, :])
    return scores


def weigh(scores, peak, pairs, width, lo):
    mixed = None
    total = None
    for one, (ref, _) in zip(scores, pairs):
        weight = jnp.exp2(one - peak)
        total = weight if total is None else total + weight
        term = jnp.dot(
            weight.astype(BF16),
            ref[:, width + lo : width + lo + HEAD_DIM],
            preferred_element_type=F32,
        )
        mixed = term if mixed is None else mixed + term
    return mixed, jnp.sum(total, axis=1, keepdims=True)


def key_pairs(blocks, order, n_seq):
    n = len(order)
    return [(blocks[i], order[i]) for i in range(n)] + [
        (blocks[n + i], n_seq + order[i]) for i in range(n)
    ]


def first_kernel(order, n_seq, *refs):
    query_ref = refs[0]
    n = 2 * len(order)
    blocks, drop_ref = refs[1 : 1 + n], refs[1 + n]
    mixed_ref, stat_ref = refs[2 + n :]
    width = query_ref.shape[1]
    pairs = key_pairs(blocks, order, n_seq)
    for i, lo in enumerate(range(0, width, HEAD_DIM)):
        at = slice(lo, lo + HEAD_DIM)
        scores = scan_keys(query_ref[:, at], at, pairs, drop_ref)
        peak = jnp.max(functools.reduce(jnp.maximum, scores), axis=1, keepdims=True)
        mixed, total = weigh(scores, peak, pairs, width, lo)
        mixed_ref[:, at] = mixed
        stat_ref[0, :, i : i + 1] = peak
        stat_ref[1, :, i : i + 1] = total


def last_kernel(order, n_seq, *refs):
    query_ref = refs[0]
    n = 2 * len(order)
    blocks, drop_ref = refs[1 : 1 + n], refs[1 + n]
    mixed_ref, stat_ref, out_ref = refs[2 + n :]
    width = query_ref.shape[1]
    pairs = key_pairs(blocks, order, n_seq)
    for i, lo in enumerate(range(0, width, HEAD_DIM)):
        at = slice(lo, lo + HEAD_DIM)
        scores = scan_keys(query_ref[:, at], at, pairs, drop_ref)
        before = stat_ref[0, :, i : i + 1]
        peak = jnp.max(functools.reduce(jnp.maximum, scores), axis=1, keepdims=True)
        peak = jnp.maximum(peak, before)
        mixed, total = weigh(scores, peak, pairs, width, lo)
        keep = jnp.exp2(before - peak)
        mixed = mixed + mixed_ref[:, at] * keep
        total = total + stat_ref[1, :, i : i + 1] * keep
        out_ref[:, at] = (mixed / total).astype(BF16)


def out_kernel(blk, n_head, *refs):
    attended = refs[:n_head]
    mine = refs[n_head : 2 * n_head]
    others = refs[2 * n_head : 3 * n_head]
    x_ref, mod_ref, out_ref = refs[3 * n_head :]
    b = lax.axis_index("branch")
    h = lax.axis_index("head")
    quarter = x_ref.shape[1]
    part = mine[0].shape[1]
    for weights, core in ((mine, b), (others, 1 - b)):
        total = None
        for value, weight in zip(attended, weights):
            term = jnp.dot(value[...], weight[...], preferred_element_type=F32)
            total = term if total is None else total + term
        start = pl.multiple_of(core * part, part)
        at = pl.ds(pl.multiple_of(h * quarter + start, part), part)
        here = pl.ds(start, part)
        gate = mod_ref[2, blk : blk + 1, at]
        out_ref[:, here] = (x_ref[:, here].astype(F32) + gate * total).astype(BF16)


def join_kernel(strong_ref, forked_ref, got_ref, out_ref):
    b = lax.axis_index("branch")
    rows = strong_ref.shape[0]

    @pl.when(b == 0)
    def _():
        out_ref[:rows, :] = strong_ref[...]
        out_ref[rows:, :] = got_ref[...]

    @pl.when(b != 0)
    def _():
        out_ref[:rows, :] = got_ref[...]
        out_ref[rows:, :] = forked_ref[...]


def block(tokens, x, valid, weights, outs, mod, gains, blk, sizes, later):
    n_branch, n_seq, n_head = sizes
    if blk == 0:
        weights = (weights, swap(weights))
        outs = (outs, swap(outs))
        x = take_half(tokens, n_branch)
    rows, quarter = x.shape
    width = weights[0].shape[2]
    part = quarter // n_branch
    pieces = [x] + [cross(x, "head", k, n_head) for k in range(1, n_head)]
    if blk == 0:
        valid = [valid] + [turn(valid, "seq", k, n_seq) for k in range(1, n_seq)]
        valid = pl.pallas_call(
            functools.partial(drop_kernel, n_seq),
            out_shape=SHAPE((2 * n_seq, rows), F32),
            in_specs=[SMEM] * n_seq,
            out_specs=VMEM,
            compiler_params=params(4),
            name="drop",
        )(*valid)
    own, mod, gains, *spread = pl.pallas_call(
        functools.partial(prep_kernel, n_head),
        out_shape=[SHAPE(weights[0].shape, BF16), SHAPE(mod.shape, F32), SHAPE(gains.shape, F32)]
        + [SHAPE((width, part), BF16)] * (n_head + 1),
        in_specs=[FAR, VMEM, VMEM, FAR, FAR],
        out_specs=[VMEM] * (n_head + 4),
        scratch_shapes=[pltpu.SemaphoreType.DMA((3,))],
        compiler_params=params(16),
    )(far(weights[0]), *outs, far(mod), far(gains))
    weights = (own, weights[1])
    packed, moded = pl.pallas_call(
        functools.partial(kv_kernel, blk, n_head),
        out_shape=(SHAPE((rows, 2 * width), BF16), SHAPE((n_head, rows, quarter), BF16)),
        in_specs=[VMEM] * (n_head + 4),
        out_specs=(VMEM, VMEM),
        compiler_params=params(16),
    )(*pieces, *weights, mod, gains)
    blocks = [packed] + [turn(packed, "seq", k, n_seq) for k in range(1, n_seq)]
    mine = [spread[0]] + [cross(spread[k], "head", k, n_head) for k in range(1, n_head)]
    query = pl.pallas_call(
        functools.partial(q_kernel, blk, n_head),
        out_shape=SHAPE((rows, width), BF16),
        in_specs=[VMEM] * 4,
        out_specs=VMEM,
        compiler_params=params(16),
    )(moded, *weights, gains)
    if blk == 0:
        qkv, out_weight = later
        later = ((qkv, swap(qkv)), (out_weight, swap(out_weight)))
    partner = [swap(p) for p in blocks]
    others = [spread[n_head]] + [swap(p) for p in mine[1:]]
    cut = max(1, n_seq // 2)
    early, late = tuple(range(cut)), tuple(range(cut, n_seq))
    pick = lambda which: [blocks[i] for i in which] + [partner[i] for i in which]
    mixed, stat = pl.pallas_call(
        functools.partial(first_kernel, early, n_seq),
        out_shape=(SHAPE((rows, width), F32), SHAPE((2, rows, HEAD_DIM), F32)),
        in_specs=[VMEM] * (2 + 2 * len(early)),
        out_specs=(VMEM, VMEM),
        compiler_params=params(16),
    )(query, *pick(early), valid)
    attended = pl.pallas_call(
        functools.partial(last_kernel, late, n_seq),
        out_shape=SHAPE((rows, width), BF16),
        in_specs=[VMEM] * (4 + 2 * len(late)),
        out_specs=VMEM,
        compiler_params=params(16),
    )(query, *pick(late), valid, mixed, stat)
    gathered = [attended] + [cross(attended, "head", k, n_head) for k in range(1, n_head)]
    out = pl.pallas_call(
        functools.partial(out_kernel, blk, n_head),
        out_shape=SHAPE((rows, quarter), BF16),
        in_specs=[VMEM] * (3 * n_head + 2),
        out_specs=VMEM,
        compiler_params=params(16),
    )(*gathered, *mine, *others, x, mod)
    return out, valid, later


def solution(mesh):
    sizes = tuple(mesh.shape[a] for a in ("branch", "seq", "head"))

    def per_device(
        tokens, valid_counts, shared_qkv, shared_out, skipped_qkv, skipped_out, modulation, qk_gains
    ):
        b = lax.axis_index("branch")
        mod = modulation.transpose(1, 0, 2)
        later = skipped_qkv.transpose(1, 0, 2), skipped_out
        forked, valid, later = block(
            tokens, None, valid_counts, shared_qkv.transpose(1, 0, 2), shared_out, mod,
            qk_gains, 0, sizes, later,
        )
        strong, _, _ = block(None, forked, valid, *later, mod, qk_gains, 1, sizes, None)
        got = swap(jnp.where(b == 0, forked, strong))
        rows, quarter = strong.shape
        out = pl.pallas_call(
            join_kernel,
            out_shape=SHAPE((2 * rows, quarter), BF16),
            in_specs=[VMEM] * 3,
            out_specs=VMEM,
            compiler_params=params(8),
            name="join",
        )(strong, forked, got)
        return out[None]

    in_specs = (
        P("seq", "head"),
        P("seq"),
        P("branch", None, "head"),
        P("head", "branch"),
        P("branch", None, "head"),
        P("head", "branch"),
        P(),
        P(),
    )
    return jax.shard_map(
        per_device,
        mesh=mesh,
        in_specs=in_specs,
        out_specs=P("branch", "seq", "head"),
        check_vma=False,
    )
```

time: 114 us -> 123 us (1.079)
  starting transfers between devices: 34.2 us -> 47.1 us
  Pallas kernels: 14 us -> 19.4 us
  local copies, waits for them, and re-layouts: 5.1 us -> 1.27 us
  waiting for transfers between devices: 56.9 us -> 53.5 us
    ppermute x25 -> x18, waiting for transfers between devices: 36.1 us -> 21.2 us  [cross(): return lax.ppermute(x, axis, [(i, i ^ k) for i in range(n)])]
    ppermute x0 -> x19, waiting for transfers between devices: none -> 10.4 us  [swap(): return lax.ppermute(x, 'branch', [(0, 1), (1, 0)])]
    pallas_call x9 -> x15, Pallas kernels: 14 us -> 19.4 us  [the longest x2 4.16 us: block(): pl.pallas_call(functools.partial(prep_kernel, n_head), out_shape=[SHAPE(w...]
    ppermute x25 -> x18, starting transfers between devices: 20.1 us -> 25 us  [cross(): return lax.ppermute(x, axis, [(i, i ^ k) for i in range(n)])]
    ppermute x9, starting transfers between devices: 14.2 us -> 18.7 us  [turn(): return lax.ppermute(x, axis, [(i, (i + k) % n) for i in range(n)])]
    unnamed x18 -> x4, local copies, waits for them, and re-layouts: 5.1 us -> 1.27 us
    ppermute x0 -> x19, starting transfers between devices: none -> 3.43 us  [swap(): return lax.ppermute(x, 'branch', [(0, 1), (1, 0)])]
  transfers between devices with their start and end apart: 34 -> 46, of which waited for: 16 -> 21; matrix products, arithmetic and copies ran while one was open for 0% -> 0% of each run, Pallas kernels for 9% -> 15%
where the time goes in v3:
time: 123 us; the launch traced here: 122 us
  waiting for transfers between devices  53.5 us (43%)
  starting transfers between devices  47.1 us (38%)
  Pallas kernels  19.4 us (16%)
  local copies, waits for them, and re-layouts  1.27 us (1%)
    ppermute x18, starting transfers between devices, cross(): return lax.ppermute(x, axis, [(i, i ^ k) for i in range(n)])  25 us
    ppermute x9, waiting for transfers between devices, turn(): return lax.ppermute(x, axis, [(i, (i + k) % n) for i in range(n)])  21.8 us
    ppermute x18, waiting for transfers between devices, cross(): return lax.ppermute(x, axis, [(i, i ^ k) for i in range(n)])  21.2 us
    ppermute x9, starting transfers between devices, turn(): return lax.ppermute(x, axis, [(i, (i + k) % n) for i in range(n)])  18.7 us
    ppermute x19, waiting for transfers between devices, swap(): return lax.ppermute(x, 'branch', [(0, 1), (1, 0)])  10.4 us
    pallas_call x2, Pallas kernels, block(): pl.pallas_call(functools.partial(prep_kernel, n_head), out_shape=[SHAPE(w...  4.16 us
    pallas_call x2, Pallas kernels, block(): pl.pallas_call(functools.partial(kv_kernel, blk, n_head), out_shape=(SHAP...  3.73 us
    ppermute x19, starting transfers between devices, swap(): return lax.ppermute(x, 'branch', [(0, 1), (1, 0)])  3.43 us
  transfers between devices with their start and end apart: 46, of which 21 were waited for; matrix products, arithmetic and copies ran while one was open for 0% of the time, Pallas kernels for 15%

profile of v3, /device:TPU:0, one launch (start us, length us, event | category | flops | bytes accessed | tf_op | source)
XLA Modules:
  0.0 122.1 jit_solution(6595938057665991446)
XLA Ops:
  1.9 2.5 %collective-permute-start = (bf16[128,768]{1,0:T(8,128)(2,1)S(1)}, bf16[128,768]{1,0:T(8,128)(2,1)S(1)}, u32[]{:S(2)}, u32[]{:S(2)}) collective-permute-start(bf16[128,768]{1,0:T(8,128)(2,1)S(1)} %take_half.1.refs_0_.refs_12_), channel_id=1, source_target_pairs={{0,1},{1,0},{2,3},{3,2},{4,5},{5,4},{6,7},{7,6},{8,9},{9,8},{10,11... | collective-permute-start | bytes 589832 | tf_op jit(solution)/shard_map/ppermute | solution.py:28
  4.5 1.5 %collective-permute-start.1 = (bf16[128,768]{1,0:T(8,128)(2,1)S(1)}, bf16[128,768]{1,0:T(8,128)(2,1)S(1)}, u32[]{:S(2)}, u32[]{:S(2)}) collective-permute-start(bf16[128,768]{1,0:T(8,128)(2,1)S(1)} %take_half.1.refs_0_.refs_12_), channel_id=1, source_target_pairs={{0,2},{1,3},{2,0},{3,1},{4,6},{5,7},{6,4},{7,5},{8,10},{9,11},{10,... | collective-permute-start | bytes 589832 | tf_op jit(solution)/shard_map/ppermute | solution.py:28
  6.0 7.3 %collective-permute-done.3.refs_2_ = bf16[384,1536]{1,0:T(8,128)(2,1)S(1)} collective-permute-done((bf16[384,1536]{1,0:T(8,128)(2,1)}, bf16[384,1536]{1,0:T(8,128)(2,1)S(1)}, u32[]{:S(2)}, u32[]{:S(2)}) %collective-permute-start.3) | collective-permute-done | bytes 1179680 | tf_op jit(solution)/shard_map/ppermute | solution.py:32
  13.3 2.9 %collective-permute-start.9 = (s32[1]{0:T(128)}, s32[1]{0:T(128)}, u32[]{:S(2)}, u32[]{:S(2)}) collective-permute-start(s32[1]{0:T(128)} %param.9), channel_id=1, source_target_pairs={{0,4},{4,8},{8,12},{12,0},{1,5},{5,9},{9,13},{13,1},{2,6},{6,10},{... | collective-permute-start | bytes 20 | tf_op jit(solution)/shard_map/ppermute | solution.py:24
  17.5 2.1 %shard_map.82 = (bf16[3,1536,384]{2,1,0:T(8,128)(2,1)S(1)}, f32[3,2,3072]{2,1,0:T(2,128)S(1)}, f32[2,2,128]{2,1,0:T(2,128)S(1)}, bf16[384,384]{1,0:T(8,128)(2,1)...) custom-call(bf16[3,1536,384]{2,1,0:T(8,128)(2,1)} %bitcast.5, ...), custom_call_target="tpu_custom_call" | custom-call | tf_op jit(solution)/shard_map/pallas_call | solution.py:297
  20.0 2.3 %collective-permute-start.10 = (s32[1]{0:T(128)}, s32[1]{0:T(128)}, u32[]{:S(2)}, u32[]{:S(2)}) collective-permute-start(s32[1]{0:T(128)} %param.9), channel_id=1, source_target_pairs={{0,8},{4,12},{8,0},{12,4},{1,9},{5,13},{9,1},{13,5},{2,10},{6,14},... | collective-permute-start | bytes 20 | tf_op jit(solution)/shard_map/ppermute | solution.py:24
  22.3 2.3 %collective-permute-done.10.refs_2_ = s32[1]{0:T(128)} collective-permute-done((s32[1]{0:T(128)}, s32[1]{0:T(128)}, u32[]{:S(2)}, u32[]{:S(2)}) %collective-permute-start.10) | collective-permute-done | bytes 36 | tf_op jit(solution)/shard_map/ppermute | solution.py:24
  24.6 2.0 %collective-permute-start.11 = (s32[1]{0:T(128)}, s32[1]{0:T(128)}, u32[]{:S(2)}, u32[]{:S(2)}) collective-permute-start(s32[1]{0:T(128)} %param.9), channel_id=1, source_target_pairs={{0,12},{4,0},{8,4},{12,8},{1,13},{5,1},{9,5},{13,9},{2,14},{6,2},{... | collective-permute-start | bytes 20 | tf_op jit(solution)/shard_map/ppermute | solution.py:24
  26.6 1.6 %collective-permute-done.11.refs_3_ = s32[1]{0:T(128)} collective-permute-done((s32[1]{0:T(128)}, s32[1]{0:T(128)}, u32[]{:S(2)}, u32[]{:S(2)}) %collective-permute-start.11) | collective-permute-done | bytes 36 | tf_op jit(solution)/shard_map/ppermute | solution.py:24
  28.3 2.7 %collective-permute-start.2 = (bf16[128,768]{1,0:T(8,128)(2,1)S(1)}, bf16[128,768]{1,0:T(8,128)(2,1)S(1)}, u32[]{:S(2)}, u32[]{:S(2)}) collective-permute-start(bf16[128,768]{1,0:T(8,128)(2,1)S(1)} %take_half.1.refs_0_.refs_12_), channel_id=1, source_target_pairs={{0,3},{1,2},{2,1},{3,0},{4,7},{5,6},{6,5},{7,4},{8,11},{9,10},{10,... | collective-permute-start | bytes 589832 | tf_op jit(solution)/shard_map/ppermute | solution.py:28
  31.8 5.3 %collective-permute-done.2.refs_3_ = bf16[128,768]{1,0:T(8,128)(2,1)S(1)} collective-permute-done((bf16[128,768]{1,0:T(8,128)(2,1)S(1)}, bf16[128,768]{1,0:T(8,128)(2,1)S(1)}, u32[]{:S(2)}, u32[]{:S(2)}) %collective-permute-start.2) | collective-permute-done | bytes 196640 | tf_op jit(solution)/shard_map/ppermute | solution.py:28
  37.0 2.7 %collective-permute-start.20 = (bf16[384,384]{1,0:T(8,128)(2,1)S(1)}, bf16[384,384]{1,0:T(8,128)(2,1)S(1)}, u32[]{:S(2)}, u32[]{:S(2)}) collective-permute-start(bf16[384,384]{1,0:T(8,128)(2,1)S(1)} %get-tuple-element.39), channel_id=1, source_target_pairs={{0,3},{1,2},{2,1},{3,0},{4,7},{5,6},{6,5},{7,4},{8,11},{9,10},{10,... | collective-permute-start | bytes 884744 | tf_op jit(solution)/shard_map/ppermute | solution.py:28
  39.7 1.9 %shard_map.83 = (bf16[128,768]{1,0:T(8,128)(2,1)S(1)}, bf16[4,128,768]{2,1,0:T(8,128)(2,1)S(1)}) custom-call(bf16[128,768]{1,0:T(8,128)(2,1)S(1)} %take_half.1.refs_0_.refs_12_, bf16[128,768]{1,0:T(8,128)(2,1)S(1)} %collective-permute-done.refs_1_, bf16[128,768]{1,0:T(8,128)(2,1)S(1)} %collective-permute-done.1.refs_2_, ...), custom_call_target="tpu_custom_call" | custom-call | tf_op jit(solution)/shard_map/pallas_call | solution.py:307
  41.6 1.7 %collective-permute-done.18.refs_5_ = bf16[384,384]{1,0:T(8,128)(2,1)S(1)} collective-permute-done((bf16[384,384]{1,0:T(8,128)(2,1)S(1)}, bf16[384,384]{1,0:T(8,128)(2,1)S(1)}, u32[]{:S(2)}, u32[]{:S(2)}) %collective-permute-start.18) | collective-permute-done | bytes 294944 | tf_op jit(solution)/shard_map/ppermute | solution.py:28
  43.3 2.3 %collective-permute-start.5 = (bf16[128,768]{1,0:T(8,128)(2,1)S(1)}, bf16[128,768]{1,0:T(8,128)(2,1)S(1)}, u32[]{:S(2)}, u32[]{:S(2)}) collective-permute-start(bf16[128,768]{1,0:T(8,128)(2,1)S(1)} %get-tuple-element.33.refs_1_), channel_id=1, source_target_pairs={{0,8},{4,12},{8,0},{12,4},{1,9},{5,13},{9,1},{13,5},{2,10},{6,14},... | collective-permute-start | bytes 589832 | tf_op jit(solution)/shard_map/ppermute | solution.py:24
  45.6 1.6 %collective-permute-start.6 = (bf16[128,768]{1,0:T(8,128)(2,1)S(1)}, bf16[128,768]{1,0:T(8,128)(2,1)S(1)}, u32[]{:S(2)}, u32[]{:S(2)}) collective-permute-start(bf16[128,768]{1,0:T(8,128)(2,1)S(1)} %get-tuple-element.33.refs_1_), channel_id=1, source_target_pairs={{0,12},{4,0},{8,4},{12,8},{1,13},{5,1},{9,5},{13,9},{2,14},{6,2},{... | collective-permute-start | bytes 589832 | tf_op jit(solution)/shard_map/ppermute | solution.py:24
  47.8 11.5 %collective-permute-done.5.refs_1_ = bf16[128,768]{1,0:T(8,128)(2,1)S(1)} collective-permute-done((bf16[128,768]{1,0:T(8,128)(2,1)S(1)}, bf16[128,768]{1,0:T(8,128)(2,1)S(1)}, u32[]{:S(2)}, u32[]{:S(2)}) %collective-permute-start.5) | collective-permute-done | bytes 196640 | tf_op jit(solution)/shard_map/ppermute | solution.py:24
  62.9 1.8 %drop.1.refs_5_ = f32[8,128]{1,0:T(8,128)S(1)} custom-call(s32[1]{0:T(128)S(6)} %copy.9.refs_0_, s32[1]{0:T(128)} %collective-permute-done.9.refs_1_, s32[1]{0:T(128)} %collective-permute-done.10.refs_2_, s32[1]{0:T(128)} %collective-permute-done.11.refs_3_), custom_call_target="tpu_custom_call" | custom-call | tf_op jit(solution)/shard_map/drop/pallas_call | solution.py:289
  68.8 2.9 %collective-permute-start.17 = (bf16[128,384]{1,0:T(8,128)(2,1)S(1)}, bf16[128,384]{1,0:T(8,128)(2,1)S(1)}, u32[]{:S(2)}, u32[]{:S(2)}) collective-permute-start(bf16[128,384]{1,0:T(8,128)(2,1)S(1)} %shard_map.86.refs_0_), channel_id=1, source_target_pairs={{0,3},{1,2},{2,1},{3,0},{4,7},{5,6},{6,5},{7,4},{8,11},{9,10},{10,... | collective-permute-start | bytes 294920 | tf_op jit(solution)/shard_map/ppermute | solution.py:28
  71.7 2.2 %collective-permute-done.15.refs_1_ = bf16[128,384]{1,0:T(8,128)(2,1)S(1)} collective-permute-done((bf16[128,384]{1,0:T(8,128)(2,1)S(1)}, bf16[128,384]{1,0:T(8,128)(2,1)S(1)}, u32[]{:S(2)}, u32[]{:S(2)}) %collective-permute-start.15) | collective-permute-done | bytes 98336 | tf_op jit(solution)/shard_map/ppermute | solution.py:28
  73.8 1.6 %collective-permute-done.16.refs_2_ = bf16[128,384]{1,0:T(8,128)(2,1)S(1)} collective-permute-done((bf16[128,384]{1,0:T(8,128)(2,1)S(1)}, bf16[128,384]{1,0:T(8,128)(2,1)S(1)}, u32[]{:S(2)}, u32[]{:S(2)}) %collective-permute-start.16) | collective-permute-done | bytes 98336 | tf_op jit(solution)/shard_map/ppermute | solution.py:28
  76.1 1.7 %collective-permute-start.24 = (bf16[128,768]{1,0:T(8,128)(2,1)S(1)}, bf16[128,768]{1,0:T(8,128)(2,1)S(1)}, u32[]{:S(2)}, u32[]{:S(2)}) collective-permute-start(bf16[128,768]{1,0:T(8,128)(2,1)S(1)} %shard_map.87.refs_0_.refs_12_.forked_ref), channel_id=1, source_target_pairs={{0,1},{1,0},{2,3},{3,2},{4,5},{5,4},{6,7},{7,6},{8,9},{9,8},{10,11... | collective-permute-start | bytes 589832 | tf_op jit(solution)/shard_map/ppermute | solution.py:28
  79.7 2.0 %shard_map.88 = (bf16[3,1536,384]{2,1,0:T(8,128)(2,1)S(1)}, f32[3,2,3072]{2,1,0:T(2,128)S(1)}, f32[2,2,128]{2,1,0:T(2,128)S(1)}, bf16[384,384]{1,0:T(8,128)(2,1)...) custom-call(bf16[3,1536,384]{2,1,0:T(8,128)(2,1)} %bitcast.7, ...), custom_call_target="tpu_custom_call" | custom-call | tf_op jit(solution)/shard_map/pallas_call | solution.py:297
  81.7 1.7 %collective-permute-start.39 = (bf16[384,384]{1,0:T(8,128)(2,1)S(1)}, bf16[384,384]{1,0:T(8,128)(2,1)S(1)}, u32[]{:S(2)}, u32[]{:S(2)}) collective-permute-start(bf16[384,384]{1,0:T(8,128)(2,1)S(1)} %get-tuple-element.49), channel_id=1, source_target_pairs={{0,1},{1,0},{2,3},{3,2},{4,5},{5,4},{6,7},{7,6},{8,9},{9,8},{10,11... | collective-permute-start | bytes 884744 | tf_op jit(solution)/shard_map/ppermute | solution.py:28
  84.1 4.5 %collective-permute-done.25.refs_2_ = bf16[128,768]{1,0:T(8,128)(2,1)S(1)} collective-permute-done((bf16[128,768]{1,0:T(8,128)(2,1)S(1)}, bf16[128,768]{1,0:T(8,128)(2,1)S(1)}, u32[]{:S(2)}, u32[]{:S(2)}) %collective-permute-start.25) | collective-permute-done | bytes 196640 | tf_op jit(solution)/shard_map/ppermute | solution.py:28
  89.0 1.9 %shard_map.89 = (bf16[128,768]{1,0:T(8,128)(2,1)S(1)}, bf16[4,128,768]{2,1,0:T(8,128)(2,1)S(1)}) custom-call(bf16[128,768]{1,0:T(8,128)(2,1)S(1)} %shard_map.87.refs_0_.refs_12_.forked_ref, bf16[128,768]{1,0:T(8,128)(2,1)S(1)} %collective-permute-done.24.refs_1_, bf16[128,768]{1,0:T(8,128)(2,1)S(1)} %collective-permute-done.25.refs_2_, ...), custom_call_target="tpu_custom_call" | custom-call | tf_op jit(solution)/shard_map/pallas_call | solution.py:307
  90.9 3.0 %collective-permute-start.33 = (bf16[128,768]{1,0:T(8,128)(2,1)S(1)}, bf16[128,768]{1,0:T(8,128)(2,1)S(1)}, u32[]{:S(2)}, u32[]{:S(2)}) collective-permute-start(bf16[128,768]{1,0:T(8,128)(2,1)S(1)} %get-tuple-element.45.refs_1_), channel_id=1, source_target_pairs={{0,4},{4,8},{8,12},{12,0},{1,5},{5,9},{9,13},{13,1},{2,6},{6,10},{... | collective-permute-start | bytes 589832 | tf_op jit(solution)/shard_map/ppermute | solution.py:24
  93.9 1.7 %collective-permute-start.41 = (bf16[384,384]{1,0:T(8,128)(2,1)S(1)}, bf16[384,384]{1,0:T(8,128)(2,1)S(1)}, u32[]{:S(2)}, u32[]{:S(2)}) collective-permute-start(bf16[384,384]{1,0:T(8,128)(2,1)S(1)} %get-tuple-element.51), channel_id=1, source_target_pairs={{0,3},{1,2},{2,1},{3,0},{4,7},{5,6},{6,5},{7,4},{8,11},{9,10},{10,... | collective-permute-start | bytes 884744 | tf_op jit(solution)/shard_map/ppermute | solution.py:28
  96.8 2.8 %collective-permute-start.30 = (bf16[128,768]{1,0:T(8,128)(2,1)S(1)}, bf16[128,768]{1,0:T(8,128)(2,1)S(1)}, u32[]{:S(2)}, u32[]{:S(2)}) collective-permute-start(bf16[128,768]{1,0:T(8,128)(2,1)S(1)} %get-tuple-element.45.refs_1_), channel_id=1, source_target_pairs={{0,12},{4,0},{8,4},{12,8},{1,13},{5,1},{9,5},{13,9},{2,14},{6,2},{... | collective-permute-start | bytes 589832 | tf_op jit(solution)/shard_map/ppermute | solution.py:24
  101.5 5.1 %collective-permute-done.29.refs_1_ = bf16[128,768]{1,0:T(8,128)(2,1)S(1)} collective-permute-done((bf16[128,768]{1,0:T(8,128)(2,1)S(1)}, bf16[128,768]{1,0:T(8,128)(2,1)S(1)}, u32[]{:S(2)}, u32[]{:S(2)}) %collective-permute-start.29) | collective-permute-done | bytes 196640 | tf_op jit(solution)/shard_map/ppermute | solution.py:24
  111.7 1.9 %collective-permute-start.37 = (bf16[128,384]{1,0:T(8,128)(2,1)S(1)}, bf16[128,384]{1,0:T(8,128)(2,1)S(1)}, u32[]{:S(2)}, u32[]{:S(2)}) collective-permute-start(bf16[128,384]{1,0:T(8,128)(2,1)S(1)} %shard_map.92.refs_0_), channel_id=1, source_target_pairs={{0,2},{1,3},{2,0},{3,1},{4,6},{5,7},{6,4},{7,5},{8,10},{9,11},{10,... | collective-permute-start | bytes 294920 | tf_op jit(solution)/shard_map/ppermute | solution.py:28
  114.5 1.7 %collective-permute-done.36.refs_1_ = bf16[128,384]{1,0:T(8,128)(2,1)S(1)} collective-permute-done((bf16[128,384]{1,0:T(8,128)(2,1)S(1)}, bf16[128,384]{1,0:T(8,128)(2,1)S(1)}, u32[]{:S(2)}, u32[]{:S(2)}) %collective-permute-start.36) | collective-permute-done | bytes 98336 | tf_op jit(solution)/shard_map/ppermute | solution.py:28
  (80 shorter events, 30.4 us)
Async XLA Ops:
  0.0 39.7 %collective-permute-start.4 = (bf16[3,1536,384]{2,1,0:T(8,128)(2,1)}, bf16[3,1536,384]{2,1,0:T(8,128)(2,1)S(1)}, u32[]{:S(2)}, u32[]{:S(2)}) collective-permute-start(bf16[3,1536,384]{2,1,0:T(8,128)(2,1)} %bitcast.4), channel_id=1, source_target_pairs={{0,16},{16,0},{1,17},{17,1},{2,18},{18,2},{3,19},{19,3},{4,20},{20... | collective-permute-start | bytes 10616840 | tf_op jit(solution)/shard_map/ppermute | solution.py:32
  0.5 83.0 %collective-permute-start.28 = (bf16[3,1536,384]{2,1,0:T(8,128)(2,1)}, bf16[3,1536,384]{2,1,0:T(8,128)(2,1)S(1)}, u32[]{:S(2)}, u32[]{:S(2)}) collective-permute-start(bf16[3,1536,384]{2,1,0:T(8,128)(2,1)} %bitcast.6), channel_id=1, source_target_pairs={{0,16},{16,0},{1,17},{17,1},{2,18},{18,2},{3,19},{19,3},{4,20},{20... | collective-permute-start | bytes 10616840 | tf_op jit(solution)/shard_map/ppermute | solution.py:32
  0.5 12.8 %collective-permute-start.3 = (bf16[384,1536]{1,0:T(8,128)(2,1)}, bf16[384,1536]{1,0:T(8,128)(2,1)S(1)}, u32[]{:S(2)}, u32[]{:S(2)}) collective-permute-start(bf16[384,1536]{1,0:T(8,128)(2,1)} %refs_1_.2), channel_id=1, source_target_pairs={{0,16},{16,0},{1,17},{17,1},{2,18},{18,2},{3,19},{19,3},{4,20},{20... | collective-permute-start | bytes 3538952 | tf_op jit(solution)/shard_map/ppermute | solution.py:32
  1.9 29.0 %collective-permute-start = (bf16[128,768]{1,0:T(8,128)(2,1)S(1)}, bf16[128,768]{1,0:T(8,128)(2,1)S(1)}, u32[]{:S(2)}, u32[]{:S(2)}) collective-permute-start(bf16[128,768]{1,0:T(8,128)(2,1)S(1)} %take_half.1.refs_0_.refs_12_), channel_id=1, source_target_pairs={{0,1},{1,0},{2,3},{3,2},{4,5},{5,4},{6,7},{7,6},{8,9},{9,8},{10,11... | collective-permute-start | bytes 589832 | tf_op jit(solution)/shard_map/ppermute | solution.py:28
  4.5 27.0 %collective-permute-start.1 = (bf16[128,768]{1,0:T(8,128)(2,1)S(1)}, bf16[128,768]{1,0:T(8,128)(2,1)S(1)}, u32[]{:S(2)}, u32[]{:S(2)}) collective-permute-start(bf16[128,768]{1,0:T(8,128)(2,1)S(1)} %take_half.1.refs_0_.refs_12_), channel_id=1, source_target_pairs={{0,2},{1,3},{2,0},{3,1},{4,6},{5,7},{6,4},{7,5},{8,10},{9,11},{10,... | collective-permute-start | bytes 589832 | tf_op jit(solution)/shard_map/ppermute | solution.py:28
  13.3 6.7 %collective-permute-start.9 = (s32[1]{0:T(128)}, s32[1]{0:T(128)}, u32[]{:S(2)}, u32[]{:S(2)}) collective-permute-start(s32[1]{0:T(128)} %param.9), channel_id=1, source_target_pairs={{0,4},{4,8},{8,12},{12,0},{1,5},{5,9},{9,13},{13,1},{2,6},{6,10},{... | collective-permute-start | bytes 20 | tf_op jit(solution)/shard_map/ppermute | solution.py:24
  28.3 8.8 %collective-permute-start.2 = (bf16[128,768]{1,0:T(8,128)(2,1)S(1)}, bf16[128,768]{1,0:T(8,128)(2,1)S(1)}, u32[]{:S(2)}, u32[]{:S(2)}) collective-permute-start(bf16[128,768]{1,0:T(8,128)(2,1)S(1)} %take_half.1.refs_0_.refs_12_), channel_id=1, source_target_pairs={{0,3},{1,2},{2,1},{3,0},{4,7},{5,6},{6,5},{7,4},{8,11},{9,10},{10,... | collective-permute-start | bytes 589832 | tf_op jit(solution)/shard_map/ppermute | solution.py:28
  30.9 12.3 %collective-permute-start.18 = (bf16[384,384]{1,0:T(8,128)(2,1)S(1)}, bf16[384,384]{1,0:T(8,128)(2,1)S(1)}, u32[]{:S(2)}, u32[]{:S(2)}) collective-permute-start(bf16[384,384]{1,0:T(8,128)(2,1)S(1)} %get-tuple-element.37), channel_id=1, source_target_pairs={{0,1},{1,0},{2,3},{3,2},{4,5},{5,4},{6,7},{7,6},{8,9},{9,8},{10,11... | collective-permute-start | bytes 884744 | tf_op jit(solution)/shard_map/ppermute | solution.py:28
  31.5 14.1 %collective-permute-start.19 = (bf16[384,384]{1,0:T(8,128)(2,1)S(1)}, bf16[384,384]{1,0:T(8,128)(2,1)S(1)}, u32[]{:S(2)}, u32[]{:S(2)}) collective-permute-start(bf16[384,384]{1,0:T(8,128)(2,1)S(1)} %get-tuple-element.38), channel_id=1, source_target_pairs={{0,2},{1,3},{2,0},{3,1},{4,6},{5,7},{6,4},{7,5},{8,10},{9,11},{10,... | collective-permute-start | bytes 884744 | tf_op jit(solution)/shard_map/ppermute | solution.py:28
  37.0 10.1 %collective-permute-start.20 = (bf16[384,384]{1,0:T(8,128)(2,1)S(1)}, bf16[384,384]{1,0:T(8,128)(2,1)S(1)}, u32[]{:S(2)}, u32[]{:S(2)}) collective-permute-start(bf16[384,384]{1,0:T(8,128)(2,1)S(1)} %get-tuple-element.39), channel_id=1, source_target_pairs={{0,3},{1,2},{2,1},{3,0},{4,7},{5,6},{6,5},{7,4},{8,11},{9,10},{10,... | collective-permute-start | bytes 884744 | tf_op jit(solution)/shard_map/ppermute | solution.py:28
  39.7 40.0 %collective-permute-start.27 = (bf16[384,1536]{1,0:T(8,128)(2,1)S(1)}, bf16[384,1536]{1,0:T(8,128)(2,1)S(1)}, u32[]{:S(2)}, u32[]{:S(2)}) collective-permute-start(bf16[384,1536]{1,0:T(8,128)(2,1)S(1)} %copy-done.1), channel_id=1, source_target_pairs={{0,16},{16,0},{1,17},{17,1},{2,18},{18,2},{3,19},{19,3},{4,20},{20... | collective-permute-start | bytes 3538952 | tf_op jit(solution)/shard_map/ppermute | solution.py:32
  43.3 16.0 %collective-permute-start.5 = (bf16[128,768]{1,0:T(8,128)(2,1)S(1)}, bf16[128,768]{1,0:T(8,128)(2,1)S(1)}, u32[]{:S(2)}, u32[]{:S(2)}) collective-permute-start(bf16[128,768]{1,0:T(8,128)(2,1)S(1)} %get-tuple-element.33.refs_1_), channel_id=1, source_target_pairs={{0,8},{4,12},{8,0},{12,4},{1,9},{5,13},{9,1},{13,5},{2,10},{6,14},... | collective-permute-start | bytes 589832 | tf_op jit(solution)/shard_map/ppermute | solution.py:24
  45.6 13.7 %collective-permute-start.6 = (bf16[128,768]{1,0:T(8,128)(2,1)S(1)}, bf16[128,768]{1,0:T(8,128)(2,1)S(1)}, u32[]{:S(2)}, u32[]{:S(2)}) collective-permute-start(bf16[128,768]{1,0:T(8,128)(2,1)S(1)} %get-tuple-element.33.refs_1_), channel_id=1, source_target_pairs={{0,12},{4,0},{8,4},{12,8},{1,13},{5,1},{9,5},{13,9},{2,14},{6,2},{... | collective-permute-start | bytes 589832 | tf_op jit(solution)/shard_map/ppermute | solution.py:24
  47.1 12.6 %collective-permute-start.12 = (bf16[128,768]{1,0:T(8,128)(2,1)S(1)}, bf16[128,768]{1,0:T(8,128)(2,1)S(1)}, u32[]{:S(2)}, u32[]{:S(2)}) collective-permute-start(bf16[128,768]{1,0:T(8,128)(2,1)S(1)} %get-tuple-element.33.refs_1_), channel_id=1, source_target_pairs={{0,4},{4,8},{8,12},{12,0},{1,5},{5,9},{9,13},{13,1},{2,6},{6,10},{... | collective-permute-start | bytes 589832 | tf_op jit(solution)/shard_map/ppermute | solution.py:24
  61.0 7.1 %collective-permute-start.21 = (bf16[384,384]{1,0:T(8,128)(2,1)S(1)}, bf16[384,384]{1,0:T(8,128)(2,1)S(1)}, u32[]{:S(2)}, u32[]{:S(2)}) collective-permute-start(bf16[384,384]{1,0:T(8,128)(2,1)S(1)} %collective-permute-done.18.refs_5_), channel_id=1, source_target_pairs={{0,16},{16,0},{1,17},{17,1},{2,18},{18,2},{3,19},{19,3},{4,20},{20... | collective-permute-start | bytes 884744 | tf_op jit(solution)/shard_map/ppermute | solution.py:32
  61.3 6.9 %collective-permute-start.22 = (bf16[384,384]{1,0:T(8,128)(2,1)S(1)}, bf16[384,384]{1,0:T(8,128)(2,1)S(1)}, u32[]{:S(2)}, u32[]{:S(2)}) collective-permute-start(bf16[384,384]{1,0:T(8,128)(2,1)S(1)} %collective-permute-done.19.refs_6_), channel_id=1, source_target_pairs={{0,16},{16,0},{1,17},{17,1},{2,18},{18,2},{3,19},{19,3},{4,20},{20... | collective-permute-start | bytes 884744 | tf_op jit(solution)/shard_map/ppermute | solution.py:32
  68.2 7.2 %collective-permute-start.16 = (bf16[128,384]{1,0:T(8,128)(2,1)S(1)}, bf16[128,384]{1,0:T(8,128)(2,1)S(1)}, u32[]{:S(2)}, u32[]{:S(2)}) collective-permute-start(bf16[128,384]{1,0:T(8,128)(2,1)S(1)} %shard_map.86.refs_0_), channel_id=1, source_target_pairs={{0,2},{1,3},{2,0},{3,1},{4,6},{5,7},{6,4},{7,5},{8,10},{9,11},{10,... | collective-permute-start | bytes 294920 | tf_op jit(solution)/shard_map/ppermute | solution.py:28
  68.8 6.7 %collective-permute-start.17 = (bf16[128,384]{1,0:T(8,128)(2,1)S(1)}, bf16[128,384]{1,0:T(8,128)(2,1)S(1)}, u32[]{:S(2)}, u32[]{:S(2)}) collective-permute-start(bf16[128,384]{1,0:T(8,128)(2,1)S(1)} %shard_map.86.refs_0_), channel_id=1, source_target_pairs={{0,3},{1,2},{2,1},{3,0},{4,7},{5,6},{6,5},{7,4},{8,11},{9,10},{10,... | collective-permute-start | bytes 294920 | tf_op jit(solution)/shard_map/ppermute | solution.py:28
  76.1 8.0 %collective-permute-start.24 = (bf16[128,768]{1,0:T(8,128)(2,1)S(1)}, bf16[128,768]{1,0:T(8,128)(2,1)S(1)}, u32[]{:S(2)}, u32[]{:S(2)}) collective-permute-start(bf16[128,768]{1,0:T(8,128)(2,1)S(1)} %shard_map.87.refs_0_.refs_12_.forked_ref), channel_id=1, source_target_pairs={{0,1},{1,0},{2,3},{3,2},{4,5},{5,4},{6,7},{7,6},{8,9},{9,8},{10,11... | collective-permute-start | bytes 589832 | tf_op jit(solution)/shard_map/ppermute | solution.py:28
  77.8 10.8 %collective-permute-start.25 = (bf16[128,768]{1,0:T(8,128)(2,1)S(1)}, bf16[128,768]{1,0:T(8,128)(2,1)S(1)}, u32[]{:S(2)}, u32[]{:S(2)}) collective-permute-start(bf16[128,768]{1,0:T(8,128)(2,1)S(1)} %shard_map.87.refs_0_.refs_12_.forked_ref), channel_id=1, source_target_pairs={{0,2},{1,3},{2,0},{3,1},{4,6},{5,7},{6,4},{7,5},{8,10},{9,11},{10,... | collective-permute-start | bytes 589832 | tf_op jit(solution)/shard_map/ppermute | solution.py:28
  78.5 10.5 %collective-permute-start.26 = (bf16[128,768]{1,0:T(8,128)(2,1)S(1)}, bf16[128,768]{1,0:T(8,128)(2,1)S(1)}, u32[]{:S(2)}, u32[]{:S(2)}) collective-permute-start(bf16[128,768]{1,0:T(8,128)(2,1)S(1)} %shard_map.87.refs_0_.refs_12_.forked_ref), channel_id=1, source_target_pairs={{0,3},{1,2},{2,1},{3,0},{4,7},{5,6},{6,5},{7,4},{8,11},{9,10},{10,... | collective-permute-start | bytes 589832 | tf_op jit(solution)/shard_map/ppermute | solution.py:28
  81.7 15.1 %collective-permute-start.39 = (bf16[384,384]{1,0:T(8,128)(2,1)S(1)}, bf16[384,384]{1,0:T(8,128)(2,1)S(1)}, u32[]{:S(2)}, u32[]{:S(2)}) collective-permute-start(bf16[384,384]{1,0:T(8,128)(2,1)S(1)} %get-tuple-element.49), channel_id=1, source_target_pairs={{0,1},{1,0},{2,3},{3,2},{4,5},{5,4},{6,7},{7,6},{8,9},{9,8},{10,11... | collective-permute-start | bytes 884744 | tf_op jit(solution)/shard_map/ppermute | solution.py:28
  83.4 16.2 %collective-permute-start.40 = (bf16[384,384]{1,0:T(8,128)(2,1)S(1)}, bf16[384,384]{1,0:T(8,128)(2,1)S(1)}, u32[]{:S(2)}, u32[]{:S(2)}) collective-permute-start(bf16[384,384]{1,0:T(8,128)(2,1)S(1)} %get-tuple-element.50), channel_id=1, source_target_pairs={{0,2},{1,3},{2,0},{3,1},{4,6},{5,7},{6,4},{7,5},{8,10},{9,11},{10,... | collective-permute-start | bytes 884744 | tf_op jit(solution)/shard_map/ppermute | solution.py:28
  90.9 9.6 %collective-permute-start.33 = (bf16[128,768]{1,0:T(8,128)(2,1)S(1)}, bf16[128,768]{1,0:T(8,128)(2,1)S(1)}, u32[]{:S(2)}, u32[]{:S(2)}) collective-permute-start(bf16[128,768]{1,0:T(8,128)(2,1)S(1)} %get-tuple-element.45.refs_1_), channel_id=1, source_target_pairs={{0,4},{4,8},{8,12},{12,0},{1,5},{5,9},{9,13},{13,1},{2,6},{6,10},{... | collective-permute-start | bytes 589832 | tf_op jit(solution)/shard_map/ppermute | solution.py:24
  93.9 7.6 %collective-permute-start.41 = (bf16[384,384]{1,0:T(8,128)(2,1)S(1)}, bf16[384,384]{1,0:T(8,128)(2,1)S(1)}, u32[]{:S(2)}, u32[]{:S(2)}) collective-permute-start(bf16[384,384]{1,0:T(8,128)(2,1)S(1)} %get-tuple-element.51), channel_id=1, source_target_pairs={{0,3},{1,2},{2,1},{3,0},{4,7},{5,6},{6,5},{7,4},{8,11},{9,10},{10,... | collective-permute-start | bytes 884744 | tf_op jit(solution)/shard_map/ppermute | solution.py:28
  95.6 11.0 %collective-permute-start.29 = (bf16[128,768]{1,0:T(8,128)(2,1)S(1)}, bf16[128,768]{1,0:T(8,128)(2,1)S(1)}, u32[]{:S(2)}, u32[]{:S(2)}) collective-permute-start(bf16[128,768]{1,0:T(8,128)(2,1)S(1)} %get-tuple-element.45.refs_1_), channel_id=1, source_target_pairs={{0,8},{4,12},{8,0},{12,4},{1,9},{5,13},{9,1},{13,5},{2,10},{6,14},... | collective-permute-start | bytes 589832 | tf_op jit(solution)/shard_map/ppermute | solution.py:24
  96.8 9.8 %collective-permute-start.30 = (bf16[128,768]{1,0:T(8,128)(2,1)S(1)}, bf16[128,768]{1,0:T(8,128)(2,1)S(1)}, u32[]{:S(2)}, u32[]{:S(2)}) collective-permute-start(bf16[128,768]{1,0:T(8,128)(2,1)S(1)} %get-tuple-element.45.refs_1_), channel_id=1, source_target_pairs={{0,12},{4,0},{8,4},{12,8},{1,13},{5,1},{9,5},{13,9},{2,14},{6,2},{... | collective-permute-start | bytes 589832 | tf_op jit(solution)/shard_map/ppermute | solution.py:24
  99.6 7.5 %collective-permute-start.34 = (bf16[128,768]{1,0:T(8,128)(2,1)S(1)}, bf16[128,768]{1,0:T(8,128)(2,1)S(1)}, u32[]{:S(2)}, u32[]{:S(2)}) collective-permute-start(bf16[128,768]{1,0:T(8,128)(2,1)S(1)} %get-tuple-element.45.refs_1_), channel_id=1, source_target_pairs={{0,16},{16,0},{1,17},{17,1},{2,18},{18,2},{3,19},{19,3},{4,20},{20... | collective-permute-start | bytes 589832 | tf_op jit(solution)/shard_map/ppermute | solution.py:32
  100.5 6.7 %collective-permute-start.35 = (bf16[128,768]{1,0:T(8,128)(2,1)S(1)}, bf16[128,768]{1,0:T(8,128)(2,1)S(1)}, u32[]{:S(2)}, u32[]{:S(2)}) collective-permute-start(bf16[128,768]{1,0:T(8,128)(2,1)S(1)} %collective-permute-done.33.refs_2_), channel_id=1, source_target_pairs={{0,16},{16,0},{1,17},{17,1},{2,18},{18,2},{3,19},{19,3},{4,20},{20... | collective-permute-start | bytes 589832 | tf_op jit(solution)/shard_map/ppermute | solution.py:32
  101.5 12.0 %collective-permute-start.42 = (bf16[384,384]{1,0:T(8,128)(2,1)S(1)}, bf16[384,384]{1,0:T(8,128)(2,1)S(1)}, u32[]{:S(2)}, u32[]{:S(2)}) collective-permute-start(bf16[384,384]{1,0:T(8,128)(2,1)S(1)} %collective-permute-done.39.refs_5_), channel_id=1, source_target_pairs={{0,16},{16,0},{1,17},{17,1},{2,18},{18,2},{3,19},{19,3},{4,20},{20... | collective-permute-start | bytes 884744 | tf_op jit(solution)/shard_map/ppermute | solution.py:32
  107.1 7.4 %collective-permute-start.43 = (bf16[384,384]{1,0:T(8,128)(2,1)S(1)}, bf16[384,384]{1,0:T(8,128)(2,1)S(1)}, u32[]{:S(2)}, u32[]{:S(2)}) collective-permute-start(bf16[384,384]{1,0:T(8,128)(2,1)S(1)} %collective-permute-done.40.refs_6_), channel_id=1, source_target_pairs={{0,16},{16,0},{1,17},{17,1},{2,18},{18,2},{3,19},{19,3},{4,20},{20... | collective-permute-start | bytes 884744 | tf_op jit(solution)/shard_map/ppermute | solution.py:32
  107.2 7.3 %collective-permute-start.44 = (bf16[384,384]{1,0:T(8,128)(2,1)S(1)}, bf16[384,384]{1,0:T(8,128)(2,1)S(1)}, u32[]{:S(2)}, u32[]{:S(2)}) collective-permute-start(bf16[384,384]{1,0:T(8,128)(2,1)S(1)} %collective-permute-done.41.refs_7_), channel_id=1, source_target_pairs={{0,16},{16,0},{1,17},{17,1},{2,18},{18,2},{3,19},{19,3},{4,20},{20... | collective-permute-start | bytes 884744 | tf_op jit(solution)/shard_map/ppermute | solution.py:32
  (16 other events, 74.1 us)

commit v4 on v3

v4 whole, which is shorter than its diff:
```python
import functools
import math

import jax
import jax.numpy as jnp
from jax import lax
from jax.experimental import pallas as pl
from jax.experimental.pallas import tpu as pltpu
from jax.sharding import PartitionSpec as P


HEAD_DIM = 128
EPS = 1e-06
MARK = 1e4
MARK_SUM = 1e5
F32 = jnp.float32
BF16 = jnp.bfloat16
VMEM = pl.BlockSpec(memory_space=pltpu.VMEM)
SMEM = pl.BlockSpec(memory_space=pltpu.SMEM)
FAR = pl.BlockSpec(memory_space=pl.ANY)
MIB = 1 << 20
SHAPE = jax.ShapeDtypeStruct


def turn(x, axis, k, n):
    return lax.ppermute(x, axis, [(i, (i + k) % n) for i in range(n)])


def cross(x, axis, k, n):
    return lax.ppermute(x, axis, [(i, i ^ k) for i in range(n)])


def swap(x):
    return lax.ppermute(x, "branch", [(0, 1), (1, 0)])


def far(x):
    return pltpu.with_memory_space_constraint(x, pltpu.HBM)


def params(mib):
    return pltpu.CompilerParams(vmem_limit_bytes=mib * MIB)


def half_kernel(tok_ref, *refs):
    outs, sem = refs[:-1], refs[-1]
    rows = outs[0].shape[0]
    start = pl.multiple_of(lax.axis_index("branch") * len(outs) * rows, rows)
    copies = [
        pltpu.make_async_copy(tok_ref.at[pl.ds(start + i * rows, rows)], out, sem.at[i])
        for i, out in enumerate(outs)
    ]
    for copy in copies:
        copy.start()
    for copy in copies:
        copy.wait()


def take_half(tokens, n_branch, chunks):
    rows, cols = tokens.shape
    return pl.pallas_call(
        half_kernel,
        out_shape=[SHAPE((rows // n_branch // chunks, cols), tokens.dtype)] * chunks,
        in_specs=[FAR],
        out_specs=[VMEM] * chunks,
        scratch_shapes=[pltpu.SemaphoreType.DMA((chunks,))],
        compiler_params=params(4),
        name="take_half",
    )(far(tokens))


def prep_kernel(marks, *refs):
    far_qkv, far_mod, far_gain = refs[:3]
    rest = refs[3:]
    if marks:
        count_ref, rest = rest[0], rest[1:]
    qkv_ref, mod_ref, gain_ref = rest[:3]
    sems = rest[-1]
    copies = [
        pltpu.make_async_copy(far_qkv.at[pl.ds(1, 2)], qkv_ref, sems.at[0]),
        pltpu.make_async_copy(far_mod, mod_ref, sems.at[1]),
        pltpu.make_async_copy(far_gain, gain_ref, sems.at[2]),
    ]
    if marks:
        mark_ref = rest[3]
    for copy in copies:
        copy.start()
    if marks:
        place = lax.broadcasted_iota(jnp.int32, mark_ref.shape, 0)
        place = place + lax.axis_index("branch") * mark_ref.shape[0]
        mark_ref[...] = jnp.where(place < count_ref[0], 0.0, 1.0).astype(F32)
    for copy in copies:
        copy.wait()


def cut_kernel(n_head, near_ref, across_ref, far_qkv, *refs):
    pieces, query_ref, sem = refs[: n_head + 1], refs[n_head + 1], refs[n_head + 2]
    fetch = pltpu.make_async_copy(far_qkv.at[pl.ds(0, 1)], query_ref, sem)
    fetch.start()
    b = lax.axis_index("branch")
    h = lax.axis_index("head")
    per_core = n_head // 2
    part = pieces[0].shape[1]
    for k in range(n_head + 1):
        j = h ^ (k % n_head)
        half = b if k < n_head else 1 - b
        at = pl.ds(pl.multiple_of(lax.rem(j, per_core) * 2 * part + half * part, part), part)
        mine = lax.div(j, per_core) == b
        piece = pieces[k]

        @pl.when(mine)
        def _():
            piece[...] = near_ref[:, at]

        @pl.when(jnp.logical_not(mine))
        def _():
            piece[...] = across_ref[:, at]

    fetch.wait()


def contract(moded_ref, own_ref, other_ref, which, first, n_head):
    b = lax.axis_index("branch")
    h = lax.axis_index("head")
    quarter = moded_ref.shape[2]
    per_core = n_head // 2
    total = None
    for ref, core, at in ((own_ref, b, which - first), (other_ref, 1 - b, which)):
        for i in range(per_core):
            piece = moded_ref[(core * per_core + i) ^ h]
            term = jnp.dot(
                piece,
                ref[at, i * quarter : (i + 1) * quarter, :],
                preferred_element_type=F32,
            )
            total = term if total is None else total + term
    return total


def norm_heads(part, gain, width):
    outs = []
    for lo in range(0, width, HEAD_DIM):
        one = part[:, lo : lo + HEAD_DIM]
        scale = lax.rsqrt(jnp.mean(one * one, axis=1, keepdims=True) + EPS)
        outs.append(one * scale * gain)
    return outs


def kv_kernel(blk, chunk, n_head, *refs):
    xs = refs[:n_head]
    own_ref, other_ref, mod_ref, gain_ref, mark_ref, packed_ref, moded_ref = refs[n_head:]
    rows = xs[0].shape[0]
    padding = mark_ref[chunk * rows : (chunk + 1) * rows, :] > 0.5
    h = lax.axis_index("head")
    quarter = xs[0].shape[1]
    width = own_ref.shape[2]
    total = sum(jnp.sum(x[...].astype(F32), axis=1, keepdims=True) for x in xs)
    mean = total / (n_head * quarter)
    square = 0.0
    for x in xs:
        centered = x[...].astype(F32) - mean
        square = square + jnp.sum(centered * centered, axis=1, keepdims=True)
    scale = lax.rsqrt(square / (n_head * quarter) + EPS)
    for k, x in enumerate(xs):
        at = pl.ds(pl.multiple_of((h ^ k) * quarter, quarter), quarter)
        shift = mod_ref[0, blk : blk + 1, at]
        gain = mod_ref[1, blk : blk + 1, at] + 1.0
        normed = (x[...].astype(F32) - mean) * scale
        moded_ref[k] = (normed * gain + shift).astype(BF16)
    key = contract(moded_ref, own_ref, other_ref, 1, 1, n_head)
    for i, out in enumerate(norm_heads(key, gain_ref[blk, 1:2, :], width)):
        packed_ref[:, i * HEAD_DIM : (i + 1) * HEAD_DIM] = jnp.where(padding, MARK, out).astype(BF16)
    packed_ref[:, width:] = contract(moded_ref, own_ref, other_ref, 2, 1, n_head).astype(BF16)


def q_kernel(blk, n_head, chunks, *refs):
    moded = refs[:chunks]
    own_ref, other_ref, gain_ref, query_ref = refs[chunks:]
    width = own_ref.shape[2]
    rows = moded[0].shape[1]
    for c, moded_ref in enumerate(moded):
        query = contract(moded_ref, own_ref, other_ref, 0, 0, n_head)
        for i, out in enumerate(norm_heads(query, gain_ref[blk, 0:1, :], width)):
            query_ref[c * rows : (c + 1) * rows, i * HEAD_DIM : (i + 1) * HEAD_DIM] = out.astype(BF16)


def step_kernel(n, opens, closes, *refs):
    query_ref = refs[0]
    blocks = refs[1 : 1 + n]
    rest = refs[1 + n :]
    if not opens:
        mixed_in, stat_in, rest = rest[0], rest[1], rest[2:]
    width = query_ref.shape[1]
    scale = math.log2(math.e) / HEAD_DIM**0.5
    rows = query_ref.shape[0]
    ones = jnp.ones((16, HEAD_DIM), BF16)
    for i, lo in enumerate(range(0, width, HEAD_DIM)):
        at = slice(lo, lo + HEAD_DIM)
        key = jnp.concatenate([ref[:, at] for ref in blocks], axis=0)
        value = jnp.concatenate(
            [ref[:, width + lo : width + lo + HEAD_DIM] for ref in blocks], axis=0
        )
        query = jnp.concatenate([query_ref[:, at], ones], axis=0)
        scores = lax.dot_general(
            query, key, (((1,), (1,)), ((), ())), preferred_element_type=F32
        )
        drop = jnp.where(scores[rows : rows + 1, :] > MARK_SUM, -1e30, 0.0)
        scores = scores[:rows, :] * scale + drop
        peak = jnp.max(scores, axis=1, keepdims=True)
        if not opens:
            before = stat_in[0, :, i : i + 1]
            peak = jnp.maximum(peak, before)
        weight = jnp.exp2(scores - peak)
        total = jnp.sum(weight, axis=1, keepdims=True)
        mixed = jnp.dot(weight.astype(BF16), value, preferred_element_type=F32)
        if not opens:
            keep = jnp.exp2(before - peak)
            mixed = mixed + mixed_in[:, at] * keep
            total = total + stat_in[1, :, i : i + 1] * keep
        if closes:
            rest[0][:, at] = (mixed / total).astype(BF16)
        else:
            rest[0][:, at] = mixed
            rest[1][0, :, i : i + 1] = peak
            rest[1][1, :, i : i + 1] = total


def out_kernel(blk, n_head, chunks, closes, *refs):
    attended = refs[:n_head]
    mine = refs[n_head : 2 * n_head]
    others = refs[2 * n_head : 3 * n_head]
    xs = refs[3 * n_head : 3 * n_head + chunks]
    mod_ref = refs[3 * n_head + chunks]
    outs = refs[3 * n_head + chunks + 1 :]
    b = lax.axis_index("branch")
    h = lax.axis_index("head")
    rows, quarter = xs[0].shape
    part = mine[0].shape[1]
    for weights, core in ((mine, b), (others, 1 - b)):
        total = None
        for value, weight in zip(attended, weights):
            term = jnp.dot(value[...], weight[...], preferred_element_type=F32)
            total = term if total is None else total + term
        start = pl.multiple_of(core * part, part)
        at = pl.ds(pl.multiple_of(h * quarter + start, part), part)
        here = pl.ds(start, part)
        gate = mod_ref[2, blk : blk + 1, at]
        for c, x_ref in enumerate(xs):
            old = x_ref[:, here].astype(F32)
            own = slice(c * rows, (c + 1) * rows)
            new = (old + gate * total[own, :]).astype(BF16)
            if not closes:
                outs[c][:, here] = new
            else:
                outs[0][own, here] = new
                outs[1][own, here] = jnp.where(b == 0, x_ref[:, here], new)


def join_kernel(*refs):
    strong_ref, forked, got_ref, out_ref = refs[0], refs[1:-2], refs[-2], refs[-1]
    b = lax.axis_index("branch")
    rows = strong_ref.shape[0]
    each = forked[0].shape[0]

    @pl.when(b == 0)
    def _():
        out_ref[:rows, :] = strong_ref[...]
        out_ref[rows:, :] = got_ref[...]

    @pl.when(b != 0)
    def _():
        out_ref[:rows, :] = got_ref[...]
        for c, ref in enumerate(forked):
            out_ref[rows + c * each : rows + (c + 1) * each, :] = ref[...]


def groups_of(n_seq, chunks):
    ring = range(n_seq)
    parts = [[(c, core, i) for i in ring] for c in range(chunks) for core in range(2)]
    head = sum(parts[:-2], [])
    return ([head] if head else []) + parts[-2:]


def block(tokens, xs, valid, weights, outs, mod, gains, blk, sizes, later):
    n_branch, n_seq, n_head, chunks = sizes
    if blk == 0:
        weights = (weights, swap(weights))
        outs = (outs, swap(outs))
        xs = take_half(tokens, n_branch, chunks)
    rows, quarter = xs[0].shape
    full = rows * chunks
    width = weights[0].shape[2]
    part = quarter // n_branch
    pieces = [[x] + [cross(x, "head", k, n_head) for k in range(1, n_head)] for x in xs]
    marks = blk == 0
    qkv = weights[0]
    shape = [SHAPE((2,) + qkv.shape[1:], BF16), SHAPE(mod.shape, F32), SHAPE(gains.shape, F32)]
    shape += [SHAPE((full, HEAD_DIM), F32)] * marks
    own, near_mod, near_gains, *mark = pl.pallas_call(
        functools.partial(prep_kernel, marks),
        out_shape=shape,
        in_specs=[FAR] * 3 + [SMEM] * marks,
        out_specs=[VMEM] * (3 + marks),
        scratch_shapes=[pltpu.SemaphoreType.DMA((3,))],
        compiler_params=params(16),
    )(far(qkv), far(mod), far(gains), *([valid] * marks))
    valid = mark[0] if marks else valid
    weights = (own, weights[1])
    blocks, moded = [], []
    for c in range(chunks):
        packed, mods = pl.pallas_call(
            functools.partial(kv_kernel, blk, c, n_head),
            out_shape=(SHAPE((rows, 2 * width), BF16), SHAPE((n_head, rows, quarter), BF16)),
            in_specs=[VMEM] * (n_head + 5),
            out_specs=(VMEM, VMEM),
            compiler_params=params(16),
        )(*pieces[c], *weights, near_mod, near_gains, valid)
        moded.append(mods)
        blocks.append([packed] + [turn(packed, "seq", k, n_seq) for k in range(1, n_seq)])
    *spread, own = pl.pallas_call(
        functools.partial(cut_kernel, n_head),
        out_shape=[SHAPE((width, part), BF16)] * (n_head + 1)
        + [SHAPE((1,) + qkv.shape[1:], BF16)],
        in_specs=[VMEM] * 2 + [FAR],
        out_specs=[VMEM] * (n_head + 2),
        scratch_shapes=[pltpu.SemaphoreType.DMA],
        compiler_params=params(8),
    )(*outs, far(qkv))
    mine = [spread[0]] + [cross(spread[k], "head", k, n_head) for k in range(1, n_head)]
    query = pl.pallas_call(
        functools.partial(q_kernel, blk, n_head, chunks),
        out_shape=SHAPE((full, width), BF16),
        in_specs=[VMEM] * (chunks + 3),
        out_specs=VMEM,
        compiler_params=params(16),
    )(*moded, own, weights[1], near_gains)
    if blk == 0:
        qkv, out_weight = later
        later = ((qkv, swap(qkv)), (out_weight, swap(out_weight)))
    held = [[line, [swap(p) for p in line]] for line in blocks]
    others = [spread[n_head]] + [swap(p) for p in mine[1:]]
    groups = groups_of(n_seq, chunks)
    carry = []
    for i, group in enumerate(groups):
        closes = i == len(groups) - 1
        shape = [SHAPE((full, width), F32), SHAPE((2, full, HEAD_DIM), F32)]
        if closes:
            shape = [SHAPE((full, width), BF16)]
        carry = pl.pallas_call(
            functools.partial(step_kernel, len(group), i == 0, closes),
            out_shape=shape,
            in_specs=[VMEM] * (1 + len(group) + len(carry)),
            out_specs=[VMEM] * len(shape),
            compiler_params=params(16),
        )(query, *[held[c][core][k] for c, core, k in group], *carry)
    (attended,) = carry
    gathered = [attended] + [cross(attended, "head", k, n_head) for k in range(1, n_head)]
    shape = [SHAPE((rows, quarter), BF16)] * chunks
    if blk == 1:
        shape = [SHAPE((full, quarter), BF16)] * 2
    out = pl.pallas_call(
        functools.partial(out_kernel, blk, n_head, chunks, blk == 1),
        out_shape=shape,
        in_specs=[VMEM] * (3 * n_head + chunks + 1),
        out_specs=[VMEM] * len(shape),
        compiler_params=params(16),
    )(*gathered, *mine, *others, *xs, near_mod)
    return out, valid, later


def solution(mesh):
    n_branch, n_seq, n_head = (mesh.shape[a] for a in ("branch", "seq", "head"))
    chunks = 2 if n_seq <= 8 else 1
    sizes = n_branch, n_seq, n_head, chunks

    def per_device(
        tokens, valid_counts, shared_qkv, shared_out, skipped_qkv, skipped_out, modulation, qk_gains
    ):
        mod = modulation.transpose(1, 0, 2)
        later = skipped_qkv.transpose(1, 0, 2), skipped_out
        forked, valid, later = block(
            tokens, None, valid_counts, shared_qkv.transpose(1, 0, 2), shared_out, mod,
            qk_gains, 0, sizes, later,
        )
        (strong, sent), _, _ = block(
            None, forked, valid, *later, mod, qk_gains, 1, sizes, None
        )
        got = swap(sent)
        rows, quarter = strong.shape
        out = pl.pallas_call(
            join_kernel,
            out_shape=SHAPE((2 * rows, quarter), BF16),
            in_specs=[VMEM] * (2 + chunks),
            out_specs=VMEM,
            compiler_params=params(8),
            name="join",
        )(strong, *forked, got)
        return out[None]

    in_specs = (
        P("seq", "head"),
        P("seq"),
        P("branch", None, "head"),
        P("head", "branch"),
        P("branch", None, "head"),
        P("head", "branch"),
        P(),
        P(),
    )
    return jax.shard_map(
        per_device,
        mesh=mesh,
        in_specs=in_specs,
        out_specs=P("branch", "seq", "head"),
        check_vma=False,
    )
```

time: 123 us -> 135 us (1.098)
  starting transfers between devices: 47.1 us -> 56.9 us
  Pallas kernels: 19.4 us -> 22.3 us
    ppermute x18 -> x24, waiting for transfers between devices: 21.2 us -> 32.3 us  [cross(): return lax.ppermute(x, axis, [(i, i ^ k) for i in range(n)])]
    ppermute x9 -> x12, waiting for transfers between devices: 21.8 us -> 15.4 us  [turn(): return lax.ppermute(x, axis, [(i, (i + k) % n) for i in range(n)])]
    ppermute x18 -> x24, starting transfers between devices: 25 us -> 31.2 us  [cross(): return lax.ppermute(x, axis, [(i, i ^ k) for i in range(n)])]
    ppermute x19 -> x27, waiting for transfers between devices: 10.4 us -> 5.53 us  [swap(): return lax.ppermute(x, 'branch', [(0, 1), (1, 0)])]
    pallas_call x14 -> x19, Pallas kernels: 18.6 us -> 21.6 us  [the longest x6 6.08 us: block(): pl.pallas_call(functools.partial(step_kernel, len(group), i == 0, closes)...]
    ppermute x9 -> x12, starting transfers between devices: 18.7 us -> 20.7 us  [turn(): return lax.ppermute(x, axis, [(i, (i + k) % n) for i in range(n)])]
    ppermute x19 -> x27, starting transfers between devices: 3.43 us -> 4.95 us  [swap(): return lax.ppermute(x, 'branch', [(0, 1), (1, 0)])]
  transfers between devices with their start and end apart: 46 -> 63, of which waited for: 21 -> 24; matrix products, arithmetic and copies ran while one was open for 0% -> 0% of each run, Pallas kernels for 15% -> 16%
where the time goes in v4:
time: 135 us
  starting transfers between devices  56.9 us (42%)
  waiting for transfers between devices  53.3 us (39%)
  Pallas kernels  22.3 us (17%)
    ppermute x24, waiting for transfers between devices, cross(): return lax.ppermute(x, axis, [(i, i ^ k) for i in range(n)])  32.3 us
    ppermute x24, starting transfers between devices, cross(): return lax.ppermute(x, axis, [(i, i ^ k) for i in range(n)])  31.2 us
    ppermute x12, starting transfers between devices, turn(): return lax.ppermute(x, axis, [(i, (i + k) % n) for i in range(n)])  20.7 us
    ppermute x12, waiting for transfers between devices, turn(): return lax.ppermute(x, axis, [(i, (i + k) % n) for i in range(n)])  15.4 us
    pallas_call x6, Pallas kernels, block(): pl.pallas_call(functools.partial(step_kernel, len(group), i == 0, closes)...  6.08 us
    ppermute x27, waiting for transfers between devices, swap(): return lax.ppermute(x, 'branch', [(0, 1), (1, 0)])  5.53 us
    pallas_call x4, Pallas kernels, block(): pl.pallas_call(functools.partial(kv_kernel, blk, c, n_head), out_shape=(S...  5.19 us
    ppermute x27, starting transfers between devices, swap(): return lax.ppermute(x, 'branch', [(0, 1), (1, 0)])  4.95 us
  transfers between devices with their start and end apart: 63, of which 24 were waited for; matrix products, arithmetic and copies ran while one was open for 0% of the time, Pallas kernels for 16%

profile of v4, /device:TPU:0, one launch (start us, length us, event | category | flops | bytes accessed | tf_op | source)
XLA Modules:
  0.0 134.6 jit_solution(1845131128077028084)
XLA Ops:
  2.0 2.5 %collective-permute-start.4 = (bf16[64,768]{1,0:T(8,128)(2,1)S(1)}, bf16[64,768]{1,0:T(8,128)(2,1)S(1)}, u32[]{:S(2)}, u32[]{:S(2)}) collective-permute-start(bf16[64,768]{1,0:T(8,128)(2,1)S(1)} %get-tuple-element.52.refs_0_.refs_13_), channel_id=1, source_target_pairs={{0,1},{1,0},{2,3},{3,2},{4,5},{5,4},{6,7},{7,6},{8,9},{9,8},{10,11... | collective-permute-start | bytes 294920 | tf_op jit(solution)/shard_map/ppermute | solution.py:30
  4.5 1.5 %collective-permute-start.5 = (bf16[64,768]{1,0:T(8,128)(2,1)S(1)}, bf16[64,768]{1,0:T(8,128)(2,1)S(1)}, u32[]{:S(2)}, u32[]{:S(2)}) collective-permute-start(bf16[64,768]{1,0:T(8,128)(2,1)S(1)} %get-tuple-element.52.refs_0_.refs_13_), channel_id=1, source_target_pairs={{0,2},{1,3},{2,0},{3,1},{4,6},{5,7},{6,4},{7,5},{8,10},{9,11},{10,... | collective-permute-start | bytes 294920 | tf_op jit(solution)/shard_map/ppermute | solution.py:30
  6.0 1.9 %collective-permute-done.4.refs_1_ = bf16[64,768]{1,0:T(8,128)(2,1)S(1)} collective-permute-done((bf16[64,768]{1,0:T(8,128)(2,1)S(1)}, bf16[64,768]{1,0:T(8,128)(2,1)S(1)}, u32[]{:S(2)}, u32[]{:S(2)}) %collective-permute-start.4) | collective-permute-done | bytes 98336 | tf_op jit(solution)/shard_map/ppermute | solution.py:30
  8.0 2.7 %collective-permute-start.6 = (bf16[64,768]{1,0:T(8,128)(2,1)S(1)}, bf16[64,768]{1,0:T(8,128)(2,1)S(1)}, u32[]{:S(2)}, u32[]{:S(2)}) collective-permute-start(bf16[64,768]{1,0:T(8,128)(2,1)S(1)} %get-tuple-element.52.refs_0_.refs_13_), channel_id=1, source_target_pairs={{0,3},{1,2},{2,1},{3,0},{4,7},{5,6},{6,5},{7,4},{8,11},{9,10},{10,... | collective-permute-start | bytes 294920 | tf_op jit(solution)/shard_map/ppermute | solution.py:30
  11.2 2.1 %collective-permute-done.7.across_ref = bf16[384,1536]{1,0:T(8,128)(2,1)S(1)} collective-permute-done((bf16[384,1536]{1,0:T(8,128)(2,1)}, bf16[384,1536]{1,0:T(8,128)(2,1)S(1)}, u32[]{:S(2)}, u32[]{:S(2)}) %collective-permute-start.7) | collective-permute-done | bytes 1179680 | tf_op jit(solution)/shard_map/ppermute | solution.py:34
  13.3 2.9 %collective-permute-start.1 = (bf16[64,768]{1,0:T(8,128)(2,1)S(1)}, bf16[64,768]{1,0:T(8,128)(2,1)S(1)}, u32[]{:S(2)}, u32[]{:S(2)}) collective-permute-start(bf16[64,768]{1,0:T(8,128)(2,1)S(1)} %get-tuple-element.46.refs_0_.refs_12_), channel_id=1, source_target_pairs={{0,2},{1,3},{2,0},{3,1},{4,6},{5,7},{6,4},{7,5},{8,10},{9,11},{10,... | collective-permute-start | bytes 294920 | tf_op jit(solution)/shard_map/ppermute | solution.py:30
  18.8 1.5 %collective-permute-start.2 = (bf16[64,768]{1,0:T(8,128)(2,1)S(1)}, bf16[64,768]{1,0:T(8,128)(2,1)S(1)}, u32[]{:S(2)}, u32[]{:S(2)}) collective-permute-start(bf16[64,768]{1,0:T(8,128)(2,1)S(1)} %get-tuple-element.46.refs_0_.refs_12_), channel_id=1, source_target_pairs={{0,3},{1,2},{2,1},{3,0},{4,7},{5,6},{6,5},{7,4},{8,11},{9,10},{10,... | collective-permute-start | bytes 294920 | tf_op jit(solution)/shard_map/ppermute | solution.py:30
  20.5 1.9 %collective-permute-start.26 = (bf16[384,384]{1,0:T(8,128)(2,1)S(1)}, bf16[384,384]{1,0:T(8,128)(2,1)S(1)}, u32[]{:S(2)}, u32[]{:S(2)}) collective-permute-start(bf16[384,384]{1,0:T(8,128)(2,1)S(1)} %get-tuple-element.63), channel_id=1, source_target_pairs={{0,2},{1,3},{2,0},{3,1},{4,6},{5,7},{6,4},{7,5},{8,10},{9,11},{10,... | collective-permute-start | bytes 884744 | tf_op jit(solution)/shard_map/ppermute | solution.py:30
  22.4 3.0 %collective-permute-done.2.refs_3_ = bf16[64,768]{1,0:T(8,128)(2,1)S(1)} collective-permute-done((bf16[64,768]{1,0:T(8,128)(2,1)S(1)}, bf16[64,768]{1,0:T(8,128)(2,1)S(1)}, u32[]{:S(2)}, u32[]{:S(2)}) %collective-permute-start.2) | collective-permute-done | bytes 98336 | tf_op jit(solution)/shard_map/ppermute | solution.py:30
  25.4 1.5 %collective-permute-start.27 = (bf16[384,384]{1,0:T(8,128)(2,1)S(1)}, bf16[384,384]{1,0:T(8,128)(2,1)S(1)}, u32[]{:S(2)}, u32[]{:S(2)}) collective-permute-start(bf16[384,384]{1,0:T(8,128)(2,1)S(1)} %get-tuple-element.64), channel_id=1, source_target_pairs={{0,3},{1,2},{2,1},{3,0},{4,7},{5,6},{6,5},{7,4},{8,11},{9,10},{10,... | collective-permute-start | bytes 884744 | tf_op jit(solution)/shard_map/ppermute | solution.py:30
  27.6 1.7 %shard_map.82 = (bf16[2,1536,384]{2,1,0:T(8,128)(2,1)S(1)}, f32[3,2,3072]{2,1,0:T(2,128)S(1)}, f32[2,2,128]{2,1,0:T(2,128)S(1)}, f32[128,128]{1,0:T(8,128)S(1)}) custom-call(bf16[3,1536,384]{2,1,0:T(8,128)(2,1)} %bitcast.6, f32[3,2,3072]{2,1,0:T(2,128)} %bitcast.10, f32[2,2,128]{2,1,0:T(2,128)} %refs_2_.3, s32[1]{0:T(128)S(6)} %copy.9.refs_3_), custom_call_target="tpu_custom_call" | custom-call | tf_op jit(solution)/shard_map/pallas_call | solution.py:299
  30.6 1.7 %collective-permute-start.15 = (bf16[64,768]{1,0:T(8,128)(2,1)S(1)}, bf16[64,768]{1,0:T(8,128)(2,1)S(1)}, u32[]{:S(2)}, u32[]{:S(2)}) collective-permute-start(bf16[64,768]{1,0:T(8,128)(2,1)S(1)} %get-tuple-element.56.refs_1_), channel_id=1, source_target_pairs={{0,4},{4,8},{8,12},{12,0},{1,5},{5,9},{9,13},{13,1},{2,6},{6,10},{... | collective-permute-start | bytes 294920 | tf_op jit(solution)/shard_map/ppermute | solution.py:26
  32.3 2.6 %collective-permute-start.16 = (bf16[64,768]{1,0:T(8,128)(2,1)S(1)}, bf16[64,768]{1,0:T(8,128)(2,1)S(1)}, u32[]{:S(2)}, u32[]{:S(2)}) collective-permute-start(bf16[64,768]{1,0:T(8,128)(2,1)S(1)} %get-tuple-element.56.refs_1_), channel_id=1, source_target_pairs={{0,8},{4,12},{8,0},{12,4},{1,9},{5,13},{9,1},{13,5},{2,10},{6,14},... | collective-permute-start | bytes 294920 | tf_op jit(solution)/shard_map/ppermute | solution.py:26
  37.1 3.6 %collective-permute-start.17 = (bf16[64,768]{1,0:T(8,128)(2,1)S(1)}, bf16[64,768]{1,0:T(8,128)(2,1)S(1)}, u32[]{:S(2)}, u32[]{:S(2)}) collective-permute-start(bf16[64,768]{1,0:T(8,128)(2,1)S(1)} %get-tuple-element.56.refs_1_), channel_id=1, source_target_pairs={{0,12},{4,0},{8,4},{12,8},{1,13},{5,1},{9,5},{13,9},{2,14},{6,2},{... | collective-permute-start | bytes 294920 | tf_op jit(solution)/shard_map/ppermute | solution.py:26
  43.2 4.4 %collective-permute-start.13 = (bf16[64,768]{1,0:T(8,128)(2,1)S(1)}, bf16[64,768]{1,0:T(8,128)(2,1)S(1)}, u32[]{:S(2)}, u32[]{:S(2)}) collective-permute-start(bf16[64,768]{1,0:T(8,128)(2,1)S(1)} %get-tuple-element.55.refs_1_), channel_id=1, source_target_pairs={{0,12},{4,0},{8,4},{12,8},{1,13},{5,1},{9,5},{13,9},{2,14},{6,2},{... | collective-permute-start | bytes 294920 | tf_op jit(solution)/shard_map/ppermute | solution.py:26
  48.7 1.6 %collective-permute-done.13.refs_4_ = bf16[64,768]{1,0:T(8,128)(2,1)S(1)} collective-permute-done((bf16[64,768]{1,0:T(8,128)(2,1)S(1)}, bf16[64,768]{1,0:T(8,128)(2,1)S(1)}, u32[]{:S(2)}, u32[]{:S(2)}) %collective-permute-start.13) | collective-permute-done | bytes 98336 | tf_op jit(solution)/shard_map/ppermute | solution.py:26
  50.2 3.8 %collective-permute-done.9.refs_2_ = bf16[64,768]{1,0:T(8,128)(2,1)S(1)} collective-permute-done((bf16[64,768]{1,0:T(8,128)(2,1)S(1)}, bf16[64,768]{1,0:T(8,128)(2,1)S(1)}, u32[]{:S(2)}, u32[]{:S(2)}) %collective-permute-start.9) | collective-permute-done | bytes 98336 | tf_op jit(solution)/shard_map/ppermute | solution.py:26
  61.2 2.1 %collective-permute-start.22 = (bf16[128,384]{1,0:T(8,128)(2,1)S(1)}, bf16[128,384]{1,0:T(8,128)(2,1)S(1)}, u32[]{:S(2)}, u32[]{:S(2)}) collective-permute-start(bf16[128,384]{1,0:T(8,128)(2,1)S(1)} %shard_map.89.refs_0_), channel_id=1, source_target_pairs={{0,1},{1,0},{2,3},{3,2},{4,5},{5,4},{6,7},{7,6},{8,9},{9,8},{10,11... | collective-permute-start | bytes 294920 | tf_op jit(solution)/shard_map/ppermute | solution.py:30
  63.2 1.5 %collective-permute-start.23 = (bf16[128,384]{1,0:T(8,128)(2,1)S(1)}, bf16[128,384]{1,0:T(8,128)(2,1)S(1)}, u32[]{:S(2)}, u32[]{:S(2)}) collective-permute-start(bf16[128,384]{1,0:T(8,128)(2,1)S(1)} %shard_map.89.refs_0_), channel_id=1, source_target_pairs={{0,2},{1,3},{2,0},{3,1},{4,6},{5,7},{6,4},{7,5},{8,10},{9,11},{10,... | collective-permute-start | bytes 294920 | tf_op jit(solution)/shard_map/ppermute | solution.py:30
  64.8 1.6 %collective-permute-done.22.refs_1_ = bf16[128,384]{1,0:T(8,128)(2,1)S(1)} collective-permute-done((bf16[128,384]{1,0:T(8,128)(2,1)S(1)}, bf16[128,384]{1,0:T(8,128)(2,1)S(1)}, u32[]{:S(2)}, u32[]{:S(2)}) %collective-permute-start.22) | collective-permute-done | bytes 98336 | tf_op jit(solution)/shard_map/ppermute | solution.py:30
  66.4 2.5 %collective-permute-done.23.refs_2_ = bf16[128,384]{1,0:T(8,128)(2,1)S(1)} collective-permute-done((bf16[128,384]{1,0:T(8,128)(2,1)S(1)}, bf16[128,384]{1,0:T(8,128)(2,1)S(1)}, u32[]{:S(2)}, u32[]{:S(2)}) %collective-permute-start.23) | collective-permute-done | bytes 98336 | tf_op jit(solution)/shard_map/ppermute | solution.py:30
  76.1 1.8 %collective-permute-start.58 = (bf16[384,384]{1,0:T(8,128)(2,1)S(1)}, bf16[384,384]{1,0:T(8,128)(2,1)S(1)}, u32[]{:S(2)}, u32[]{:S(2)}) collective-permute-start(bf16[384,384]{1,0:T(8,128)(2,1)S(1)} %get-tuple-element.83), channel_id=1, source_target_pairs={{0,3},{1,2},{2,1},{3,0},{4,7},{5,6},{6,5},{7,4},{8,11},{9,10},{10,... | collective-permute-start | bytes 884744 | tf_op jit(solution)/shard_map/ppermute | solution.py:30
  80.2 15.1 %collective-permute-done.32.refs_2_ = bf16[64,768]{1,0:T(8,128)(2,1)S(1)} collective-permute-done((bf16[64,768]{1,0:T(8,128)(2,1)S(1)}, bf16[64,768]{1,0:T(8,128)(2,1)S(1)}, u32[]{:S(2)}, u32[]{:S(2)}) %collective-permute-start.32) | collective-permute-done | bytes 98336 | tf_op jit(solution)/shard_map/ppermute | solution.py:30
  96.1 1.7 %shard_map.91 = (bf16[2,1536,384]{2,1,0:T(8,128)(2,1)S(1)}, f32[3,2,3072]{2,1,0:T(2,128)S(1)}, f32[2,2,128]{2,1,0:T(2,128)S(1)}) custom-call(bf16[3,1536,384]{2,1,0:T(8,128)(2,1)} %bitcast.9, f32[3,2,3072]{2,1,0:T(2,128)} %bitcast.11, f32[2,2,128]{2,1,0:T(2,128)} %refs_2_.3), custom_call_target="tpu_custom_call" | custom-call | tf_op jit(solution)/shard_map/pallas_call | solution.py:299
  99.2 1.9 %collective-permute-done.36.refs_2_ = bf16[64,768]{1,0:T(8,128)(2,1)S(1)} collective-permute-done((bf16[64,768]{1,0:T(8,128)(2,1)S(1)}, bf16[64,768]{1,0:T(8,128)(2,1)S(1)}, u32[]{:S(2)}, u32[]{:S(2)}) %collective-permute-start.36) | collective-permute-done | bytes 98336 | tf_op jit(solution)/shard_map/ppermute | solution.py:30
  102.7 3.7 %collective-permute-start.48 = (bf16[64,768]{1,0:T(8,128)(2,1)S(1)}, bf16[64,768]{1,0:T(8,128)(2,1)S(1)}, u32[]{:S(2)}, u32[]{:S(2)}) collective-permute-start(bf16[64,768]{1,0:T(8,128)(2,1)S(1)} %get-tuple-element.75.refs_1_), channel_id=1, source_target_pairs={{0,12},{4,0},{8,4},{12,8},{1,13},{5,1},{9,5},{13,9},{2,14},{6,2},{... | collective-permute-start | bytes 294920 | tf_op jit(solution)/shard_map/ppermute | solution.py:26
  108.8 2.6 %collective-permute-start.44 = (bf16[64,768]{1,0:T(8,128)(2,1)S(1)}, bf16[64,768]{1,0:T(8,128)(2,1)S(1)}, u32[]{:S(2)}, u32[]{:S(2)}) collective-permute-start(bf16[64,768]{1,0:T(8,128)(2,1)S(1)} %get-tuple-element.74.refs_1_), channel_id=1, source_target_pairs={{0,12},{4,0},{8,4},{12,8},{1,13},{5,1},{9,5},{13,9},{2,14},{6,2},{... | collective-permute-start | bytes 294920 | tf_op jit(solution)/shard_map/ppermute | solution.py:26
  111.9 2.1 %collective-permute-done.40.refs_2_ = bf16[64,768]{1,0:T(8,128)(2,1)S(1)} collective-permute-done((bf16[64,768]{1,0:T(8,128)(2,1)S(1)}, bf16[64,768]{1,0:T(8,128)(2,1)S(1)}, u32[]{:S(2)}, u32[]{:S(2)}) %collective-permute-start.40) | collective-permute-done | bytes 98336 | tf_op jit(solution)/shard_map/ppermute | solution.py:26
  114.0 3.7 %collective-permute-done.42.refs_3_ = bf16[64,768]{1,0:T(8,128)(2,1)S(1)} collective-permute-done((bf16[64,768]{1,0:T(8,128)(2,1)S(1)}, bf16[64,768]{1,0:T(8,128)(2,1)S(1)}, u32[]{:S(2)}, u32[]{:S(2)}) %collective-permute-start.42) | collective-permute-done | bytes 98336 | tf_op jit(solution)/shard_map/ppermute | solution.py:26
  125.0 2.6 %collective-permute-start.55 = (bf16[128,384]{1,0:T(8,128)(2,1)S(1)}, bf16[128,384]{1,0:T(8,128)(2,1)S(1)}, u32[]{:S(2)}, u32[]{:S(2)}) collective-permute-start(bf16[128,384]{1,0:T(8,128)(2,1)S(1)} %shard_map.98.refs_0_), channel_id=1, source_target_pairs={{0,3},{1,2},{2,1},{3,0},{4,7},{5,6},{6,5},{7,4},{8,11},{9,10},{10,... | collective-permute-start | bytes 294920 | tf_op jit(solution)/shard_map/ppermute | solution.py:30
  127.6 1.6 %collective-permute-done.53.refs_1_ = bf16[128,384]{1,0:T(8,128)(2,1)S(1)} collective-permute-done((bf16[128,384]{1,0:T(8,128)(2,1)S(1)}, bf16[128,384]{1,0:T(8,128)(2,1)S(1)}, u32[]{:S(2)}, u32[]{:S(2)}) %collective-permute-start.53) | collective-permute-done | bytes 98336 | tf_op jit(solution)/shard_map/ppermute | solution.py:30
  129.2 2.4 %collective-permute-done.54.refs_2_ = bf16[128,384]{1,0:T(8,128)(2,1)S(1)} collective-permute-done((bf16[128,384]{1,0:T(8,128)(2,1)S(1)}, bf16[128,384]{1,0:T(8,128)(2,1)S(1)}, u32[]{:S(2)}, u32[]{:S(2)}) %collective-permute-start.54) | collective-permute-done | bytes 98336 | tf_op jit(solution)/shard_map/ppermute | solution.py:30
  (118 shorter events, 45.8 us)
Async XLA Ops:
  0.0 26.9 %collective-permute-start.3 = (bf16[3,1536,384]{2,1,0:T(8,128)(2,1)}, bf16[3,1536,384]{2,1,0:T(8,128)(2,1)S(1)}, u32[]{:S(2)}, u32[]{:S(2)}) collective-permute-start(bf16[3,1536,384]{2,1,0:T(8,128)(2,1)} %bitcast.4), channel_id=1, source_target_pairs={{0,16},{16,0},{1,17},{17,1},{2,18},{18,2},{3,19},{19,3},{4,20},{20... | collective-permute-start | bytes 10616840 | tf_op jit(solution)/shard_map/ppermute | solution.py:34
  0.5 75.6 %collective-permute-start.34 = (bf16[3,1536,384]{2,1,0:T(8,128)(2,1)}, bf16[3,1536,384]{2,1,0:T(8,128)(2,1)S(1)}, u32[]{:S(2)}, u32[]{:S(2)}) collective-permute-start(bf16[3,1536,384]{2,1,0:T(8,128)(2,1)} %bitcast.7), channel_id=1, source_target_pairs={{0,16},{16,0},{1,17},{17,1},{2,18},{18,2},{3,19},{19,3},{4,20},{20... | collective-permute-start | bytes 10616840 | tf_op jit(solution)/shard_map/ppermute | solution.py:34
  0.5 12.8 %collective-permute-start.7 = (bf16[384,1536]{1,0:T(8,128)(2,1)}, bf16[384,1536]{1,0:T(8,128)(2,1)S(1)}, u32[]{:S(2)}, u32[]{:S(2)}) collective-permute-start(bf16[384,1536]{1,0:T(8,128)(2,1)} %near_ref.2), channel_id=1, source_target_pairs={{0,16},{16,0},{1,17},{17,1},{2,18},{18,2},{3,19},{19,3},{4,20},{20... | collective-permute-start | bytes 3538952 | tf_op jit(solution)/shard_map/ppermute | solution.py:34
  8.0 10.9 %collective-permute-start.6 = (bf16[64,768]{1,0:T(8,128)(2,1)S(1)}, bf16[64,768]{1,0:T(8,128)(2,1)S(1)}, u32[]{:S(2)}, u32[]{:S(2)}) collective-permute-start(bf16[64,768]{1,0:T(8,128)(2,1)S(1)} %get-tuple-element.52.refs_0_.refs_13_), channel_id=1, source_target_pairs={{0,3},{1,2},{2,1},{3,0},{4,7},{5,6},{6,5},{7,4},{8,11},{9,10},{10,... | collective-permute-start | bytes 294920 | tf_op jit(solution)/shard_map/ppermute | solution.py:30
  10.7 9.7 %collective-permute-start = (bf16[64,768]{1,0:T(8,128)(2,1)S(1)}, bf16[64,768]{1,0:T(8,128)(2,1)S(1)}, u32[]{:S(2)}, u32[]{:S(2)}) collective-permute-start(bf16[64,768]{1,0:T(8,128)(2,1)S(1)} %get-tuple-element.46.refs_0_.refs_12_), channel_id=1, source_target_pairs={{0,1},{1,0},{2,3},{3,2},{4,5},{5,4},{6,7},{7,6},{8,9},{9,8},{10,11... | collective-permute-start | bytes 294920 | tf_op jit(solution)/shard_map/ppermute | solution.py:30
  13.3 7.2 %collective-permute-start.1 = (bf16[64,768]{1,0:T(8,128)(2,1)S(1)}, bf16[64,768]{1,0:T(8,128)(2,1)S(1)}, u32[]{:S(2)}, u32[]{:S(2)}) collective-permute-start(bf16[64,768]{1,0:T(8,128)(2,1)S(1)} %get-tuple-element.46.refs_0_.refs_12_), channel_id=1, source_target_pairs={{0,2},{1,3},{2,0},{3,1},{4,6},{5,7},{6,4},{7,5},{8,10},{9,11},{10,... | collective-permute-start | bytes 294920 | tf_op jit(solution)/shard_map/ppermute | solution.py:30
  20.3 10.3 %collective-permute-start.25 = (bf16[384,384]{1,0:T(8,128)(2,1)S(1)}, bf16[384,384]{1,0:T(8,128)(2,1)S(1)}, u32[]{:S(2)}, u32[]{:S(2)}) collective-permute-start(bf16[384,384]{1,0:T(8,128)(2,1)S(1)} %get-tuple-element.62), channel_id=1, source_target_pairs={{0,1},{1,0},{2,3},{3,2},{4,5},{5,4},{6,7},{7,6},{8,9},{9,8},{10,11... | collective-permute-start | bytes 884744 | tf_op jit(solution)/shard_map/ppermute | solution.py:30
  20.5 11.8 %collective-permute-start.26 = (bf16[384,384]{1,0:T(8,128)(2,1)S(1)}, bf16[384,384]{1,0:T(8,128)(2,1)S(1)}, u32[]{:S(2)}, u32[]{:S(2)}) collective-permute-start(bf16[384,384]{1,0:T(8,128)(2,1)S(1)} %get-tuple-element.63), channel_id=1, source_target_pairs={{0,2},{1,3},{2,0},{3,1},{4,6},{5,7},{6,4},{7,5},{8,10},{9,11},{10,... | collective-permute-start | bytes 884744 | tf_op jit(solution)/shard_map/ppermute | solution.py:30
  25.4 11.7 %collective-permute-start.27 = (bf16[384,384]{1,0:T(8,128)(2,1)S(1)}, bf16[384,384]{1,0:T(8,128)(2,1)S(1)}, u32[]{:S(2)}, u32[]{:S(2)}) collective-permute-start(bf16[384,384]{1,0:T(8,128)(2,1)S(1)} %get-tuple-element.64), channel_id=1, source_target_pairs={{0,3},{1,2},{2,1},{3,0},{4,7},{5,6},{6,5},{7,4},{8,11},{9,10},{10,... | collective-permute-start | bytes 884744 | tf_op jit(solution)/shard_map/ppermute | solution.py:30
  26.9 46.1 %collective-permute-start.38 = (bf16[384,1536]{1,0:T(8,128)(2,1)S(1)}, bf16[384,1536]{1,0:T(8,128)(2,1)S(1)}, u32[]{:S(2)}, u32[]{:S(2)}) collective-permute-start(bf16[384,1536]{1,0:T(8,128)(2,1)S(1)} %copy-done.1), channel_id=1, source_target_pairs={{0,16},{16,0},{1,17},{17,1},{2,18},{18,2},{3,19},{19,3},{4,20},{20... | collective-permute-start | bytes 3538952 | tf_op jit(solution)/shard_map/ppermute | solution.py:34
  30.6 10.1 %collective-permute-start.15 = (bf16[64,768]{1,0:T(8,128)(2,1)S(1)}, bf16[64,768]{1,0:T(8,128)(2,1)S(1)}, u32[]{:S(2)}, u32[]{:S(2)}) collective-permute-start(bf16[64,768]{1,0:T(8,128)(2,1)S(1)} %get-tuple-element.56.refs_1_), channel_id=1, source_target_pairs={{0,4},{4,8},{8,12},{12,0},{1,5},{5,9},{9,13},{13,1},{2,6},{6,10},{... | collective-permute-start | bytes 294920 | tf_op jit(solution)/shard_map/ppermute | solution.py:26
  32.3 9.7 %collective-permute-start.16 = (bf16[64,768]{1,0:T(8,128)(2,1)S(1)}, bf16[64,768]{1,0:T(8,128)(2,1)S(1)}, u32[]{:S(2)}, u32[]{:S(2)}) collective-permute-start(bf16[64,768]{1,0:T(8,128)(2,1)S(1)} %get-tuple-element.56.refs_1_), channel_id=1, source_target_pairs={{0,8},{4,12},{8,0},{12,4},{1,9},{5,13},{9,1},{13,5},{2,10},{6,14},... | collective-permute-start | bytes 294920 | tf_op jit(solution)/shard_map/ppermute | solution.py:26
  40.7 6.9 %collective-permute-start.18 = (bf16[64,768]{1,0:T(8,128)(2,1)S(1)}, bf16[64,768]{1,0:T(8,128)(2,1)S(1)}, u32[]{:S(2)}, u32[]{:S(2)}) collective-permute-start(bf16[64,768]{1,0:T(8,128)(2,1)S(1)} %get-tuple-element.56.refs_1_), channel_id=1, source_target_pairs={{0,16},{16,0},{1,17},{17,1},{2,18},{18,2},{3,19},{19,3},{4,20},{20... | collective-permute-start | bytes 294920 | tf_op jit(solution)/shard_map/ppermute | solution.py:34
  43.2 7.0 %collective-permute-start.13 = (bf16[64,768]{1,0:T(8,128)(2,1)S(1)}, bf16[64,768]{1,0:T(8,128)(2,1)S(1)}, u32[]{:S(2)}, u32[]{:S(2)}) collective-permute-start(bf16[64,768]{1,0:T(8,128)(2,1)S(1)} %get-tuple-element.55.refs_1_), channel_id=1, source_target_pairs={{0,12},{4,0},{8,4},{12,8},{1,13},{5,1},{9,5},{13,9},{2,14},{6,2},{... | collective-permute-start | bytes 294920 | tf_op jit(solution)/shard_map/ppermute | solution.py:26
  56.8 7.9 %collective-permute-start.30 = (bf16[384,384]{1,0:T(8,128)(2,1)S(1)}, bf16[384,384]{1,0:T(8,128)(2,1)S(1)}, u32[]{:S(2)}, u32[]{:S(2)}) collective-permute-start(bf16[384,384]{1,0:T(8,128)(2,1)S(1)} %collective-permute-done.27.refs_7_), channel_id=1, source_target_pairs={{0,16},{16,0},{1,17},{17,1},{2,18},{18,2},{3,19},{19,3},{4,20},{20... | collective-permute-start | bytes 884744 | tf_op jit(solution)/shard_map/ppermute | solution.py:34
  70.9 6.9 %collective-permute-start.35 = (bf16[64,768]{1,0:T(8,128)(2,1)S(1)}, bf16[64,768]{1,0:T(8,128)(2,1)S(1)}, u32[]{:S(2)}, u32[]{:S(2)}) collective-permute-start(bf16[64,768]{1,0:T(8,128)(2,1)S(1)} %get-tuple-element.71.refs_0_.refs_13_.refs_2_), channel_id=1, source_target_pairs={{0,1},{1,0},{2,3},{3,2},{4,5},{5,4},{6,7},{7,6},{8,9},{9,8},{10,11... | collective-permute-start | bytes 294920 | tf_op jit(solution)/shard_map/ppermute | solution.py:30
  71.9 7.2 %collective-permute-start.31 = (bf16[64,768]{1,0:T(8,128)(2,1)S(1)}, bf16[64,768]{1,0:T(8,128)(2,1)S(1)}, u32[]{:S(2)}, u32[]{:S(2)}) collective-permute-start(bf16[64,768]{1,0:T(8,128)(2,1)S(1)} %get-tuple-element.66.refs_0_.refs_12_.refs_1_), channel_id=1, source_target_pairs={{0,1},{1,0},{2,3},{3,2},{4,5},{5,4},{6,7},{7,6},{8,9},{9,8},{10,11... | collective-permute-start | bytes 294920 | tf_op jit(solution)/shard_map/ppermute | solution.py:30
  74.3 28.3 %collective-permute-start.56 = (bf16[384,384]{1,0:T(8,128)(2,1)S(1)}, bf16[384,384]{1,0:T(8,128)(2,1)S(1)}, u32[]{:S(2)}, u32[]{:S(2)}) collective-permute-start(bf16[384,384]{1,0:T(8,128)(2,1)S(1)} %get-tuple-element.81), channel_id=1, source_target_pairs={{0,1},{1,0},{2,3},{3,2},{4,5},{5,4},{6,7},{7,6},{8,9},{9,8},{10,11... | collective-permute-start | bytes 884744 | tf_op jit(solution)/shard_map/ppermute | solution.py:30
  75.3 31.1 %collective-permute-start.57 = (bf16[384,384]{1,0:T(8,128)(2,1)S(1)}, bf16[384,384]{1,0:T(8,128)(2,1)S(1)}, u32[]{:S(2)}, u32[]{:S(2)}) collective-permute-start(bf16[384,384]{1,0:T(8,128)(2,1)S(1)} %get-tuple-element.82), channel_id=1, source_target_pairs={{0,2},{1,3},{2,0},{3,1},{4,6},{5,7},{6,4},{7,5},{8,10},{9,11},{10,... | collective-permute-start | bytes 884744 | tf_op jit(solution)/shard_map/ppermute | solution.py:30
  76.1 30.3 %collective-permute-start.58 = (bf16[384,384]{1,0:T(8,128)(2,1)S(1)}, bf16[384,384]{1,0:T(8,128)(2,1)S(1)}, u32[]{:S(2)}, u32[]{:S(2)}) collective-permute-start(bf16[384,384]{1,0:T(8,128)(2,1)S(1)} %get-tuple-element.83), channel_id=1, source_target_pairs={{0,3},{1,2},{2,1},{3,0},{4,7},{5,6},{6,5},{7,4},{8,11},{9,10},{10,... | collective-permute-start | bytes 884744 | tf_op jit(solution)/shard_map/ppermute | solution.py:30
  77.9 17.5 %collective-permute-start.32 = (bf16[64,768]{1,0:T(8,128)(2,1)S(1)}, bf16[64,768]{1,0:T(8,128)(2,1)S(1)}, u32[]{:S(2)}, u32[]{:S(2)}) collective-permute-start(bf16[64,768]{1,0:T(8,128)(2,1)S(1)} %get-tuple-element.66.refs_0_.refs_12_.refs_1_), channel_id=1, source_target_pairs={{0,2},{1,3},{2,0},{3,1},{4,6},{5,7},{6,4},{7,5},{8,10},{9,11},{10,... | collective-permute-start | bytes 294920 | tf_op jit(solution)/shard_map/ppermute | solution.py:30
  79.1 16.3 %collective-permute-start.33 = (bf16[64,768]{1,0:T(8,128)(2,1)S(1)}, bf16[64,768]{1,0:T(8,128)(2,1)S(1)}, u32[]{:S(2)}, u32[]{:S(2)}) collective-permute-start(bf16[64,768]{1,0:T(8,128)(2,1)S(1)} %get-tuple-element.66.refs_0_.refs_12_.refs_1_), channel_id=1, source_target_pairs={{0,3},{1,2},{2,1},{3,0},{4,7},{5,6},{6,5},{7,4},{8,11},{9,10},{10,... | collective-permute-start | bytes 294920 | tf_op jit(solution)/shard_map/ppermute | solution.py:30
  101.1 7.7 %collective-permute-start.47 = (bf16[64,768]{1,0:T(8,128)(2,1)S(1)}, bf16[64,768]{1,0:T(8,128)(2,1)S(1)}, u32[]{:S(2)}, u32[]{:S(2)}) collective-permute-start(bf16[64,768]{1,0:T(8,128)(2,1)S(1)} %get-tuple-element.75.refs_1_), channel_id=1, source_target_pairs={{0,8},{4,12},{8,0},{12,4},{1,9},{5,13},{9,1},{13,5},{2,10},{6,14},... | collective-permute-start | bytes 294920 | tf_op jit(solution)/shard_map/ppermute | solution.py:26
  102.7 8.8 %collective-permute-start.48 = (bf16[64,768]{1,0:T(8,128)(2,1)S(1)}, bf16[64,768]{1,0:T(8,128)(2,1)S(1)}, u32[]{:S(2)}, u32[]{:S(2)}) collective-permute-start(bf16[64,768]{1,0:T(8,128)(2,1)S(1)} %get-tuple-element.75.refs_1_), channel_id=1, source_target_pairs={{0,12},{4,0},{8,4},{12,8},{1,13},{5,1},{9,5},{13,9},{2,14},{6,2},{... | collective-permute-start | bytes 294920 | tf_op jit(solution)/shard_map/ppermute | solution.py:26
  106.4 7.6 %collective-permute-start.40 = (bf16[64,768]{1,0:T(8,128)(2,1)S(1)}, bf16[64,768]{1,0:T(8,128)(2,1)S(1)}, u32[]{:S(2)}, u32[]{:S(2)}) collective-permute-start(bf16[64,768]{1,0:T(8,128)(2,1)S(1)} %get-tuple-element.74.refs_1_), channel_id=1, source_target_pairs={{0,4},{4,8},{8,12},{12,0},{1,5},{5,9},{9,13},{13,1},{2,6},{6,10},{... | collective-permute-start | bytes 294920 | tf_op jit(solution)/shard_map/ppermute | solution.py:26
  107.6 10.2 %collective-permute-start.42 = (bf16[64,768]{1,0:T(8,128)(2,1)S(1)}, bf16[64,768]{1,0:T(8,128)(2,1)S(1)}, u32[]{:S(2)}, u32[]{:S(2)}) collective-permute-start(bf16[64,768]{1,0:T(8,128)(2,1)S(1)} %get-tuple-element.74.refs_1_), channel_id=1, source_target_pairs={{0,8},{4,12},{8,0},{12,4},{1,9},{5,13},{9,1},{13,5},{2,10},{6,14},... | collective-permute-start | bytes 294920 | tf_op jit(solution)/shard_map/ppermute | solution.py:26
  108.8 9.0 %collective-permute-start.44 = (bf16[64,768]{1,0:T(8,128)(2,1)S(1)}, bf16[64,768]{1,0:T(8,128)(2,1)S(1)}, u32[]{:S(2)}, u32[]{:S(2)}) collective-permute-start(bf16[64,768]{1,0:T(8,128)(2,1)S(1)} %get-tuple-element.74.refs_1_), channel_id=1, source_target_pairs={{0,12},{4,0},{8,4},{12,8},{1,13},{5,1},{9,5},{13,9},{2,14},{6,2},{... | collective-permute-start | bytes 294920 | tf_op jit(solution)/shard_map/ppermute | solution.py:26
  111.4 6.8 %collective-permute-start.39 = (bf16[64,768]{1,0:T(8,128)(2,1)S(1)}, bf16[64,768]{1,0:T(8,128)(2,1)S(1)}, u32[]{:S(2)}, u32[]{:S(2)}) collective-permute-start(bf16[64,768]{1,0:T(8,128)(2,1)S(1)} %get-tuple-element.74.refs_1_), channel_id=1, source_target_pairs={{0,16},{16,0},{1,17},{17,1},{2,18},{18,2},{3,19},{19,3},{4,20},{20... | collective-permute-start | bytes 294920 | tf_op jit(solution)/shard_map/ppermute | solution.py:34
  111.4 6.9 %collective-permute-start.50 = (bf16[64,768]{1,0:T(8,128)(2,1)S(1)}, bf16[64,768]{1,0:T(8,128)(2,1)S(1)}, u32[]{:S(2)}, u32[]{:S(2)}) collective-permute-start(bf16[64,768]{1,0:T(8,128)(2,1)S(1)} %collective-permute-done.46.refs_2_), channel_id=1, source_target_pairs={{0,16},{16,0},{1,17},{17,1},{2,18},{18,2},{3,19},{19,3},{4,20},{20... | collective-permute-start | bytes 294920 | tf_op jit(solution)/shard_map/ppermute | solution.py:34
  117.7 7.3 %collective-permute-start.59 = (bf16[384,384]{1,0:T(8,128)(2,1)S(1)}, bf16[384,384]{1,0:T(8,128)(2,1)S(1)}, u32[]{:S(2)}, u32[]{:S(2)}) collective-permute-start(bf16[384,384]{1,0:T(8,128)(2,1)S(1)} %collective-permute-done.56.refs_5_), channel_id=1, source_target_pairs={{0,16},{16,0},{1,17},{17,1},{2,18},{18,2},{3,19},{19,3},{4,20},{20... | collective-permute-start | bytes 884744 | tf_op jit(solution)/shard_map/ppermute | solution.py:34
  118.3 9.2 %collective-permute-start.60 = (bf16[384,384]{1,0:T(8,128)(2,1)S(1)}, bf16[384,384]{1,0:T(8,128)(2,1)S(1)}, u32[]{:S(2)}, u32[]{:S(2)}) collective-permute-start(bf16[384,384]{1,0:T(8,128)(2,1)S(1)} %collective-permute-done.57.refs_6_), channel_id=1, source_target_pairs={{0,16},{16,0},{1,17},{17,1},{2,18},{18,2},{3,19},{19,3},{4,20},{20... | collective-permute-start | bytes 884744 | tf_op jit(solution)/shard_map/ppermute | solution.py:34
  118.8 8.8 %collective-permute-start.61 = (bf16[384,384]{1,0:T(8,128)(2,1)S(1)}, bf16[384,384]{1,0:T(8,128)(2,1)S(1)}, u32[]{:S(2)}, u32[]{:S(2)}) collective-permute-start(bf16[384,384]{1,0:T(8,128)(2,1)S(1)} %collective-permute-done.58.refs_7_), channel_id=1, source_target_pairs={{0,16},{16,0},{1,17},{17,1},{2,18},{18,2},{3,19},{19,3},{4,20},{20... | collective-permute-start | bytes 884744 | tf_op jit(solution)/shard_map/ppermute | solution.py:34
  (33 other events, 151.0 us)

commit v5 on v4

--- a/solution.py
+++ b/solution.py
@@ -69,34 +69,22 @@
     )(far(tokens))
 
 
-def prep_kernel(marks, *refs):
-    far_qkv, far_mod, far_gain = refs[:3]
-    rest = refs[3:]
-    if marks:
-        count_ref, rest = rest[0], rest[1:]
-    qkv_ref, mod_ref, gain_ref = rest[:3]
-    sems = rest[-1]
+def prep_kernel(far_qkv, far_mod, far_gain, count_ref, qkv_ref, mod_ref, gain_ref, mark_ref, sems):
     copies = [
         pltpu.make_async_copy(far_qkv.at[pl.ds(1, 2)], qkv_ref, sems.at[0]),
         pltpu.make_async_copy(far_mod, mod_ref, sems.at[1]),
         pltpu.make_async_copy(far_gain, gain_ref, sems.at[2]),
     ]
-    if marks:
-        mark_ref = rest[3]
     for copy in copies:
         copy.start()
-    if marks:
-        place = lax.broadcasted_iota(jnp.int32, mark_ref.shape, 0)
-        place = place + lax.axis_index("branch") * mark_ref.shape[0]
-        mark_ref[...] = jnp.where(place < count_ref[0], 0.0, 1.0).astype(F32)
+    place = lax.broadcasted_iota(jnp.int32, mark_ref.shape, 0)
+    place = place + lax.axis_index("branch") * mark_ref.shape[0]
+    mark_ref[...] = jnp.where(place < count_ref[0], 0.0, 1.0).astype(F32)
     for copy in copies:
         copy.wait()
 
 
-def cut_kernel(n_head, near_ref, across_ref, far_qkv, *refs):
-    pieces, query_ref, sem = refs[: n_head + 1], refs[n_head + 1], refs[n_head + 2]
-    fetch = pltpu.make_async_copy(far_qkv.at[pl.ds(0, 1)], query_ref, sem)
-    fetch.start()
+def cut_kernel(n_head, near_ref, across_ref, *pieces):
     b = lax.axis_index("branch")
     h = lax.axis_index("head")
     per_core = n_head // 2
@@ -115,8 +103,6 @@
         @pl.when(jnp.logical_not(mine))
         def _():
             piece[...] = across_ref[:, at]
-
-    fetch.wait()
 
 
 def contract(moded_ref, own_ref, other_ref, which, first, n_head):
@@ -150,6 +136,7 @@
     xs = refs[:n_head]
     own_ref, other_ref, mod_ref, gain_ref, mark_ref, packed_ref, moded_ref = refs[n_head:]
     rows = xs[0].shape[0]
+    first = other_ref.shape[0] - own_ref.shape[0]
     padding = mark_ref[chunk * rows : (chunk + 1) * rows, :] > 0.5
     h = lax.axis_index("head")
     quarter = xs[0].shape[1]
@@ -167,10 +154,10 @@
         gain = mod_ref[1, blk : blk + 1, at] + 1.0
         normed = (x[...].astype(F32) - mean) * scale
         moded_ref[k] = (normed * gain + shift).astype(BF16)
-    key = contract(moded_ref, own_ref, other_ref, 1, 1, n_head)
+    key = contract(moded_ref, own_ref, other_ref, 1, first, n_head)
     for i, out in enumerate(norm_heads(key, gain_ref[blk, 1:2, :], width)):
         packed_ref[:, i * HEAD_DIM : (i + 1) * HEAD_DIM] = jnp.where(padding, MARK, out).astype(BF16)
-    packed_ref[:, width:] = contract(moded_ref, own_ref, other_ref, 2, 1, n_head).astype(BF16)
+    packed_ref[:, width:] = contract(moded_ref, own_ref, other_ref, 2, first, n_head).astype(BF16)
 
 
 def q_kernel(blk, n_head, chunks, *refs):
@@ -194,34 +181,37 @@
     scale = math.log2(math.e) / HEAD_DIM**0.5
     rows = query_ref.shape[0]
     ones = jnp.ones((16, HEAD_DIM), BF16)
-    for i, lo in enumerate(range(0, width, HEAD_DIM)):
-        at = slice(lo, lo + HEAD_DIM)
+    heads = [slice(lo, lo + HEAD_DIM) for lo in range(0, width, HEAD_DIM)]
+    raw = []
+    for at in heads:
         key = jnp.concatenate([ref[:, at] for ref in blocks], axis=0)
+        query = jnp.concatenate([query_ref[:, at], ones], axis=0)
+        raw.append(
+            lax.dot_general(query, key, (((1,), (1,)), ((), ())), preferred_element_type=F32)
+        )
+    drop = jnp.where(raw[0][rows : rows + 1, :] > MARK_SUM, -1e30, 0.0)
+    scores = [one[:rows, :] * scale + drop for one in raw]
+    peaks = [jnp.max(one, axis=1, keepdims=True) for one in scores]
+    if not opens:
+        before = [stat_in[0, :, i : i + 1] for i in range(len(heads))]
+        peaks = [jnp.maximum(one, old) for one, old in zip(peaks, before)]
+    weights = [jnp.exp2(one - peak) for one, peak in zip(scores, peaks)]
+    totals = [jnp.sum(one, axis=1, keepdims=True) for one in weights]
+    for i, at in enumerate(heads):
         value = jnp.concatenate(
-            [ref[:, width + lo : width + lo + HEAD_DIM] for ref in blocks], axis=0
+            [ref[:, width + at.start : width + at.stop] for ref in blocks], axis=0
         )
-        query = jnp.concatenate([query_ref[:, at], ones], axis=0)
-        scores = lax.dot_general(
-            query, key, (((1,), (1,)), ((), ())), preferred_element_type=F32
-        )
-        drop = jnp.where(scores[rows : rows + 1, :] > MARK_SUM, -1e30, 0.0)
-        scores = scores[:rows, :] * scale + drop
-        peak = jnp.max(scores, axis=1, keepdims=True)
+        mixed = jnp.dot(weights[i].astype(BF16), value, preferred_element_type=F32)
+        total = totals[i]
         if not opens:
-            before = stat_in[0, :, i : i + 1]
-            peak = jnp.maximum(peak, before)
-        weight = jnp.exp2(scores - peak)
-        total = jnp.sum(weight, axis=1, keepdims=True)
-        mixed = jnp.dot(weight.astype(BF16), value, preferred_element_type=F32)
-        if not opens:
-            keep = jnp.exp2(before - peak)
+            keep = jnp.exp2(before[i] - peaks[i])
             mixed = mixed + mixed_in[:, at] * keep
             total = total + stat_in[1, :, i : i + 1] * keep
         if closes:
             rest[0][:, at] = (mixed / total).astype(BF16)
         else:
             rest[0][:, at] = mixed
-            rest[1][0, :, i : i + 1] = peak
+            rest[1][0, :, i : i + 1] = peaks[i]
             rest[1][1, :, i : i + 1] = total
 
 
@@ -277,8 +267,10 @@
 def groups_of(n_seq, chunks):
     ring = range(n_seq)
     parts = [[(c, core, i) for i in ring] for c in range(chunks) for core in range(2)]
-    head = sum(parts[:-2], [])
-    return ([head] if head else []) + parts[-2:]
+    joined = [parts[0]]
+    for i in range(1, len(parts) - 1, 2):
+        joined.append(parts[i] + parts[i + 1])
+    return joined + parts[-1:]
 
 
 def block(tokens, xs, valid, weights, outs, mod, gains, blk, sizes, later):
@@ -292,20 +284,21 @@
     width = weights[0].shape[2]
     part = quarter // n_branch
     pieces = [[x] + [cross(x, "head", k, n_head) for k in range(1, n_head)] for x in xs]
-    marks = blk == 0
     qkv = weights[0]
-    shape = [SHAPE((2,) + qkv.shape[1:], BF16), SHAPE(mod.shape, F32), SHAPE(gains.shape, F32)]
-    shape += [SHAPE((full, HEAD_DIM), F32)] * marks
-    own, near_mod, near_gains, *mark = pl.pallas_call(
-        functools.partial(prep_kernel, marks),
-        out_shape=shape,
-        in_specs=[FAR] * 3 + [SMEM] * marks,
-        out_specs=[VMEM] * (3 + marks),
-        scratch_shapes=[pltpu.SemaphoreType.DMA((3,))],
-        compiler_params=params(16),
-    )(far(qkv), far(mod), far(gains), *([valid] * marks))
-    valid = mark[0] if marks else valid
-    weights = (own, weights[1])
+    if blk == 0:
+        shape = [SHAPE((2,) + qkv.shape[1:], BF16)]
+        shape += [SHAPE(mod.shape, F32), SHAPE(gains.shape, F32), SHAPE((full, HEAD_DIM), F32)]
+        own, mod, gains, valid = pl.pallas_call(
+            prep_kernel,
+            out_shape=shape,
+            in_specs=[FAR] * 3 + [SMEM],
+            out_specs=[VMEM] * 4,
+            scratch_shapes=[pltpu.SemaphoreType.DMA((3,))],
+            compiler_params=params(16),
+            name="prep",
+        )(far(qkv), far(mod), far(gains), valid)
+    else:
+        own = qkv
     blocks, moded = [], []
     for c in range(chunks):
         packed, mods = pl.pallas_call(
@@ -314,18 +307,16 @@
             in_specs=[VMEM] * (n_head + 5),
             out_specs=(VMEM, VMEM),
             compiler_params=params(16),
-        )(*pieces[c], *weights, near_mod, near_gains, valid)
+        )(*pieces[c], own, weights[1], mod, gains, valid)
         moded.append(mods)
         blocks.append([packed] + [turn(packed, "seq", k, n_seq) for k in range(1, n_seq)])
-    *spread, own = pl.pallas_call(
+    spread = pl.pallas_call(
         functools.partial(cut_kernel, n_head),
-        out_shape=[SHAPE((width, part), BF16)] * (n_head + 1)
-        + [SHAPE((1,) + qkv.shape[1:], BF16)],
-        in_specs=[VMEM] * 2 + [FAR],
-        out_specs=[VMEM] * (n_head + 2),
-        scratch_shapes=[pltpu.SemaphoreType.DMA],
+        out_shape=[SHAPE((width, part), BF16)] * (n_head + 1),
+        in_specs=[VMEM] * 2,
+        out_specs=[VMEM] * (n_head + 1),
         compiler_params=params(8),
-    )(*outs, far(qkv))
+    )(*outs)
     mine = [spread[0]] + [cross(spread[k], "head", k, n_head) for k in range(1, n_head)]
     query = pl.pallas_call(
         functools.partial(q_kernel, blk, n_head, chunks),
@@ -333,7 +324,7 @@
         in_specs=[VMEM] * (chunks + 3),
         out_specs=VMEM,
         compiler_params=params(16),
-    )(*moded, own, weights[1], near_gains)
+    )(*moded, *weights, gains)
     if blk == 0:
         qkv, out_weight = later
         later = ((qkv, swap(qkv)), (out_weight, swap(out_weight)))
@@ -364,8 +355,8 @@
         in_specs=[VMEM] * (3 * n_head + chunks + 1),
         out_specs=[VMEM] * len(shape),
         compiler_params=params(16),
-    )(*gathered, *mine, *others, *xs, near_mod)
-    return out, valid, later
+    )(*gathered, *mine, *others, *xs, mod)
+    return out, (valid, mod, gains), later
 
 
 def solution(mesh):
@@ -378,12 +369,13 @@
     ):
         mod = modulation.transpose(1, 0, 2)
         later = skipped_qkv.transpose(1, 0, 2), skipped_out
-        forked, valid, later = block(
+        forked, near, later = block(
             tokens, None, valid_counts, shared_qkv.transpose(1, 0, 2), shared_out, mod,
             qk_gains, 0, sizes, later,
         )
+        valid, mod, gains = near
         (strong, sent), _, _ = block(
-            None, forked, valid, *later, mod, qk_gains, 1, sizes, None
+            None, forked, valid, *later, mod, gains, 1, sizes, None
         )
         got = swap(sent)
         rows, quarter = strong.shape

time: 135 us -> 131 us (0.970)
  Pallas kernels: 22.3 us -> 15.9 us
  starting transfers between devices: 56.9 us -> 62.7 us
  waiting for transfers between devices: 53.3 us -> 50 us
    ppermute x24, starting transfers between devices: 31.2 us -> 38.2 us  [cross(): return lax.ppermute(x, axis, [(i, i ^ k) for i in range(n)])]
    ppermute x12, waiting for transfers between devices: 15.4 us -> 12 us  [turn(): return lax.ppermute(x, axis, [(i, (i + k) % n) for i in range(n)])]
    pallas_call x6, Pallas kernels: 6.08 us -> 3.68 us  [block(): pl.pallas_call(functools.partial(step_kernel, len(group), i == 0, closes)...]
    pallas_call x2, Pallas kernels: 2.65 us -> 0.34 us  [block(): pl.pallas_call(functools.partial(cut_kernel, n_head), out_shape=[SHAPE((w...]
    ppermute x12, starting transfers between devices: 20.7 us -> 19 us  [turn(): return lax.ppermute(x, axis, [(i, (i + k) % n) for i in range(n)])]
    pallas_call x2 -> x1, Pallas kernels: 3.39 us -> 1.7 us  [block(): pl.pallas_call(prep_kernel, out_shape=shape, in_specs=[FAR] * 3 + [SMEM],...]
  transfers between devices with their start and end apart: 63 -> 63, of which waited for: 24 -> 24; matrix products, arithmetic and copies ran while one was open for 0% -> 0% of each run, Pallas kernels for 16% -> 11%
where the time goes in v5:
time: 131 us
  starting transfers between devices  62.7 us (48%)
  waiting for transfers between devices  50 us (38%)
  Pallas kernels  15.9 us (12%)
    ppermute x24, starting transfers between devices, cross(): return lax.ppermute(x, axis, [(i, i ^ k) for i in range(n)])  38.2 us
    ppermute x24, waiting for transfers between devices, cross(): return lax.ppermute(x, axis, [(i, i ^ k) for i in range(n)])  31.9 us
    ppermute x12, starting transfers between devices, turn(): return lax.ppermute(x, axis, [(i, (i + k) % n) for i in range(n)])  19 us
    ppermute x12, waiting for transfers between devices, turn(): return lax.ppermute(x, axis, [(i, (i + k) % n) for i in range(n)])  12 us
    ppermute x27, waiting for transfers between devices, swap(): return lax.ppermute(x, 'branch', [(0, 1), (1, 0)])  6.05 us
    ppermute x27, starting transfers between devices, swap(): return lax.ppermute(x, 'branch', [(0, 1), (1, 0)])  5.5 us
    pallas_call x4, Pallas kernels, block(): pl.pallas_call(functools.partial(kv_kernel, blk, c, n_head), out_shape=(S...  5.22 us
    pallas_call x6, Pallas kernels, block(): pl.pallas_call(functools.partial(step_kernel, len(group), i == 0, closes)...  3.68 us
  transfers between devices with their start and end apart: 63, of which 24 were waited for; matrix products, arithmetic and copies ran while one was open for 0% of the time, Pallas kernels for 11%

profile of v5, /device:TPU:0, one launch (start us, length us, event | category | flops | bytes accessed | tf_op | source)
XLA Modules:
  0.0 130.8 jit_solution(12967457846453078478)
XLA Ops:
  2.0 2.5 %collective-permute-start.4 = (bf16[64,768]{1,0:T(8,128)(2,1)S(1)}, bf16[64,768]{1,0:T(8,128)(2,1)S(1)}, u32[]{:S(2)}, u32[]{:S(2)}) collective-permute-start(bf16[64,768]{1,0:T(8,128)(2,1)S(1)} %get-tuple-element.47.refs_0_.refs_13_), channel_id=1, source_target_pairs={{0,1},{1,0},{2,3},{3,2},{4,5},{5,4},{6,7},{7,6},{8,9},{9,8},{10,11... | collective-permute-start | bytes 294920 | tf_op jit(solution)/shard_map/ppermute | solution.py:30
  4.5 1.5 %collective-permute-start.5 = (bf16[64,768]{1,0:T(8,128)(2,1)S(1)}, bf16[64,768]{1,0:T(8,128)(2,1)S(1)}, u32[]{:S(2)}, u32[]{:S(2)}) collective-permute-start(bf16[64,768]{1,0:T(8,128)(2,1)S(1)} %get-tuple-element.47.refs_0_.refs_13_), channel_id=1, source_target_pairs={{0,2},{1,3},{2,0},{3,1},{4,6},{5,7},{6,4},{7,5},{8,10},{9,11},{10,... | collective-permute-start | bytes 294920 | tf_op jit(solution)/shard_map/ppermute | solution.py:30
  6.0 1.9 %collective-permute-done.4.refs_1_ = bf16[64,768]{1,0:T(8,128)(2,1)S(1)} collective-permute-done((bf16[64,768]{1,0:T(8,128)(2,1)S(1)}, bf16[64,768]{1,0:T(8,128)(2,1)S(1)}, u32[]{:S(2)}, u32[]{:S(2)}) %collective-permute-start.4) | collective-permute-done | bytes 98336 | tf_op jit(solution)/shard_map/ppermute | solution.py:30
  8.0 2.7 %collective-permute-start.6 = (bf16[64,768]{1,0:T(8,128)(2,1)S(1)}, bf16[64,768]{1,0:T(8,128)(2,1)S(1)}, u32[]{:S(2)}, u32[]{:S(2)}) collective-permute-start(bf16[64,768]{1,0:T(8,128)(2,1)S(1)} %get-tuple-element.47.refs_0_.refs_13_), channel_id=1, source_target_pairs={{0,3},{1,2},{2,1},{3,0},{4,7},{5,6},{6,5},{7,4},{8,11},{9,10},{10,... | collective-permute-start | bytes 294920 | tf_op jit(solution)/shard_map/ppermute | solution.py:30
  11.2 2.1 %collective-permute-done.24.across_ref = bf16[384,1536]{1,0:T(8,128)(2,1)S(1)} collective-permute-done((bf16[384,1536]{1,0:T(8,128)(2,1)}, bf16[384,1536]{1,0:T(8,128)(2,1)S(1)}, u32[]{:S(2)}, u32[]{:S(2)}) %collective-permute-start.24) | collective-permute-done | bytes 1179680 | tf_op jit(solution)/shard_map/ppermute | solution.py:34
  13.3 2.9 %collective-permute-start.1 = (bf16[64,768]{1,0:T(8,128)(2,1)S(1)}, bf16[64,768]{1,0:T(8,128)(2,1)S(1)}, u32[]{:S(2)}, u32[]{:S(2)}) collective-permute-start(bf16[64,768]{1,0:T(8,128)(2,1)S(1)} %get-tuple-element.41.refs_0_.refs_12_), channel_id=1, source_target_pairs={{0,2},{1,3},{2,0},{3,1},{4,6},{5,7},{6,4},{7,5},{8,10},{9,11},{10,... | collective-permute-start | bytes 294920 | tf_op jit(solution)/shard_map/ppermute | solution.py:30
  17.6 1.5 %collective-permute-start.2 = (bf16[64,768]{1,0:T(8,128)(2,1)S(1)}, bf16[64,768]{1,0:T(8,128)(2,1)S(1)}, u32[]{:S(2)}, u32[]{:S(2)}) collective-permute-start(bf16[64,768]{1,0:T(8,128)(2,1)S(1)} %get-tuple-element.41.refs_0_.refs_12_), channel_id=1, source_target_pairs={{0,3},{1,2},{2,1},{3,0},{4,7},{5,6},{6,5},{7,4},{8,11},{9,10},{10,... | collective-permute-start | bytes 294920 | tf_op jit(solution)/shard_map/ppermute | solution.py:30
  19.3 1.9 %collective-permute-start.26 = (bf16[384,384]{1,0:T(8,128)(2,1)S(1)}, bf16[384,384]{1,0:T(8,128)(2,1)S(1)}, u32[]{:S(2)}, u32[]{:S(2)}) collective-permute-start(bf16[384,384]{1,0:T(8,128)(2,1)S(1)} %get-tuple-element.57), channel_id=1, source_target_pairs={{0,2},{1,3},{2,0},{3,1},{4,6},{5,7},{6,4},{7,5},{8,10},{9,11},{10,... | collective-permute-start | bytes 884744 | tf_op jit(solution)/shard_map/ppermute | solution.py:30
  21.2 3.0 %collective-permute-done.2.refs_3_ = bf16[64,768]{1,0:T(8,128)(2,1)S(1)} collective-permute-done((bf16[64,768]{1,0:T(8,128)(2,1)S(1)}, bf16[64,768]{1,0:T(8,128)(2,1)S(1)}, u32[]{:S(2)}, u32[]{:S(2)}) %collective-permute-start.2) | collective-permute-done | bytes 98336 | tf_op jit(solution)/shard_map/ppermute | solution.py:30
  24.2 1.5 %collective-permute-start.27 = (bf16[384,384]{1,0:T(8,128)(2,1)S(1)}, bf16[384,384]{1,0:T(8,128)(2,1)S(1)}, u32[]{:S(2)}, u32[]{:S(2)}) collective-permute-start(bf16[384,384]{1,0:T(8,128)(2,1)S(1)} %get-tuple-element.58), channel_id=1, source_target_pairs={{0,3},{1,2},{2,1},{3,0},{4,7},{5,6},{6,5},{7,4},{8,11},{9,10},{10,... | collective-permute-start | bytes 884744 | tf_op jit(solution)/shard_map/ppermute | solution.py:30
  26.4 1.7 %prep.1 = (bf16[2,1536,384]{2,1,0:T(8,128)(2,1)S(1)}, f32[3,2,3072]{2,1,0:T(2,128)S(1)}, f32[2,2,128]{2,1,0:T(2,128)S(1)}, f32[128,128]{1,0:T(8,128)S(1)}) custom-call(bf16[3,1536,384]{2,1,0:T(8,128)(2,1)} %bitcast.9, f32[3,2,3072]{2,1,0:T(2,128)} %bitcast.11, f32[2,2,128]{2,1,0:T(2,128)} %far_gain.1, s32[1]{0:T(128)S(6)} %copy.9.count_ref), custom_call_target="tpu_custom_call" | custom-call | tf_op jit(solution)/shard_map/prep/pallas_call | solution.py:291
  29.4 1.7 %collective-permute-start.15 = (bf16[64,768]{1,0:T(8,128)(2,1)S(1)}, bf16[64,768]{1,0:T(8,128)(2,1)S(1)}, u32[]{:S(2)}, u32[]{:S(2)}) collective-permute-start(bf16[64,768]{1,0:T(8,128)(2,1)S(1)} %get-tuple-element.50.refs_1_), channel_id=1, source_target_pairs={{0,4},{4,8},{8,12},{12,0},{1,5},{5,9},{9,13},{13,1},{2,6},{6,10},{... | collective-permute-start | bytes 294920 | tf_op jit(solution)/shard_map/ppermute | solution.py:26
  31.1 2.6 %collective-permute-start.17 = (bf16[64,768]{1,0:T(8,128)(2,1)S(1)}, bf16[64,768]{1,0:T(8,128)(2,1)S(1)}, u32[]{:S(2)}, u32[]{:S(2)}) collective-permute-start(bf16[64,768]{1,0:T(8,128)(2,1)S(1)} %get-tuple-element.50.refs_1_), channel_id=1, source_target_pairs={{0,8},{4,12},{8,0},{12,4},{1,9},{5,13},{9,1},{13,5},{2,10},{6,14},... | collective-permute-start | bytes 294920 | tf_op jit(solution)/shard_map/ppermute | solution.py:26
  35.9 3.6 %collective-permute-start.19 = (bf16[64,768]{1,0:T(8,128)(2,1)S(1)}, bf16[64,768]{1,0:T(8,128)(2,1)S(1)}, u32[]{:S(2)}, u32[]{:S(2)}) collective-permute-start(bf16[64,768]{1,0:T(8,128)(2,1)S(1)} %get-tuple-element.50.refs_1_), channel_id=1, source_target_pairs={{0,12},{4,0},{8,4},{12,8},{1,13},{5,1},{9,5},{13,9},{2,14},{6,2},{... | collective-permute-start | bytes 294920 | tf_op jit(solution)/shard_map/ppermute | solution.py:26
  39.9 1.8 %collective-permute-done.17.refs_3_ = bf16[64,768]{1,0:T(8,128)(2,1)S(1)} collective-permute-done((bf16[64,768]{1,0:T(8,128)(2,1)S(1)}, bf16[64,768]{1,0:T(8,128)(2,1)S(1)}, u32[]{:S(2)}, u32[]{:S(2)}) %collective-permute-start.17) | collective-permute-done | bytes 98336 | tf_op jit(solution)/shard_map/ppermute | solution.py:26
  42.5 3.1 %collective-permute-start.8 = (bf16[64,768]{1,0:T(8,128)(2,1)S(1)}, bf16[64,768]{1,0:T(8,128)(2,1)S(1)}, u32[]{:S(2)}, u32[]{:S(2)}) collective-permute-start(bf16[64,768]{1,0:T(8,128)(2,1)S(1)} %get-tuple-element.49.refs_5_), channel_id=1, source_target_pairs={{0,4},{4,8},{8,12},{12,0},{1,5},{5,9},{9,13},{13,1},{2,6},{6,10},{... | collective-permute-start | bytes 294920 | tf_op jit(solution)/shard_map/ppermute | solution.py:26
  45.6 3.7 %collective-permute-done.10.refs_7_ = bf16[64,768]{1,0:T(8,128)(2,1)S(1)} collective-permute-done((bf16[64,768]{1,0:T(8,128)(2,1)S(1)}, bf16[64,768]{1,0:T(8,128)(2,1)S(1)}, u32[]{:S(2)}, u32[]{:S(2)}) %collective-permute-start.10) | collective-permute-done | bytes 98336 | tf_op jit(solution)/shard_map/ppermute | solution.py:26
  57.4 8.7 %collective-permute-start.22 = (bf16[128,384]{1,0:T(8,128)(2,1)S(1)}, bf16[128,384]{1,0:T(8,128)(2,1)S(1)}, u32[]{:S(2)}, u32[]{:S(2)}) collective-permute-start(bf16[128,384]{1,0:T(8,128)(2,1)S(1)} %shard_map.87.refs_0_), channel_id=1, source_target_pairs={{0,2},{1,3},{2,0},{3,1},{4,6},{5,7},{6,4},{7,5},{8,10},{9,11},{10,... | collective-permute-start | bytes 294920 | tf_op jit(solution)/shard_map/ppermute | solution.py:30
  66.3 4.1 %collective-permute-done.22.refs_2_ = bf16[128,384]{1,0:T(8,128)(2,1)S(1)} collective-permute-done((bf16[128,384]{1,0:T(8,128)(2,1)S(1)}, bf16[128,384]{1,0:T(8,128)(2,1)S(1)}, u32[]{:S(2)}, u32[]{:S(2)}) %collective-permute-start.22) | collective-permute-done | bytes 98336 | tf_op jit(solution)/shard_map/ppermute | solution.py:30
  80.1 1.5 %collective-permute-start.33 = (bf16[64,768]{1,0:T(8,128)(2,1)S(1)}, bf16[64,768]{1,0:T(8,128)(2,1)S(1)}, u32[]{:S(2)}, u32[]{:S(2)}) collective-permute-start(bf16[64,768]{1,0:T(8,128)(2,1)S(1)} %get-tuple-element.60.refs_0_.refs_12_.refs_1_), channel_id=1, source_target_pairs={{0,3},{1,2},{2,1},{3,0},{4,7},{5,6},{6,5},{7,4},{8,11},{9,10},{10,... | collective-permute-start | bytes 294920 | tf_op jit(solution)/shard_map/ppermute | solution.py:30
  81.6 12.6 %collective-permute-done.32.refs_2_ = bf16[64,768]{1,0:T(8,128)(2,1)S(1)} collective-permute-done((bf16[64,768]{1,0:T(8,128)(2,1)S(1)}, bf16[64,768]{1,0:T(8,128)(2,1)S(1)}, u32[]{:S(2)}, u32[]{:S(2)}) %collective-permute-start.32) | collective-permute-done | bytes 98336 | tf_op jit(solution)/shard_map/ppermute | solution.py:30
  97.3 1.6 %collective-permute-done.36.refs_2_ = bf16[64,768]{1,0:T(8,128)(2,1)S(1)} collective-permute-done((bf16[64,768]{1,0:T(8,128)(2,1)S(1)}, bf16[64,768]{1,0:T(8,128)(2,1)S(1)}, u32[]{:S(2)}, u32[]{:S(2)}) %collective-permute-start.36) | collective-permute-done | bytes 98336 | tf_op jit(solution)/shard_map/ppermute | solution.py:30
  98.9 2.0 %collective-permute-done.37.refs_3_ = bf16[64,768]{1,0:T(8,128)(2,1)S(1)} collective-permute-done((bf16[64,768]{1,0:T(8,128)(2,1)S(1)}, bf16[64,768]{1,0:T(8,128)(2,1)S(1)}, u32[]{:S(2)}, u32[]{:S(2)}) %collective-permute-start.37) | collective-permute-done | bytes 98336 | tf_op jit(solution)/shard_map/ppermute | solution.py:30
  102.2 1.9 %collective-permute-start.50 = (bf16[64,768]{1,0:T(8,128)(2,1)S(1)}, bf16[64,768]{1,0:T(8,128)(2,1)S(1)}, u32[]{:S(2)}, u32[]{:S(2)}) collective-permute-start(bf16[64,768]{1,0:T(8,128)(2,1)S(1)} %get-tuple-element.65.refs_1_), channel_id=1, source_target_pairs={{0,12},{4,0},{8,4},{12,8},{1,13},{5,1},{9,5},{13,9},{2,14},{6,2},{... | collective-permute-start | bytes 294920 | tf_op jit(solution)/shard_map/ppermute | solution.py:26
  104.7 2.5 %collective-permute-start.41 = (bf16[64,768]{1,0:T(8,128)(2,1)S(1)}, bf16[64,768]{1,0:T(8,128)(2,1)S(1)}, u32[]{:S(2)}, u32[]{:S(2)}) collective-permute-start(bf16[64,768]{1,0:T(8,128)(2,1)S(1)} %get-tuple-element.64.refs_5_), channel_id=1, source_target_pairs={{0,8},{4,12},{8,0},{12,4},{1,9},{5,13},{9,1},{13,5},{2,10},{6,14},... | collective-permute-start | bytes 294920 | tf_op jit(solution)/shard_map/ppermute | solution.py:26
  107.2 1.8 %collective-permute-start.43 = (bf16[64,768]{1,0:T(8,128)(2,1)S(1)}, bf16[64,768]{1,0:T(8,128)(2,1)S(1)}, u32[]{:S(2)}, u32[]{:S(2)}) collective-permute-start(bf16[64,768]{1,0:T(8,128)(2,1)S(1)} %get-tuple-element.64.refs_5_), channel_id=1, source_target_pairs={{0,12},{4,0},{8,4},{12,8},{1,13},{5,1},{9,5},{13,9},{2,14},{6,2},{... | collective-permute-start | bytes 294920 | tf_op jit(solution)/shard_map/ppermute | solution.py:26
  111.5 3.6 %collective-permute-done.41.refs_7_ = bf16[64,768]{1,0:T(8,128)(2,1)S(1)} collective-permute-done((bf16[64,768]{1,0:T(8,128)(2,1)S(1)}, bf16[64,768]{1,0:T(8,128)(2,1)S(1)}, u32[]{:S(2)}, u32[]{:S(2)}) %collective-permute-start.41) | collective-permute-done | bytes 98336 | tf_op jit(solution)/shard_map/ppermute | solution.py:26
  120.8 1.5 %collective-permute-start.53 = (bf16[128,384]{1,0:T(8,128)(2,1)S(1)}, bf16[128,384]{1,0:T(8,128)(2,1)S(1)}, u32[]{:S(2)}, u32[]{:S(2)}) collective-permute-start(bf16[128,384]{1,0:T(8,128)(2,1)S(1)} %shard_map.95.refs_0_), channel_id=1, source_target_pairs={{0,2},{1,3},{2,0},{3,1},{4,6},{5,7},{6,4},{7,5},{8,10},{9,11},{10,... | collective-permute-start | bytes 294920 | tf_op jit(solution)/shard_map/ppermute | solution.py:30
  122.3 1.5 %collective-permute-start.54 = (bf16[128,384]{1,0:T(8,128)(2,1)S(1)}, bf16[128,384]{1,0:T(8,128)(2,1)S(1)}, u32[]{:S(2)}, u32[]{:S(2)}) collective-permute-start(bf16[128,384]{1,0:T(8,128)(2,1)S(1)} %shard_map.95.refs_0_), channel_id=1, source_target_pairs={{0,3},{1,2},{2,1},{3,0},{4,7},{5,6},{6,5},{7,4},{8,11},{9,10},{10,... | collective-permute-start | bytes 294920 | tf_op jit(solution)/shard_map/ppermute | solution.py:30
  123.8 2.2 %collective-permute-done.52.refs_1_ = bf16[128,384]{1,0:T(8,128)(2,1)S(1)} collective-permute-done((bf16[128,384]{1,0:T(8,128)(2,1)S(1)}, bf16[128,384]{1,0:T(8,128)(2,1)S(1)}, u32[]{:S(2)}, u32[]{:S(2)}) %collective-permute-start.52) | collective-permute-done | bytes 98336 | tf_op jit(solution)/shard_map/ppermute | solution.py:30
  126.0 1.8 %collective-permute-done.54.refs_3_ = bf16[128,384]{1,0:T(8,128)(2,1)S(1)} collective-permute-done((bf16[128,384]{1,0:T(8,128)(2,1)S(1)}, bf16[128,384]{1,0:T(8,128)(2,1)S(1)}, u32[]{:S(2)}, u32[]{:S(2)}) %collective-permute-start.54) | collective-permute-done | bytes 98336 | tf_op jit(solution)/shard_map/ppermute | solution.py:30
  128.6 1.4 %collective-permute-done.62.refs_3_ = bf16[128,768]{1,0:T(8,128)(2,1)S(1)} collective-permute-done((bf16[128,768]{1,0:T(8,128)(2,1)S(1)}, bf16[128,768]{1,0:T(8,128)(2,1)S(1)}, u32[]{:S(2)}, u32[]{:S(2)}) %collective-permute-start.62) | collective-permute-done | bytes 196640 | tf_op jit(solution)/shard_map/ppermute | solution.py:34
  (121 shorter events, 41.2 us)
Async XLA Ops:
  0.0 25.7 %collective-permute-start.3 = (bf16[3,1536,384]{2,1,0:T(8,128)(2,1)}, bf16[3,1536,384]{2,1,0:T(8,128)(2,1)S(1)}, u32[]{:S(2)}, u32[]{:S(2)}) collective-permute-start(bf16[3,1536,384]{2,1,0:T(8,128)(2,1)} %bitcast.8), channel_id=1, source_target_pairs={{0,16},{16,0},{1,17},{17,1},{2,18},{18,2},{3,19},{19,3},{4,20},{20... | collective-permute-start | bytes 10616840 | tf_op jit(solution)/shard_map/ppermute | solution.py:34
  0.5 76.2 %collective-permute-start.34 = (bf16[3,1536,384]{2,1,0:T(8,128)(2,1)}, bf16[3,1536,384]{2,1,0:T(8,128)(2,1)S(1)}, u32[]{:S(2)}, u32[]{:S(2)}) collective-permute-start(bf16[3,1536,384]{2,1,0:T(8,128)(2,1)} %bitcast.4), channel_id=1, source_target_pairs={{0,16},{16,0},{1,17},{17,1},{2,18},{18,2},{3,19},{19,3},{4,20},{20... | collective-permute-start | bytes 10616840 | tf_op jit(solution)/shard_map/ppermute | solution.py:34
  0.5 12.8 %collective-permute-start.24 = (bf16[384,1536]{1,0:T(8,128)(2,1)}, bf16[384,1536]{1,0:T(8,128)(2,1)S(1)}, u32[]{:S(2)}, u32[]{:S(2)}) collective-permute-start(bf16[384,1536]{1,0:T(8,128)(2,1)} %near_ref.2), channel_id=1, source_target_pairs={{0,16},{16,0},{1,17},{17,1},{2,18},{18,2},{3,19},{19,3},{4,20},{20... | collective-permute-start | bytes 3538952 | tf_op jit(solution)/shard_map/ppermute | solution.py:34
  8.0 9.7 %collective-permute-start.6 = (bf16[64,768]{1,0:T(8,128)(2,1)S(1)}, bf16[64,768]{1,0:T(8,128)(2,1)S(1)}, u32[]{:S(2)}, u32[]{:S(2)}) collective-permute-start(bf16[64,768]{1,0:T(8,128)(2,1)S(1)} %get-tuple-element.47.refs_0_.refs_13_), channel_id=1, source_target_pairs={{0,3},{1,2},{2,1},{3,0},{4,7},{5,6},{6,5},{7,4},{8,11},{9,10},{10,... | collective-permute-start | bytes 294920 | tf_op jit(solution)/shard_map/ppermute | solution.py:30
  10.7 8.5 %collective-permute-start = (bf16[64,768]{1,0:T(8,128)(2,1)S(1)}, bf16[64,768]{1,0:T(8,128)(2,1)S(1)}, u32[]{:S(2)}, u32[]{:S(2)}) collective-permute-start(bf16[64,768]{1,0:T(8,128)(2,1)S(1)} %get-tuple-element.41.refs_0_.refs_12_), channel_id=1, source_target_pairs={{0,1},{1,0},{2,3},{3,2},{4,5},{5,4},{6,7},{7,6},{8,9},{9,8},{10,11... | collective-permute-start | bytes 294920 | tf_op jit(solution)/shard_map/ppermute | solution.py:30
  19.1 10.3 %collective-permute-start.25 = (bf16[384,384]{1,0:T(8,128)(2,1)S(1)}, bf16[384,384]{1,0:T(8,128)(2,1)S(1)}, u32[]{:S(2)}, u32[]{:S(2)}) collective-permute-start(bf16[384,384]{1,0:T(8,128)(2,1)S(1)} %get-tuple-element.56), channel_id=1, source_target_pairs={{0,1},{1,0},{2,3},{3,2},{4,5},{5,4},{6,7},{7,6},{8,9},{9,8},{10,11... | collective-permute-start | bytes 884744 | tf_op jit(solution)/shard_map/ppermute | solution.py:30
  19.3 11.8 %collective-permute-start.26 = (bf16[384,384]{1,0:T(8,128)(2,1)S(1)}, bf16[384,384]{1,0:T(8,128)(2,1)S(1)}, u32[]{:S(2)}, u32[]{:S(2)}) collective-permute-start(bf16[384,384]{1,0:T(8,128)(2,1)S(1)} %get-tuple-element.57), channel_id=1, source_target_pairs={{0,2},{1,3},{2,0},{3,1},{4,6},{5,7},{6,4},{7,5},{8,10},{9,11},{10,... | collective-permute-start | bytes 884744 | tf_op jit(solution)/shard_map/ppermute | solution.py:30
  24.2 11.7 %collective-permute-start.27 = (bf16[384,384]{1,0:T(8,128)(2,1)S(1)}, bf16[384,384]{1,0:T(8,128)(2,1)S(1)}, u32[]{:S(2)}, u32[]{:S(2)}) collective-permute-start(bf16[384,384]{1,0:T(8,128)(2,1)S(1)} %get-tuple-element.58), channel_id=1, source_target_pairs={{0,3},{1,2},{2,1},{3,0},{4,7},{5,6},{6,5},{7,4},{8,11},{9,10},{10,... | collective-permute-start | bytes 884744 | tf_op jit(solution)/shard_map/ppermute | solution.py:30
  25.7 48.6 %collective-permute-start.55 = (bf16[384,1536]{1,0:T(8,128)(2,1)S(1)}, bf16[384,1536]{1,0:T(8,128)(2,1)S(1)}, u32[]{:S(2)}, u32[]{:S(2)}) collective-permute-start(bf16[384,1536]{1,0:T(8,128)(2,1)S(1)} %copy-done.3), channel_id=1, source_target_pairs={{0,16},{16,0},{1,17},{17,1},{2,18},{18,2},{3,19},{19,3},{4,20},{20... | collective-permute-start | bytes 3538952 | tf_op jit(solution)/shard_map/ppermute | solution.py:34
  29.4 10.0 %collective-permute-start.15 = (bf16[64,768]{1,0:T(8,128)(2,1)S(1)}, bf16[64,768]{1,0:T(8,128)(2,1)S(1)}, u32[]{:S(2)}, u32[]{:S(2)}) collective-permute-start(bf16[64,768]{1,0:T(8,128)(2,1)S(1)} %get-tuple-element.50.refs_1_), channel_id=1, source_target_pairs={{0,4},{4,8},{8,12},{12,0},{1,5},{5,9},{9,13},{13,1},{2,6},{6,10},{... | collective-permute-start | bytes 294920 | tf_op jit(solution)/shard_map/ppermute | solution.py:26
  31.1 10.6 %collective-permute-start.17 = (bf16[64,768]{1,0:T(8,128)(2,1)S(1)}, bf16[64,768]{1,0:T(8,128)(2,1)S(1)}, u32[]{:S(2)}, u32[]{:S(2)}) collective-permute-start(bf16[64,768]{1,0:T(8,128)(2,1)S(1)} %get-tuple-element.50.refs_1_), channel_id=1, source_target_pairs={{0,8},{4,12},{8,0},{12,4},{1,9},{5,13},{9,1},{13,5},{2,10},{6,14},... | collective-permute-start | bytes 294920 | tf_op jit(solution)/shard_map/ppermute | solution.py:26
  39.5 9.8 %collective-permute-start.10 = (bf16[64,768]{1,0:T(8,128)(2,1)S(1)}, bf16[64,768]{1,0:T(8,128)(2,1)S(1)}, u32[]{:S(2)}, u32[]{:S(2)}) collective-permute-start(bf16[64,768]{1,0:T(8,128)(2,1)S(1)} %get-tuple-element.49.refs_5_), channel_id=1, source_target_pairs={{0,8},{4,12},{8,0},{12,4},{1,9},{5,13},{9,1},{13,5},{2,10},{6,14},... | collective-permute-start | bytes 294920 | tf_op jit(solution)/shard_map/ppermute | solution.py:26
  41.7 8.5 %collective-permute-start.12 = (bf16[64,768]{1,0:T(8,128)(2,1)S(1)}, bf16[64,768]{1,0:T(8,128)(2,1)S(1)}, u32[]{:S(2)}, u32[]{:S(2)}) collective-permute-start(bf16[64,768]{1,0:T(8,128)(2,1)S(1)} %get-tuple-element.49.refs_5_), channel_id=1, source_target_pairs={{0,12},{4,0},{8,4},{12,8},{1,13},{5,1},{9,5},{13,9},{2,14},{6,2},{... | collective-permute-start | bytes 294920 | tf_op jit(solution)/shard_map/ppermute | solution.py:26
  42.5 7.8 %collective-permute-start.8 = (bf16[64,768]{1,0:T(8,128)(2,1)S(1)}, bf16[64,768]{1,0:T(8,128)(2,1)S(1)}, u32[]{:S(2)}, u32[]{:S(2)}) collective-permute-start(bf16[64,768]{1,0:T(8,128)(2,1)S(1)} %get-tuple-element.49.refs_5_), channel_id=1, source_target_pairs={{0,4},{4,8},{8,12},{12,0},{1,5},{5,9},{9,13},{13,1},{2,6},{6,10},{... | collective-permute-start | bytes 294920 | tf_op jit(solution)/shard_map/ppermute | solution.py:26
  54.1 11.9 %collective-permute-start.30 = (bf16[384,384]{1,0:T(8,128)(2,1)S(1)}, bf16[384,384]{1,0:T(8,128)(2,1)S(1)}, u32[]{:S(2)}, u32[]{:S(2)}) collective-permute-start(bf16[384,384]{1,0:T(8,128)(2,1)S(1)} %collective-permute-done.27.refs_7_), channel_id=1, source_target_pairs={{0,16},{16,0},{1,17},{17,1},{2,18},{18,2},{3,19},{19,3},{4,20},{20... | collective-permute-start | bytes 884744 | tf_op jit(solution)/shard_map/ppermute | solution.py:34
  57.1 9.1 %collective-permute-start.21 = (bf16[128,384]{1,0:T(8,128)(2,1)S(1)}, bf16[128,384]{1,0:T(8,128)(2,1)S(1)}, u32[]{:S(2)}, u32[]{:S(2)}) collective-permute-start(bf16[128,384]{1,0:T(8,128)(2,1)S(1)} %shard_map.87.refs_0_), channel_id=1, source_target_pairs={{0,1},{1,0},{2,3},{3,2},{4,5},{5,4},{6,7},{7,6},{8,9},{9,8},{10,11... | collective-permute-start | bytes 294920 | tf_op jit(solution)/shard_map/ppermute | solution.py:30
  57.4 13.1 %collective-permute-start.22 = (bf16[128,384]{1,0:T(8,128)(2,1)S(1)}, bf16[128,384]{1,0:T(8,128)(2,1)S(1)}, u32[]{:S(2)}, u32[]{:S(2)}) collective-permute-start(bf16[128,384]{1,0:T(8,128)(2,1)S(1)} %shard_map.87.refs_0_), channel_id=1, source_target_pairs={{0,2},{1,3},{2,0},{3,1},{4,6},{5,7},{6,4},{7,5},{8,10},{9,11},{10,... | collective-permute-start | bytes 294920 | tf_op jit(solution)/shard_map/ppermute | solution.py:30
  73.4 6.7 %collective-permute-start.31 = (bf16[64,768]{1,0:T(8,128)(2,1)S(1)}, bf16[64,768]{1,0:T(8,128)(2,1)S(1)}, u32[]{:S(2)}, u32[]{:S(2)}) collective-permute-start(bf16[64,768]{1,0:T(8,128)(2,1)S(1)} %get-tuple-element.60.refs_0_.refs_12_.refs_1_), channel_id=1, source_target_pairs={{0,1},{1,0},{2,3},{3,2},{4,5},{5,4},{6,7},{7,6},{8,9},{9,8},{10,11... | collective-permute-start | bytes 294920 | tf_op jit(solution)/shard_map/ppermute | solution.py:30
  74.5 27.7 %collective-permute-start.56 = (bf16[384,384]{1,0:T(8,128)(2,1)S(1)}, bf16[384,384]{1,0:T(8,128)(2,1)S(1)}, u32[]{:S(2)}, u32[]{:S(2)}) collective-permute-start(bf16[384,384]{1,0:T(8,128)(2,1)S(1)} %get-tuple-element.71), channel_id=1, source_target_pairs={{0,1},{1,0},{2,3},{3,2},{4,5},{5,4},{6,7},{7,6},{8,9},{9,8},{10,11... | collective-permute-start | bytes 884744 | tf_op jit(solution)/shard_map/ppermute | solution.py:30
  75.7 28.4 %collective-permute-start.57 = (bf16[384,384]{1,0:T(8,128)(2,1)S(1)}, bf16[384,384]{1,0:T(8,128)(2,1)S(1)}, u32[]{:S(2)}, u32[]{:S(2)}) collective-permute-start(bf16[384,384]{1,0:T(8,128)(2,1)S(1)} %get-tuple-element.72), channel_id=1, source_target_pairs={{0,2},{1,3},{2,0},{3,1},{4,6},{5,7},{6,4},{7,5},{8,10},{9,11},{10,... | collective-permute-start | bytes 884744 | tf_op jit(solution)/shard_map/ppermute | solution.py:30
  76.7 28.0 %collective-permute-start.58 = (bf16[384,384]{1,0:T(8,128)(2,1)S(1)}, bf16[384,384]{1,0:T(8,128)(2,1)S(1)}, u32[]{:S(2)}, u32[]{:S(2)}) collective-permute-start(bf16[384,384]{1,0:T(8,128)(2,1)S(1)} %get-tuple-element.73), channel_id=1, source_target_pairs={{0,3},{1,2},{2,1},{3,0},{4,7},{5,6},{6,5},{7,4},{8,11},{9,10},{10,... | collective-permute-start | bytes 884744 | tf_op jit(solution)/shard_map/ppermute | solution.py:30
  78.1 16.2 %collective-permute-start.32 = (bf16[64,768]{1,0:T(8,128)(2,1)S(1)}, bf16[64,768]{1,0:T(8,128)(2,1)S(1)}, u32[]{:S(2)}, u32[]{:S(2)}) collective-permute-start(bf16[64,768]{1,0:T(8,128)(2,1)S(1)} %get-tuple-element.60.refs_0_.refs_12_.refs_1_), channel_id=1, source_target_pairs={{0,2},{1,3},{2,0},{3,1},{4,6},{5,7},{6,4},{7,5},{8,10},{9,11},{10,... | collective-permute-start | bytes 294920 | tf_op jit(solution)/shard_map/ppermute | solution.py:30
  80.1 15.3 %collective-permute-start.33 = (bf16[64,768]{1,0:T(8,128)(2,1)S(1)}, bf16[64,768]{1,0:T(8,128)(2,1)S(1)}, u32[]{:S(2)}, u32[]{:S(2)}) collective-permute-start(bf16[64,768]{1,0:T(8,128)(2,1)S(1)} %get-tuple-element.60.refs_0_.refs_12_.refs_1_), channel_id=1, source_target_pairs={{0,3},{1,2},{2,1},{3,0},{4,7},{5,6},{6,5},{7,4},{8,11},{9,10},{10,... | collective-permute-start | bytes 294920 | tf_op jit(solution)/shard_map/ppermute | solution.py:30
  98.9 8.3 %collective-permute-start.46 = (bf16[64,768]{1,0:T(8,128)(2,1)S(1)}, bf16[64,768]{1,0:T(8,128)(2,1)S(1)}, u32[]{:S(2)}, u32[]{:S(2)}) collective-permute-start(bf16[64,768]{1,0:T(8,128)(2,1)S(1)} %get-tuple-element.65.refs_1_), channel_id=1, source_target_pairs={{0,4},{4,8},{8,12},{12,0},{1,5},{5,9},{9,13},{13,1},{2,6},{6,10},{... | collective-permute-start | bytes 294920 | tf_op jit(solution)/shard_map/ppermute | solution.py:26
  100.9 9.4 %collective-permute-start.48 = (bf16[64,768]{1,0:T(8,128)(2,1)S(1)}, bf16[64,768]{1,0:T(8,128)(2,1)S(1)}, u32[]{:S(2)}, u32[]{:S(2)}) collective-permute-start(bf16[64,768]{1,0:T(8,128)(2,1)S(1)} %get-tuple-element.65.refs_1_), channel_id=1, source_target_pairs={{0,8},{4,12},{8,0},{12,4},{1,9},{5,13},{9,1},{13,5},{2,10},{6,14},... | collective-permute-start | bytes 294920 | tf_op jit(solution)/shard_map/ppermute | solution.py:26
  102.2 8.2 %collective-permute-start.50 = (bf16[64,768]{1,0:T(8,128)(2,1)S(1)}, bf16[64,768]{1,0:T(8,128)(2,1)S(1)}, u32[]{:S(2)}, u32[]{:S(2)}) collective-permute-start(bf16[64,768]{1,0:T(8,128)(2,1)S(1)} %get-tuple-element.65.refs_1_), channel_id=1, source_target_pairs={{0,12},{4,0},{8,4},{12,8},{1,13},{5,1},{9,5},{13,9},{2,14},{6,2},{... | collective-permute-start | bytes 294920 | tf_op jit(solution)/shard_map/ppermute | solution.py:26
  104.1 7.4 %collective-permute-start.39 = (bf16[64,768]{1,0:T(8,128)(2,1)S(1)}, bf16[64,768]{1,0:T(8,128)(2,1)S(1)}, u32[]{:S(2)}, u32[]{:S(2)}) collective-permute-start(bf16[64,768]{1,0:T(8,128)(2,1)S(1)} %get-tuple-element.64.refs_5_), channel_id=1, source_target_pairs={{0,4},{4,8},{8,12},{12,0},{1,5},{5,9},{9,13},{13,1},{2,6},{6,10},{... | collective-permute-start | bytes 294920 | tf_op jit(solution)/shard_map/ppermute | solution.py:26
  104.7 10.4 %collective-permute-start.41 = (bf16[64,768]{1,0:T(8,128)(2,1)S(1)}, bf16[64,768]{1,0:T(8,128)(2,1)S(1)}, u32[]{:S(2)}, u32[]{:S(2)}) collective-permute-start(bf16[64,768]{1,0:T(8,128)(2,1)S(1)} %get-tuple-element.64.refs_5_), channel_id=1, source_target_pairs={{0,8},{4,12},{8,0},{12,4},{1,9},{5,13},{9,1},{13,5},{2,10},{6,14},... | collective-permute-start | bytes 294920 | tf_op jit(solution)/shard_map/ppermute | solution.py:26
  107.2 7.9 %collective-permute-start.43 = (bf16[64,768]{1,0:T(8,128)(2,1)S(1)}, bf16[64,768]{1,0:T(8,128)(2,1)S(1)}, u32[]{:S(2)}, u32[]{:S(2)}) collective-permute-start(bf16[64,768]{1,0:T(8,128)(2,1)S(1)} %get-tuple-element.64.refs_5_), channel_id=1, source_target_pairs={{0,12},{4,0},{8,4},{12,8},{1,13},{5,1},{9,5},{13,9},{2,14},{6,2},{... | collective-permute-start | bytes 294920 | tf_op jit(solution)/shard_map/ppermute | solution.py:26
  115.1 7.2 %collective-permute-start.59 = (bf16[384,384]{1,0:T(8,128)(2,1)S(1)}, bf16[384,384]{1,0:T(8,128)(2,1)S(1)}, u32[]{:S(2)}, u32[]{:S(2)}) collective-permute-start(bf16[384,384]{1,0:T(8,128)(2,1)S(1)} %collective-permute-done.56.refs_5_), channel_id=1, source_target_pairs={{0,16},{16,0},{1,17},{17,1},{2,18},{18,2},{3,19},{19,3},{4,20},{20... | collective-permute-start | bytes 884744 | tf_op jit(solution)/shard_map/ppermute | solution.py:34
  116.1 7.7 %collective-permute-start.60 = (bf16[384,384]{1,0:T(8,128)(2,1)S(1)}, bf16[384,384]{1,0:T(8,128)(2,1)S(1)}, u32[]{:S(2)}, u32[]{:S(2)}) collective-permute-start(bf16[384,384]{1,0:T(8,128)(2,1)S(1)} %collective-permute-done.57.refs_6_), channel_id=1, source_target_pairs={{0,16},{16,0},{1,17},{17,1},{2,18},{18,2},{3,19},{19,3},{4,20},{20... | collective-permute-start | bytes 884744 | tf_op jit(solution)/shard_map/ppermute | solution.py:34
  116.4 7.4 %collective-permute-start.61 = (bf16[384,384]{1,0:T(8,128)(2,1)S(1)}, bf16[384,384]{1,0:T(8,128)(2,1)S(1)}, u32[]{:S(2)}, u32[]{:S(2)}) collective-permute-start(bf16[384,384]{1,0:T(8,128)(2,1)S(1)} %collective-permute-done.58.refs_7_), channel_id=1, source_target_pairs={{0,16},{16,0},{1,17},{17,1},{2,18},{18,2},{3,19},{19,3},{4,20},{20... | collective-permute-start | bytes 884744 | tf_op jit(solution)/shard_map/ppermute | solution.py:34
  (35 other events, 172.9 us)

commit v6 on v5

--- a/solution.py
+++ b/solution.py
@@ -70,10 +70,19 @@
 
 
 def prep_kernel(far_qkv, far_mod, far_gain, count_ref, qkv_ref, mod_ref, gain_ref, mark_ref, sems):
+    depth = qkv_ref.shape[1] // 4
     copies = [
-        pltpu.make_async_copy(far_qkv.at[pl.ds(1, 2)], qkv_ref, sems.at[0]),
-        pltpu.make_async_copy(far_mod, mod_ref, sems.at[1]),
-        pltpu.make_async_copy(far_gain, gain_ref, sems.at[2]),
+        pltpu.make_async_copy(
+            far_qkv.at[i + 1, pl.ds(j * depth, depth)],
+            qkv_ref.at[i, pl.ds(j * depth, depth)],
+            sems.at[i * 4 + j],
+        )
+        for i in range(2)
+        for j in range(4)
+    ]
+    copies += [
+        pltpu.make_async_copy(far_mod, mod_ref, sems.at[8]),
+        pltpu.make_async_copy(far_gain, gain_ref, sems.at[9]),
     ]
     for copy in copies:
         copy.start()
@@ -105,15 +114,15 @@
             piece[...] = across_ref[:, at]
 
 
-def contract(moded_ref, own_ref, other_ref, which, first, n_head):
+def contract(moded, own_ref, other_ref, which, first, n_head):
     b = lax.axis_index("branch")
     h = lax.axis_index("head")
-    quarter = moded_ref.shape[2]
+    quarter = moded[0].shape[2]
     per_core = n_head // 2
     total = None
     for ref, core, at in ((own_ref, b, which - first), (other_ref, 1 - b, which)):
         for i in range(per_core):
-            piece = moded_ref[(core * per_core + i) ^ h]
+            piece = jnp.concatenate([m[(core * per_core + i) ^ h] for m in moded], axis=0)
             term = jnp.dot(
                 piece,
                 ref[at, i * quarter : (i + 1) * quarter, :],
@@ -154,21 +163,19 @@
         gain = mod_ref[1, blk : blk + 1, at] + 1.0
         normed = (x[...].astype(F32) - mean) * scale
         moded_ref[k] = (normed * gain + shift).astype(BF16)
-    key = contract(moded_ref, own_ref, other_ref, 1, first, n_head)
+    key = contract([moded_ref], own_ref, other_ref, 1, first, n_head)
     for i, out in enumerate(norm_heads(key, gain_ref[blk, 1:2, :], width)):
         packed_ref[:, i * HEAD_DIM : (i + 1) * HEAD_DIM] = jnp.where(padding, MARK, out).astype(BF16)
-    packed_ref[:, width:] = contract(moded_ref, own_ref, other_ref, 2, first, n_head).astype(BF16)
+    packed_ref[:, width:] = contract([moded_ref], own_ref, other_ref, 2, first, n_head).astype(BF16)
 
 
 def q_kernel(blk, n_head, chunks, *refs):
     moded = refs[:chunks]
     own_ref, other_ref, gain_ref, query_ref = refs[chunks:]
     width = own_ref.shape[2]
-    rows = moded[0].shape[1]
-    for c, moded_ref in enumerate(moded):
-        query = contract(moded_ref, own_ref, other_ref, 0, 0, n_head)
-        for i, out in enumerate(norm_heads(query, gain_ref[blk, 0:1, :], width)):
-            query_ref[c * rows : (c + 1) * rows, i * HEAD_DIM : (i + 1) * HEAD_DIM] = out.astype(BF16)
+    query = contract(moded, own_ref, other_ref, 0, 0, n_head)
+    for i, out in enumerate(norm_heads(query, gain_ref[blk, 0:1, :], width)):
+        query_ref[:, i * HEAD_DIM : (i + 1) * HEAD_DIM] = out.astype(BF16)
 
 
 def step_kernel(n, opens, closes, *refs):
@@ -293,7 +300,7 @@
             out_shape=shape,
             in_specs=[FAR] * 3 + [SMEM],
             out_specs=[VMEM] * 4,
-            scratch_shapes=[pltpu.SemaphoreType.DMA((3,))],
+            scratch_shapes=[pltpu.SemaphoreType.DMA((10,))],
             compiler_params=params(16),
             name="prep",
         )(far(qkv), far(mod), far(gains), valid)

time: 131 us -> 130 us (level)
  no operation moved by 1% of the time
where the time goes in v6:
time: 130 us
  starting transfers between devices  62.7 us (48%)
  waiting for transfers between devices  50 us (38%)
  Pallas kernels  15.4 us (12%)
    ppermute x24, starting transfers between devices, cross(): return lax.ppermute(x, axis, [(i, i ^ k) for i in range(n)])  38.2 us
    ppermute x24, waiting for transfers between devices, cross(): return lax.ppermute(x, axis, [(i, i ^ k) for i in range(n)])  32 us
    ppermute x12, starting transfers between devices, turn(): return lax.ppermute(x, axis, [(i, (i + k) % n) for i in range(n)])  19 us
    ppermute x12, waiting for transfers between devices, turn(): return lax.ppermute(x, axis, [(i, (i + k) % n) for i in range(n)])  12 us
    ppermute x27, waiting for transfers between devices, swap(): return lax.ppermute(x, 'branch', [(0, 1), (1, 0)])  6.05 us
    ppermute x27, starting transfers between devices, swap(): return lax.ppermute(x, 'branch', [(0, 1), (1, 0)])  5.5 us
    pallas_call x4, Pallas kernels, block(): pl.pallas_call(functools.partial(kv_kernel, blk, c, n_head), out_shape=(S...  5.22 us
    pallas_call x6, Pallas kernels, block(): pl.pallas_call(functools.partial(step_kernel, len(group), i == 0, closes)...  3.68 us
  transfers between devices with their start and end apart: 63, of which 24 were waited for; matrix products, arithmetic and copies ran while one was open for 0% of the time, Pallas kernels for 11%

profile of v6, /device:TPU:0, one launch (start us, length us, event | category | flops | bytes accessed | tf_op | source)
XLA Modules:
  0.0 130.2 jit_solution(15656612695050075650)
XLA Ops:
  2.0 2.5 %collective-permute-start.4 = (bf16[64,768]{1,0:T(8,128)(2,1)S(1)}, bf16[64,768]{1,0:T(8,128)(2,1)S(1)}, u32[]{:S(2)}, u32[]{:S(2)}) collective-permute-start(bf16[64,768]{1,0:T(8,128)(2,1)S(1)} %get-tuple-element.47.refs_0_.refs_13_), channel_id=1, source_target_pairs={{0,1},{1,0},{2,3},{3,2},{4,5},{5,4},{6,7},{7,6},{8,9},{9,8},{10,11... | collective-permute-start | bytes 294920 | tf_op jit(solution)/shard_map/ppermute | solution.py:30
  4.5 1.5 %collective-permute-start.5 = (bf16[64,768]{1,0:T(8,128)(2,1)S(1)}, bf16[64,768]{1,0:T(8,128)(2,1)S(1)}, u32[]{:S(2)}, u32[]{:S(2)}) collective-permute-start(bf16[64,768]{1,0:T(8,128)(2,1)S(1)} %get-tuple-element.47.refs_0_.refs_13_), channel_id=1, source_target_pairs={{0,2},{1,3},{2,0},{3,1},{4,6},{5,7},{6,4},{7,5},{8,10},{9,11},{10,... | collective-permute-start | bytes 294920 | tf_op jit(solution)/shard_map/ppermute | solution.py:30
  6.0 1.9 %collective-permute-done.4.refs_1_ = bf16[64,768]{1,0:T(8,128)(2,1)S(1)} collective-permute-done((bf16[64,768]{1,0:T(8,128)(2,1)S(1)}, bf16[64,768]{1,0:T(8,128)(2,1)S(1)}, u32[]{:S(2)}, u32[]{:S(2)}) %collective-permute-start.4) | collective-permute-done | bytes 98336 | tf_op jit(solution)/shard_map/ppermute | solution.py:30
  8.0 2.7 %collective-permute-start.6 = (bf16[64,768]{1,0:T(8,128)(2,1)S(1)}, bf16[64,768]{1,0:T(8,128)(2,1)S(1)}, u32[]{:S(2)}, u32[]{:S(2)}) collective-permute-start(bf16[64,768]{1,0:T(8,128)(2,1)S(1)} %get-tuple-element.47.refs_0_.refs_13_), channel_id=1, source_target_pairs={{0,3},{1,2},{2,1},{3,0},{4,7},{5,6},{6,5},{7,4},{8,11},{9,10},{10,... | collective-permute-start | bytes 294920 | tf_op jit(solution)/shard_map/ppermute | solution.py:30
  11.2 2.1 %collective-permute-done.24.across_ref = bf16[384,1536]{1,0:T(8,128)(2,1)S(1)} collective-permute-done((bf16[384,1536]{1,0:T(8,128)(2,1)}, bf16[384,1536]{1,0:T(8,128)(2,1)S(1)}, u32[]{:S(2)}, u32[]{:S(2)}) %collective-permute-start.24) | collective-permute-done | bytes 1179680 | tf_op jit(solution)/shard_map/ppermute | solution.py:34
  13.3 2.9 %collective-permute-start.1 = (bf16[64,768]{1,0:T(8,128)(2,1)S(1)}, bf16[64,768]{1,0:T(8,128)(2,1)S(1)}, u32[]{:S(2)}, u32[]{:S(2)}) collective-permute-start(bf16[64,768]{1,0:T(8,128)(2,1)S(1)} %get-tuple-element.41.refs_0_.refs_12_), channel_id=1, source_target_pairs={{0,2},{1,3},{2,0},{3,1},{4,6},{5,7},{6,4},{7,5},{8,10},{9,11},{10,... | collective-permute-start | bytes 294920 | tf_op jit(solution)/shard_map/ppermute | solution.py:30
  17.6 1.5 %collective-permute-start.2 = (bf16[64,768]{1,0:T(8,128)(2,1)S(1)}, bf16[64,768]{1,0:T(8,128)(2,1)S(1)}, u32[]{:S(2)}, u32[]{:S(2)}) collective-permute-start(bf16[64,768]{1,0:T(8,128)(2,1)S(1)} %get-tuple-element.41.refs_0_.refs_12_), channel_id=1, source_target_pairs={{0,3},{1,2},{2,1},{3,0},{4,7},{5,6},{6,5},{7,4},{8,11},{9,10},{10,... | collective-permute-start | bytes 294920 | tf_op jit(solution)/shard_map/ppermute | solution.py:30
  19.3 1.9 %collective-permute-start.26 = (bf16[384,384]{1,0:T(8,128)(2,1)S(1)}, bf16[384,384]{1,0:T(8,128)(2,1)S(1)}, u32[]{:S(2)}, u32[]{:S(2)}) collective-permute-start(bf16[384,384]{1,0:T(8,128)(2,1)S(1)} %get-tuple-element.57), channel_id=1, source_target_pairs={{0,2},{1,3},{2,0},{3,1},{4,6},{5,7},{6,4},{7,5},{8,10},{9,11},{10,... | collective-permute-start | bytes 884744 | tf_op jit(solution)/shard_map/ppermute | solution.py:30
  21.2 3.0 %collective-permute-done.2.refs_3_ = bf16[64,768]{1,0:T(8,128)(2,1)S(1)} collective-permute-done((bf16[64,768]{1,0:T(8,128)(2,1)S(1)}, bf16[64,768]{1,0:T(8,128)(2,1)S(1)}, u32[]{:S(2)}, u32[]{:S(2)}) %collective-permute-start.2) | collective-permute-done | bytes 98336 | tf_op jit(solution)/shard_map/ppermute | solution.py:30
  24.2 1.5 %collective-permute-start.27 = (bf16[384,384]{1,0:T(8,128)(2,1)S(1)}, bf16[384,384]{1,0:T(8,128)(2,1)S(1)}, u32[]{:S(2)}, u32[]{:S(2)}) collective-permute-start(bf16[384,384]{1,0:T(8,128)(2,1)S(1)} %get-tuple-element.58), channel_id=1, source_target_pairs={{0,3},{1,2},{2,1},{3,0},{4,7},{5,6},{6,5},{7,4},{8,11},{9,10},{10,... | collective-permute-start | bytes 884744 | tf_op jit(solution)/shard_map/ppermute | solution.py:30
  26.4 1.7 %prep.1 = (bf16[2,1536,384]{2,1,0:T(8,128)(2,1)S(1)}, f32[3,2,3072]{2,1,0:T(2,128)S(1)}, f32[2,2,128]{2,1,0:T(2,128)S(1)}, f32[128,128]{1,0:T(8,128)S(1)}) custom-call(bf16[3,1536,384]{2,1,0:T(8,128)(2,1)} %bitcast.9, f32[3,2,3072]{2,1,0:T(2,128)} %bitcast.11, f32[2,2,128]{2,1,0:T(2,128)} %far_gain.1, s32[1]{0:T(128)S(6)} %copy.9.count_ref), custom_call_target="tpu_custom_call" | custom-call | tf_op jit(solution)/shard_map/prep/pallas_call | solution.py:298
  29.4 1.7 %collective-permute-start.15 = (bf16[64,768]{1,0:T(8,128)(2,1)S(1)}, bf16[64,768]{1,0:T(8,128)(2,1)S(1)}, u32[]{:S(2)}, u32[]{:S(2)}) collective-permute-start(bf16[64,768]{1,0:T(8,128)(2,1)S(1)} %get-tuple-element.50.refs_1_), channel_id=1, source_target_pairs={{0,4},{4,8},{8,12},{12,0},{1,5},{5,9},{9,13},{13,1},{2,6},{6,10},{... | collective-permute-start | bytes 294920 | tf_op jit(solution)/shard_map/ppermute | solution.py:26
  31.1 2.6 %collective-permute-start.17 = (bf16[64,768]{1,0:T(8,128)(2,1)S(1)}, bf16[64,768]{1,0:T(8,128)(2,1)S(1)}, u32[]{:S(2)}, u32[]{:S(2)}) collective-permute-start(bf16[64,768]{1,0:T(8,128)(2,1)S(1)} %get-tuple-element.50.refs_1_), channel_id=1, source_target_pairs={{0,8},{4,12},{8,0},{12,4},{1,9},{5,13},{9,1},{13,5},{2,10},{6,14},... | collective-permute-start | bytes 294920 | tf_op jit(solution)/shard_map/ppermute | solution.py:26
  35.9 3.6 %collective-permute-start.19 = (bf16[64,768]{1,0:T(8,128)(2,1)S(1)}, bf16[64,768]{1,0:T(8,128)(2,1)S(1)}, u32[]{:S(2)}, u32[]{:S(2)}) collective-permute-start(bf16[64,768]{1,0:T(8,128)(2,1)S(1)} %get-tuple-element.50.refs_1_), channel_id=1, source_target_pairs={{0,12},{4,0},{8,4},{12,8},{1,13},{5,1},{9,5},{13,9},{2,14},{6,2},{... | collective-permute-start | bytes 294920 | tf_op jit(solution)/shard_map/ppermute | solution.py:26
  39.9 1.8 %collective-permute-done.17.refs_3_ = bf16[64,768]{1,0:T(8,128)(2,1)S(1)} collective-permute-done((bf16[64,768]{1,0:T(8,128)(2,1)S(1)}, bf16[64,768]{1,0:T(8,128)(2,1)S(1)}, u32[]{:S(2)}, u32[]{:S(2)}) %collective-permute-start.17) | collective-permute-done | bytes 98336 | tf_op jit(solution)/shard_map/ppermute | solution.py:26
  42.5 3.1 %collective-permute-start.8 = (bf16[64,768]{1,0:T(8,128)(2,1)S(1)}, bf16[64,768]{1,0:T(8,128)(2,1)S(1)}, u32[]{:S(2)}, u32[]{:S(2)}) collective-permute-start(bf16[64,768]{1,0:T(8,128)(2,1)S(1)} %get-tuple-element.49.refs_5_), channel_id=1, source_target_pairs={{0,4},{4,8},{8,12},{12,0},{1,5},{5,9},{9,13},{13,1},{2,6},{6,10},{... | collective-permute-start | bytes 294920 | tf_op jit(solution)/shard_map/ppermute | solution.py:26
  45.6 3.7 %collective-permute-done.10.refs_7_ = bf16[64,768]{1,0:T(8,128)(2,1)S(1)} collective-permute-done((bf16[64,768]{1,0:T(8,128)(2,1)S(1)}, bf16[64,768]{1,0:T(8,128)(2,1)S(1)}, u32[]{:S(2)}, u32[]{:S(2)}) %collective-permute-start.10) | collective-permute-done | bytes 98336 | tf_op jit(solution)/shard_map/ppermute | solution.py:26
  57.1 8.7 %collective-permute-start.22 = (bf16[128,384]{1,0:T(8,128)(2,1)S(1)}, bf16[128,384]{1,0:T(8,128)(2,1)S(1)}, u32[]{:S(2)}, u32[]{:S(2)}) collective-permute-start(bf16[128,384]{1,0:T(8,128)(2,1)S(1)} %shard_map.87.refs_0_), channel_id=1, source_target_pairs={{0,2},{1,3},{2,0},{3,1},{4,6},{5,7},{6,4},{7,5},{8,10},{9,11},{10,... | collective-permute-start | bytes 294920 | tf_op jit(solution)/shard_map/ppermute | solution.py:30
  66.0 4.2 %collective-permute-done.22.refs_2_ = bf16[128,384]{1,0:T(8,128)(2,1)S(1)} collective-permute-done((bf16[128,384]{1,0:T(8,128)(2,1)S(1)}, bf16[128,384]{1,0:T(8,128)(2,1)S(1)}, u32[]{:S(2)}, u32[]{:S(2)}) %collective-permute-start.22) | collective-permute-done | bytes 98336 | tf_op jit(solution)/shard_map/ppermute | solution.py:30
  79.8 1.5 %collective-permute-start.33 = (bf16[64,768]{1,0:T(8,128)(2,1)S(1)}, bf16[64,768]{1,0:T(8,128)(2,1)S(1)}, u32[]{:S(2)}, u32[]{:S(2)}) collective-permute-start(bf16[64,768]{1,0:T(8,128)(2,1)S(1)} %get-tuple-element.60.refs_0_.refs_12_.refs_1_), channel_id=1, source_target_pairs={{0,3},{1,2},{2,1},{3,0},{4,7},{5,6},{6,5},{7,4},{8,11},{9,10},{10,... | collective-permute-start | bytes 294920 | tf_op jit(solution)/shard_map/ppermute | solution.py:30
  81.3 12.7 %collective-permute-done.32.refs_2_ = bf16[64,768]{1,0:T(8,128)(2,1)S(1)} collective-permute-done((bf16[64,768]{1,0:T(8,128)(2,1)S(1)}, bf16[64,768]{1,0:T(8,128)(2,1)S(1)}, u32[]{:S(2)}, u32[]{:S(2)}) %collective-permute-start.32) | collective-permute-done | bytes 98336 | tf_op jit(solution)/shard_map/ppermute | solution.py:30
  97.0 1.6 %collective-permute-done.36.refs_2_ = bf16[64,768]{1,0:T(8,128)(2,1)S(1)} collective-permute-done((bf16[64,768]{1,0:T(8,128)(2,1)S(1)}, bf16[64,768]{1,0:T(8,128)(2,1)S(1)}, u32[]{:S(2)}, u32[]{:S(2)}) %collective-permute-start.36) | collective-permute-done | bytes 98336 | tf_op jit(solution)/shard_map/ppermute | solution.py:30
  98.6 2.0 %collective-permute-done.37.refs_3_ = bf16[64,768]{1,0:T(8,128)(2,1)S(1)} collective-permute-done((bf16[64,768]{1,0:T(8,128)(2,1)S(1)}, bf16[64,768]{1,0:T(8,128)(2,1)S(1)}, u32[]{:S(2)}, u32[]{:S(2)}) %collective-permute-start.37) | collective-permute-done | bytes 98336 | tf_op jit(solution)/shard_map/ppermute | solution.py:30
  101.9 1.9 %collective-permute-start.50 = (bf16[64,768]{1,0:T(8,128)(2,1)S(1)}, bf16[64,768]{1,0:T(8,128)(2,1)S(1)}, u32[]{:S(2)}, u32[]{:S(2)}) collective-permute-start(bf16[64,768]{1,0:T(8,128)(2,1)S(1)} %get-tuple-element.65.refs_1_), channel_id=1, source_target_pairs={{0,12},{4,0},{8,4},{12,8},{1,13},{5,1},{9,5},{13,9},{2,14},{6,2},{... | collective-permute-start | bytes 294920 | tf_op jit(solution)/shard_map/ppermute | solution.py:26
  104.4 2.5 %collective-permute-start.41 = (bf16[64,768]{1,0:T(8,128)(2,1)S(1)}, bf16[64,768]{1,0:T(8,128)(2,1)S(1)}, u32[]{:S(2)}, u32[]{:S(2)}) collective-permute-start(bf16[64,768]{1,0:T(8,128)(2,1)S(1)} %get-tuple-element.64.refs_5_), channel_id=1, source_target_pairs={{0,8},{4,12},{8,0},{12,4},{1,9},{5,13},{9,1},{13,5},{2,10},{6,14},... | collective-permute-start | bytes 294920 | tf_op jit(solution)/shard_map/ppermute | solution.py:26
  106.9 1.8 %collective-permute-start.43 = (bf16[64,768]{1,0:T(8,128)(2,1)S(1)}, bf16[64,768]{1,0:T(8,128)(2,1)S(1)}, u32[]{:S(2)}, u32[]{:S(2)}) collective-permute-start(bf16[64,768]{1,0:T(8,128)(2,1)S(1)} %get-tuple-element.64.refs_5_), channel_id=1, source_target_pairs={{0,12},{4,0},{8,4},{12,8},{1,13},{5,1},{9,5},{13,9},{2,14},{6,2},{... | collective-permute-start | bytes 294920 | tf_op jit(solution)/shard_map/ppermute | solution.py:26
  111.2 3.6 %collective-permute-done.41.refs_7_ = bf16[64,768]{1,0:T(8,128)(2,1)S(1)} collective-permute-done((bf16[64,768]{1,0:T(8,128)(2,1)S(1)}, bf16[64,768]{1,0:T(8,128)(2,1)S(1)}, u32[]{:S(2)}, u32[]{:S(2)}) %collective-permute-start.41) | collective-permute-done | bytes 98336 | tf_op jit(solution)/shard_map/ppermute | solution.py:26
  120.2 1.5 %collective-permute-start.53 = (bf16[128,384]{1,0:T(8,128)(2,1)S(1)}, bf16[128,384]{1,0:T(8,128)(2,1)S(1)}, u32[]{:S(2)}, u32[]{:S(2)}) collective-permute-start(bf16[128,384]{1,0:T(8,128)(2,1)S(1)} %shard_map.95.refs_0_), channel_id=1, source_target_pairs={{0,2},{1,3},{2,0},{3,1},{4,6},{5,7},{6,4},{7,5},{8,10},{9,11},{10,... | collective-permute-start | bytes 294920 | tf_op jit(solution)/shard_map/ppermute | solution.py:30
  121.8 1.5 %collective-permute-start.54 = (bf16[128,384]{1,0:T(8,128)(2,1)S(1)}, bf16[128,384]{1,0:T(8,128)(2,1)S(1)}, u32[]{:S(2)}, u32[]{:S(2)}) collective-permute-start(bf16[128,384]{1,0:T(8,128)(2,1)S(1)} %shard_map.95.refs_0_), channel_id=1, source_target_pairs={{0,3},{1,2},{2,1},{3,0},{4,7},{5,6},{6,5},{7,4},{8,11},{9,10},{10,... | collective-permute-start | bytes 294920 | tf_op jit(solution)/shard_map/ppermute | solution.py:30
  123.3 2.2 %collective-permute-done.52.refs_1_ = bf16[128,384]{1,0:T(8,128)(2,1)S(1)} collective-permute-done((bf16[128,384]{1,0:T(8,128)(2,1)S(1)}, bf16[128,384]{1,0:T(8,128)(2,1)S(1)}, u32[]{:S(2)}, u32[]{:S(2)}) %collective-permute-start.52) | collective-permute-done | bytes 98336 | tf_op jit(solution)/shard_map/ppermute | solution.py:30
  125.5 1.8 %collective-permute-done.54.refs_3_ = bf16[128,384]{1,0:T(8,128)(2,1)S(1)} collective-permute-done((bf16[128,384]{1,0:T(8,128)(2,1)S(1)}, bf16[128,384]{1,0:T(8,128)(2,1)S(1)}, u32[]{:S(2)}, u32[]{:S(2)}) %collective-permute-start.54) | collective-permute-done | bytes 98336 | tf_op jit(solution)/shard_map/ppermute | solution.py:30
  128.0 1.4 %collective-permute-done.62.refs_3_ = bf16[128,768]{1,0:T(8,128)(2,1)S(1)} collective-permute-done((bf16[128,768]{1,0:T(8,128)(2,1)S(1)}, bf16[128,768]{1,0:T(8,128)(2,1)S(1)}, u32[]{:S(2)}, u32[]{:S(2)}) %collective-permute-start.62) | collective-permute-done | bytes 196640 | tf_op jit(solution)/shard_map/ppermute | solution.py:34
  (121 shorter events, 40.7 us)
Async XLA Ops:
  0.0 25.7 %collective-permute-start.3 = (bf16[3,1536,384]{2,1,0:T(8,128)(2,1)}, bf16[3,1536,384]{2,1,0:T(8,128)(2,1)S(1)}, u32[]{:S(2)}, u32[]{:S(2)}) collective-permute-start(bf16[3,1536,384]{2,1,0:T(8,128)(2,1)} %bitcast.8), channel_id=1, source_target_pairs={{0,16},{16,0},{1,17},{17,1},{2,18},{18,2},{3,19},{19,3},{4,20},{20... | collective-permute-start | bytes 10616840 | tf_op jit(solution)/shard_map/ppermute | solution.py:34
  0.5 75.9 %collective-permute-start.34 = (bf16[3,1536,384]{2,1,0:T(8,128)(2,1)}, bf16[3,1536,384]{2,1,0:T(8,128)(2,1)S(1)}, u32[]{:S(2)}, u32[]{:S(2)}) collective-permute-start(bf16[3,1536,384]{2,1,0:T(8,128)(2,1)} %bitcast.4), channel_id=1, source_target_pairs={{0,16},{16,0},{1,17},{17,1},{2,18},{18,2},{3,19},{19,3},{4,20},{20... | collective-permute-start | bytes 10616840 | tf_op jit(solution)/shard_map/ppermute | solution.py:34
  0.5 12.8 %collective-permute-start.24 = (bf16[384,1536]{1,0:T(8,128)(2,1)}, bf16[384,1536]{1,0:T(8,128)(2,1)S(1)}, u32[]{:S(2)}, u32[]{:S(2)}) collective-permute-start(bf16[384,1536]{1,0:T(8,128)(2,1)} %near_ref.2), channel_id=1, source_target_pairs={{0,16},{16,0},{1,17},{17,1},{2,18},{18,2},{3,19},{19,3},{4,20},{20... | collective-permute-start | bytes 3538952 | tf_op jit(solution)/shard_map/ppermute | solution.py:34
  8.0 9.7 %collective-permute-start.6 = (bf16[64,768]{1,0:T(8,128)(2,1)S(1)}, bf16[64,768]{1,0:T(8,128)(2,1)S(1)}, u32[]{:S(2)}, u32[]{:S(2)}) collective-permute-start(bf16[64,768]{1,0:T(8,128)(2,1)S(1)} %get-tuple-element.47.refs_0_.refs_13_), channel_id=1, source_target_pairs={{0,3},{1,2},{2,1},{3,0},{4,7},{5,6},{6,5},{7,4},{8,11},{9,10},{10,... | collective-permute-start | bytes 294920 | tf_op jit(solution)/shard_map/ppermute | solution.py:30
  10.7 8.5 %collective-permute-start = (bf16[64,768]{1,0:T(8,128)(2,1)S(1)}, bf16[64,768]{1,0:T(8,128)(2,1)S(1)}, u32[]{:S(2)}, u32[]{:S(2)}) collective-permute-start(bf16[64,768]{1,0:T(8,128)(2,1)S(1)} %get-tuple-element.41.refs_0_.refs_12_), channel_id=1, source_target_pairs={{0,1},{1,0},{2,3},{3,2},{4,5},{5,4},{6,7},{7,6},{8,9},{9,8},{10,11... | collective-permute-start | bytes 294920 | tf_op jit(solution)/shard_map/ppermute | solution.py:30
  19.1 10.3 %collective-permute-start.25 = (bf16[384,384]{1,0:T(8,128)(2,1)S(1)}, bf16[384,384]{1,0:T(8,128)(2,1)S(1)}, u32[]{:S(2)}, u32[]{:S(2)}) collective-permute-start(bf16[384,384]{1,0:T(8,128)(2,1)S(1)} %get-tuple-element.56), channel_id=1, source_target_pairs={{0,1},{1,0},{2,3},{3,2},{4,5},{5,4},{6,7},{7,6},{8,9},{9,8},{10,11... | collective-permute-start | bytes 884744 | tf_op jit(solution)/shard_map/ppermute | solution.py:30
  19.3 11.8 %collective-permute-start.26 = (bf16[384,384]{1,0:T(8,128)(2,1)S(1)}, bf16[384,384]{1,0:T(8,128)(2,1)S(1)}, u32[]{:S(2)}, u32[]{:S(2)}) collective-permute-start(bf16[384,384]{1,0:T(8,128)(2,1)S(1)} %get-tuple-element.57), channel_id=1, source_target_pairs={{0,2},{1,3},{2,0},{3,1},{4,6},{5,7},{6,4},{7,5},{8,10},{9,11},{10,... | collective-permute-start | bytes 884744 | tf_op jit(solution)/shard_map/ppermute | solution.py:30
  24.2 11.7 %collective-permute-start.27 = (bf16[384,384]{1,0:T(8,128)(2,1)S(1)}, bf16[384,384]{1,0:T(8,128)(2,1)S(1)}, u32[]{:S(2)}, u32[]{:S(2)}) collective-permute-start(bf16[384,384]{1,0:T(8,128)(2,1)S(1)} %get-tuple-element.58), channel_id=1, source_target_pairs={{0,3},{1,2},{2,1},{3,0},{4,7},{5,6},{6,5},{7,4},{8,11},{9,10},{10,... | collective-permute-start | bytes 884744 | tf_op jit(solution)/shard_map/ppermute | solution.py:30
  25.7 48.3 %collective-permute-start.55 = (bf16[384,1536]{1,0:T(8,128)(2,1)S(1)}, bf16[384,1536]{1,0:T(8,128)(2,1)S(1)}, u32[]{:S(2)}, u32[]{:S(2)}) collective-permute-start(bf16[384,1536]{1,0:T(8,128)(2,1)S(1)} %copy-done.3), channel_id=1, source_target_pairs={{0,16},{16,0},{1,17},{17,1},{2,18},{18,2},{3,19},{19,3},{4,20},{20... | collective-permute-start | bytes 3538952 | tf_op jit(solution)/shard_map/ppermute | solution.py:34
  29.4 10.1 %collective-permute-start.15 = (bf16[64,768]{1,0:T(8,128)(2,1)S(1)}, bf16[64,768]{1,0:T(8,128)(2,1)S(1)}, u32[]{:S(2)}, u32[]{:S(2)}) collective-permute-start(bf16[64,768]{1,0:T(8,128)(2,1)S(1)} %get-tuple-element.50.refs_1_), channel_id=1, source_target_pairs={{0,4},{4,8},{8,12},{12,0},{1,5},{5,9},{9,13},{13,1},{2,6},{6,10},{... | collective-permute-start | bytes 294920 | tf_op jit(solution)/shard_map/ppermute | solution.py:26
  31.1 10.6 %collective-permute-start.17 = (bf16[64,768]{1,0:T(8,128)(2,1)S(1)}, bf16[64,768]{1,0:T(8,128)(2,1)S(1)}, u32[]{:S(2)}, u32[]{:S(2)}) collective-permute-start(bf16[64,768]{1,0:T(8,128)(2,1)S(1)} %get-tuple-element.50.refs_1_), channel_id=1, source_target_pairs={{0,8},{4,12},{8,0},{12,4},{1,9},{5,13},{9,1},{13,5},{2,10},{6,14},... | collective-permute-start | bytes 294920 | tf_op jit(solution)/shard_map/ppermute | solution.py:26
  39.5 9.8 %collective-permute-start.10 = (bf16[64,768]{1,0:T(8,128)(2,1)S(1)}, bf16[64,768]{1,0:T(8,128)(2,1)S(1)}, u32[]{:S(2)}, u32[]{:S(2)}) collective-permute-start(bf16[64,768]{1,0:T(8,128)(2,1)S(1)} %get-tuple-element.49.refs_5_), channel_id=1, source_target_pairs={{0,8},{4,12},{8,0},{12,4},{1,9},{5,13},{9,1},{13,5},{2,10},{6,14},... | collective-permute-start | bytes 294920 | tf_op jit(solution)/shard_map/ppermute | solution.py:26
  41.7 8.5 %collective-permute-start.12 = (bf16[64,768]{1,0:T(8,128)(2,1)S(1)}, bf16[64,768]{1,0:T(8,128)(2,1)S(1)}, u32[]{:S(2)}, u32[]{:S(2)}) collective-permute-start(bf16[64,768]{1,0:T(8,128)(2,1)S(1)} %get-tuple-element.49.refs_5_), channel_id=1, source_target_pairs={{0,12},{4,0},{8,4},{12,8},{1,13},{5,1},{9,5},{13,9},{2,14},{6,2},{... | collective-permute-start | bytes 294920 | tf_op jit(solution)/shard_map/ppermute | solution.py:26
  42.5 7.8 %collective-permute-start.8 = (bf16[64,768]{1,0:T(8,128)(2,1)S(1)}, bf16[64,768]{1,0:T(8,128)(2,1)S(1)}, u32[]{:S(2)}, u32[]{:S(2)}) collective-permute-start(bf16[64,768]{1,0:T(8,128)(2,1)S(1)} %get-tuple-element.49.refs_5_), channel_id=1, source_target_pairs={{0,4},{4,8},{8,12},{12,0},{1,5},{5,9},{9,13},{13,1},{2,6},{6,10},{... | collective-permute-start | bytes 294920 | tf_op jit(solution)/shard_map/ppermute | solution.py:26
  54.1 11.6 %collective-permute-start.30 = (bf16[384,384]{1,0:T(8,128)(2,1)S(1)}, bf16[384,384]{1,0:T(8,128)(2,1)S(1)}, u32[]{:S(2)}, u32[]{:S(2)}) collective-permute-start(bf16[384,384]{1,0:T(8,128)(2,1)S(1)} %collective-permute-done.27.refs_7_), channel_id=1, source_target_pairs={{0,16},{16,0},{1,17},{17,1},{2,18},{18,2},{3,19},{19,3},{4,20},{20... | collective-permute-start | bytes 884744 | tf_op jit(solution)/shard_map/ppermute | solution.py:34
  56.8 9.1 %collective-permute-start.21 = (bf16[128,384]{1,0:T(8,128)(2,1)S(1)}, bf16[128,384]{1,0:T(8,128)(2,1)S(1)}, u32[]{:S(2)}, u32[]{:S(2)}) collective-permute-start(bf16[128,384]{1,0:T(8,128)(2,1)S(1)} %shard_map.87.refs_0_), channel_id=1, source_target_pairs={{0,1},{1,0},{2,3},{3,2},{4,5},{5,4},{6,7},{7,6},{8,9},{9,8},{10,11... | collective-permute-start | bytes 294920 | tf_op jit(solution)/shard_map/ppermute | solution.py:30
  57.1 13.1 %collective-permute-start.22 = (bf16[128,384]{1,0:T(8,128)(2,1)S(1)}, bf16[128,384]{1,0:T(8,128)(2,1)S(1)}, u32[]{:S(2)}, u32[]{:S(2)}) collective-permute-start(bf16[128,384]{1,0:T(8,128)(2,1)S(1)} %shard_map.87.refs_0_), channel_id=1, source_target_pairs={{0,2},{1,3},{2,0},{3,1},{4,6},{5,7},{6,4},{7,5},{8,10},{9,11},{10,... | collective-permute-start | bytes 294920 | tf_op jit(solution)/shard_map/ppermute | solution.py:30
  73.1 6.7 %collective-permute-start.31 = (bf16[64,768]{1,0:T(8,128)(2,1)S(1)}, bf16[64,768]{1,0:T(8,128)(2,1)S(1)}, u32[]{:S(2)}, u32[]{:S(2)}) collective-permute-start(bf16[64,768]{1,0:T(8,128)(2,1)S(1)} %get-tuple-element.60.refs_0_.refs_12_.refs_1_), channel_id=1, source_target_pairs={{0,1},{1,0},{2,3},{3,2},{4,5},{5,4},{6,7},{7,6},{8,9},{9,8},{10,11... | collective-permute-start | bytes 294920 | tf_op jit(solution)/shard_map/ppermute | solution.py:30
  74.2 27.7 %collective-permute-start.56 = (bf16[384,384]{1,0:T(8,128)(2,1)S(1)}, bf16[384,384]{1,0:T(8,128)(2,1)S(1)}, u32[]{:S(2)}, u32[]{:S(2)}) collective-permute-start(bf16[384,384]{1,0:T(8,128)(2,1)S(1)} %get-tuple-element.71), channel_id=1, source_target_pairs={{0,1},{1,0},{2,3},{3,2},{4,5},{5,4},{6,7},{7,6},{8,9},{9,8},{10,11... | collective-permute-start | bytes 884744 | tf_op jit(solution)/shard_map/ppermute | solution.py:30
  75.4 28.4 %collective-permute-start.57 = (bf16[384,384]{1,0:T(8,128)(2,1)S(1)}, bf16[384,384]{1,0:T(8,128)(2,1)S(1)}, u32[]{:S(2)}, u32[]{:S(2)}) collective-permute-start(bf16[384,384]{1,0:T(8,128)(2,1)S(1)} %get-tuple-element.72), channel_id=1, source_target_pairs={{0,2},{1,3},{2,0},{3,1},{4,6},{5,7},{6,4},{7,5},{8,10},{9,11},{10,... | collective-permute-start | bytes 884744 | tf_op jit(solution)/shard_map/ppermute | solution.py:30
  76.4 28.0 %collective-permute-start.58 = (bf16[384,384]{1,0:T(8,128)(2,1)S(1)}, bf16[384,384]{1,0:T(8,128)(2,1)S(1)}, u32[]{:S(2)}, u32[]{:S(2)}) collective-permute-start(bf16[384,384]{1,0:T(8,128)(2,1)S(1)} %get-tuple-element.73), channel_id=1, source_target_pairs={{0,3},{1,2},{2,1},{3,0},{4,7},{5,6},{6,5},{7,4},{8,11},{9,10},{10,... | collective-permute-start | bytes 884744 | tf_op jit(solution)/shard_map/ppermute | solution.py:30
  77.8 16.2 %collective-permute-start.32 = (bf16[64,768]{1,0:T(8,128)(2,1)S(1)}, bf16[64,768]{1,0:T(8,128)(2,1)S(1)}, u32[]{:S(2)}, u32[]{:S(2)}) collective-permute-start(bf16[64,768]{1,0:T(8,128)(2,1)S(1)} %get-tuple-element.60.refs_0_.refs_12_.refs_1_), channel_id=1, source_target_pairs={{0,2},{1,3},{2,0},{3,1},{4,6},{5,7},{6,4},{7,5},{8,10},{9,11},{10,... | collective-permute-start | bytes 294920 | tf_op jit(solution)/shard_map/ppermute | solution.py:30
  79.8 15.3 %collective-permute-start.33 = (bf16[64,768]{1,0:T(8,128)(2,1)S(1)}, bf16[64,768]{1,0:T(8,128)(2,1)S(1)}, u32[]{:S(2)}, u32[]{:S(2)}) collective-permute-start(bf16[64,768]{1,0:T(8,128)(2,1)S(1)} %get-tuple-element.60.refs_0_.refs_12_.refs_1_), channel_id=1, source_target_pairs={{0,3},{1,2},{2,1},{3,0},{4,7},{5,6},{6,5},{7,4},{8,11},{9,10},{10,... | collective-permute-start | bytes 294920 | tf_op jit(solution)/shard_map/ppermute | solution.py:30
  98.6 8.3 %collective-permute-start.46 = (bf16[64,768]{1,0:T(8,128)(2,1)S(1)}, bf16[64,768]{1,0:T(8,128)(2,1)S(1)}, u32[]{:S(2)}, u32[]{:S(2)}) collective-permute-start(bf16[64,768]{1,0:T(8,128)(2,1)S(1)} %get-tuple-element.65.refs_1_), channel_id=1, source_target_pairs={{0,4},{4,8},{8,12},{12,0},{1,5},{5,9},{9,13},{13,1},{2,6},{6,10},{... | collective-permute-start | bytes 294920 | tf_op jit(solution)/shard_map/ppermute | solution.py:26
  100.6 9.5 %collective-permute-start.48 = (bf16[64,768]{1,0:T(8,128)(2,1)S(1)}, bf16[64,768]{1,0:T(8,128)(2,1)S(1)}, u32[]{:S(2)}, u32[]{:S(2)}) collective-permute-start(bf16[64,768]{1,0:T(8,128)(2,1)S(1)} %get-tuple-element.65.refs_1_), channel_id=1, source_target_pairs={{0,8},{4,12},{8,0},{12,4},{1,9},{5,13},{9,1},{13,5},{2,10},{6,14},... | collective-permute-start | bytes 294920 | tf_op jit(solution)/shard_map/ppermute | solution.py:26
  101.9 8.1 %collective-permute-start.50 = (bf16[64,768]{1,0:T(8,128)(2,1)S(1)}, bf16[64,768]{1,0:T(8,128)(2,1)S(1)}, u32[]{:S(2)}, u32[]{:S(2)}) collective-permute-start(bf16[64,768]{1,0:T(8,128)(2,1)S(1)} %get-tuple-element.65.refs_1_), channel_id=1, source_target_pairs={{0,12},{4,0},{8,4},{12,8},{1,13},{5,1},{9,5},{13,9},{2,14},{6,2},{... | collective-permute-start | bytes 294920 | tf_op jit(solution)/shard_map/ppermute | solution.py:26
  103.8 7.4 %collective-permute-start.39 = (bf16[64,768]{1,0:T(8,128)(2,1)S(1)}, bf16[64,768]{1,0:T(8,128)(2,1)S(1)}, u32[]{:S(2)}, u32[]{:S(2)}) collective-permute-start(bf16[64,768]{1,0:T(8,128)(2,1)S(1)} %get-tuple-element.64.refs_5_), channel_id=1, source_target_pairs={{0,4},{4,8},{8,12},{12,0},{1,5},{5,9},{9,13},{13,1},{2,6},{6,10},{... | collective-permute-start | bytes 294920 | tf_op jit(solution)/shard_map/ppermute | solution.py:26
  104.4 10.4 %collective-permute-start.41 = (bf16[64,768]{1,0:T(8,128)(2,1)S(1)}, bf16[64,768]{1,0:T(8,128)(2,1)S(1)}, u32[]{:S(2)}, u32[]{:S(2)}) collective-permute-start(bf16[64,768]{1,0:T(8,128)(2,1)S(1)} %get-tuple-element.64.refs_5_), channel_id=1, source_target_pairs={{0,8},{4,12},{8,0},{12,4},{1,9},{5,13},{9,1},{13,5},{2,10},{6,14},... | collective-permute-start | bytes 294920 | tf_op jit(solution)/shard_map/ppermute | solution.py:26
  106.9 7.9 %collective-permute-start.43 = (bf16[64,768]{1,0:T(8,128)(2,1)S(1)}, bf16[64,768]{1,0:T(8,128)(2,1)S(1)}, u32[]{:S(2)}, u32[]{:S(2)}) collective-permute-start(bf16[64,768]{1,0:T(8,128)(2,1)S(1)} %get-tuple-element.64.refs_5_), channel_id=1, source_target_pairs={{0,12},{4,0},{8,4},{12,8},{1,13},{5,1},{9,5},{13,9},{2,14},{6,2},{... | collective-permute-start | bytes 294920 | tf_op jit(solution)/shard_map/ppermute | solution.py:26
  114.8 7.0 %collective-permute-start.59 = (bf16[384,384]{1,0:T(8,128)(2,1)S(1)}, bf16[384,384]{1,0:T(8,128)(2,1)S(1)}, u32[]{:S(2)}, u32[]{:S(2)}) collective-permute-start(bf16[384,384]{1,0:T(8,128)(2,1)S(1)} %collective-permute-done.56.refs_5_), channel_id=1, source_target_pairs={{0,16},{16,0},{1,17},{17,1},{2,18},{18,2},{3,19},{19,3},{4,20},{20... | collective-permute-start | bytes 884744 | tf_op jit(solution)/shard_map/ppermute | solution.py:34
  115.8 7.5 %collective-permute-start.60 = (bf16[384,384]{1,0:T(8,128)(2,1)S(1)}, bf16[384,384]{1,0:T(8,128)(2,1)S(1)}, u32[]{:S(2)}, u32[]{:S(2)}) collective-permute-start(bf16[384,384]{1,0:T(8,128)(2,1)S(1)} %collective-permute-done.57.refs_6_), channel_id=1, source_target_pairs={{0,16},{16,0},{1,17},{17,1},{2,18},{18,2},{3,19},{19,3},{4,20},{20... | collective-permute-start | bytes 884744 | tf_op jit(solution)/shard_map/ppermute | solution.py:34
  116.1 7.2 %collective-permute-start.61 = (bf16[384,384]{1,0:T(8,128)(2,1)S(1)}, bf16[384,384]{1,0:T(8,128)(2,1)S(1)}, u32[]{:S(2)}, u32[]{:S(2)}) collective-permute-start(bf16[384,384]{1,0:T(8,128)(2,1)S(1)} %collective-permute-done.58.refs_7_), channel_id=1, source_target_pairs={{0,16},{16,0},{1,17},{17,1},{2,18},{18,2},{3,19},{19,3},{4,20},{20... | collective-permute-start | bytes 884744 | tf_op jit(solution)/shard_map/ppermute | solution.py:34
  (35 other events, 171.8 us)

commit v7 on v6

--- a/solution.py
+++ b/solution.py
@@ -188,6 +188,11 @@
     scale = math.log2(math.e) / HEAD_DIM**0.5
     rows = query_ref.shape[0]
     ones = jnp.ones((16, HEAD_DIM), BF16)
+    if opens and len(rest) == 3:
+        at = 0
+        for ref in blocks:
+            rest[2][at : at + ref.shape[0], :] = ref[...]
+            at += ref.shape[0]
     heads = [slice(lo, lo + HEAD_DIM) for lo in range(0, width, HEAD_DIM)]
     raw = []
     for at in heads:
@@ -335,7 +340,11 @@
     if blk == 0:
         qkv, out_weight = later
         later = ((qkv, swap(qkv)), (out_weight, swap(out_weight)))
-    held = [[line, [swap(p) for p in line]] for line in blocks]
+    whole = chunks > 1
+    held = [
+        [line, [] if whole and c == 0 else [swap(p) for p in line]]
+        for c, line in enumerate(blocks)
+    ]
     others = [spread[n_head]] + [swap(p) for p in mine[1:]]
     groups = groups_of(n_seq, chunks)
     carry = []
@@ -344,13 +353,20 @@
         shape = [SHAPE((full, width), F32), SHAPE((2, full, HEAD_DIM), F32)]
         if closes:
             shape = [SHAPE((full, width), BF16)]
+        elif whole and i == 0:
+            shape.append(SHAPE((len(group) * rows, 2 * width), BF16))
+        taken = [held[c][core][k] for c, core, k in group if held[c][core]]
+        if whole and i == 1:
+            taken = [swap(pack)] + taken
         carry = pl.pallas_call(
-            functools.partial(step_kernel, len(group), i == 0, closes),
+            functools.partial(step_kernel, len(taken), i == 0, closes),
             out_shape=shape,
-            in_specs=[VMEM] * (1 + len(group) + len(carry)),
+            in_specs=[VMEM] * (1 + len(taken) + len(carry)),
             out_specs=[VMEM] * len(shape),
             compiler_params=params(16),
-        )(query, *[held[c][core][k] for c, core, k in group], *carry)
+        )(query, *taken, *carry)
+        if whole and i == 0:
+            *carry, pack = carry
     (attended,) = carry
     gathered = [attended] + [cross(attended, "head", k, n_head) for k in range(1, n_head)]
     shape = [SHAPE((rows, quarter), BF16)] * chunks

time: 130 us -> 124 us (0.954)
  starting transfers between devices: 62.7 us -> 48.9 us
  waiting for transfers between devices: 50 us -> 57 us
    ppermute x12, waiting for transfers between devices: 12 us -> 20.8 us  [turn(): return lax.ppermute(x, axis, [(i, (i + k) % n) for i in range(n)])]
    ppermute x24, waiting for transfers between devices: 32 us -> 23.3 us  [cross(): return lax.ppermute(x, axis, [(i, i ^ k) for i in range(n)])]
    ppermute x24, starting transfers between devices: 38.2 us -> 30.4 us  [cross(): return lax.ppermute(x, axis, [(i, i ^ k) for i in range(n)])]
    ppermute x27 -> x21, waiting for transfers between devices: 6.05 us -> 12.8 us  [swap(): return lax.ppermute(x, 'branch', [(0, 1), (1, 0)])]
    ppermute x12, starting transfers between devices: 19 us -> 14.6 us  [turn(): return lax.ppermute(x, axis, [(i, (i + k) % n) for i in range(n)])]
    ppermute x27 -> x21, starting transfers between devices: 5.5 us -> 3.88 us  [swap(): return lax.ppermute(x, 'branch', [(0, 1), (1, 0)])]
  transfers between devices with their start and end apart: 63 -> 57, of which waited for: 24 -> 27; matrix products, arithmetic and copies ran while one was open for 0% -> 0% of each run, Pallas kernels for 11% -> 11%
where the time goes in v7:
time: 124 us
  waiting for transfers between devices  57 us (46%)
  starting transfers between devices  48.9 us (39%)
  Pallas kernels  15.4 us (12%)
  local copies, waits for them, and re-layouts  1.28 us (1%)
    ppermute x24, starting transfers between devices, cross(): return lax.ppermute(x, axis, [(i, i ^ k) for i in range(n)])  30.4 us
    ppermute x24, waiting for transfers between devices, cross(): return lax.ppermute(x, axis, [(i, i ^ k) for i in range(n)])  23.3 us
    ppermute x12, waiting for transfers between devices, turn(): return lax.ppermute(x, axis, [(i, (i + k) % n) for i in range(n)])  20.8 us
    ppermute x12, starting transfers between devices, turn(): return lax.ppermute(x, axis, [(i, (i + k) % n) for i in range(n)])  14.6 us
    ppermute x21, waiting for transfers between devices, swap(): return lax.ppermute(x, 'branch', [(0, 1), (1, 0)])  12.8 us
    pallas_call x4, Pallas kernels, block(): pl.pallas_call(functools.partial(kv_kernel, blk, c, n_head), out_shape=(S...  5.21 us
    ppermute x21, starting transfers between devices, swap(): return lax.ppermute(x, 'branch', [(0, 1), (1, 0)])  3.88 us
    pallas_call x6, Pallas kernels, block(): pl.pallas_call(functools.partial(step_kernel, len(taken), i == 0, closes)...  3.71 us
  transfers between devices with their start and end apart: 57, of which 27 were waited for; matrix products, arithmetic and copies ran while one was open for 0% of the time, Pallas kernels for 11%

profile of v7, /device:TPU:0, one launch (start us, length us, event | category | flops | bytes accessed | tf_op | source)
XLA Modules:
  0.0 123.6 jit_solution(15434254243147844246)
XLA Ops:
  2.0 2.5 %collective-permute-start = (bf16[64,768]{1,0:T(8,128)(2,1)S(1)}, bf16[64,768]{1,0:T(8,128)(2,1)S(1)}, u32[]{:S(2)}, u32[]{:S(2)}) collective-permute-start(bf16[64,768]{1,0:T(8,128)(2,1)S(1)} %get-tuple-element.43.refs_0_.refs_12_), channel_id=1, source_target_pairs={{0,1},{1,0},{2,3},{3,2},{4,5},{5,4},{6,7},{7,6},{8,9},{9,8},{10,11... | collective-permute-start | bytes 294920 | tf_op jit(solution)/shard_map/ppermute | solution.py:30
  4.5 8.8 %collective-permute-done.21.across_ref = bf16[384,1536]{1,0:T(8,128)(2,1)S(1)} collective-permute-done((bf16[384,1536]{1,0:T(8,128)(2,1)}, bf16[384,1536]{1,0:T(8,128)(2,1)S(1)}, u32[]{:S(2)}, u32[]{:S(2)}) %collective-permute-start.21) | collective-permute-done | bytes 1179680 | tf_op jit(solution)/shard_map/ppermute | solution.py:34
  14.8 2.9 %collective-permute-start.22 = (bf16[384,384]{1,0:T(8,128)(2,1)S(1)}, bf16[384,384]{1,0:T(8,128)(2,1)S(1)}, u32[]{:S(2)}, u32[]{:S(2)}) collective-permute-start(bf16[384,384]{1,0:T(8,128)(2,1)S(1)} %get-tuple-element.59), channel_id=1, source_target_pairs={{0,1},{1,0},{2,3},{3,2},{4,5},{5,4},{6,7},{7,6},{8,9},{9,8},{10,11... | collective-permute-start | bytes 884744 | tf_op jit(solution)/shard_map/ppermute | solution.py:30
  17.7 1.5 %collective-permute-start.1 = (bf16[64,768]{1,0:T(8,128)(2,1)S(1)}, bf16[64,768]{1,0:T(8,128)(2,1)S(1)}, u32[]{:S(2)}, u32[]{:S(2)}) collective-permute-start(bf16[64,768]{1,0:T(8,128)(2,1)S(1)} %get-tuple-element.43.refs_0_.refs_12_), channel_id=1, source_target_pairs={{0,2},{1,3},{2,0},{3,1},{4,6},{5,7},{6,4},{7,5},{8,10},{9,11},{10,... | collective-permute-start | bytes 294920 | tf_op jit(solution)/shard_map/ppermute | solution.py:30
  19.2 3.1 %collective-permute-done.1.refs_2_ = bf16[64,768]{1,0:T(8,128)(2,1)S(1)} collective-permute-done((bf16[64,768]{1,0:T(8,128)(2,1)S(1)}, bf16[64,768]{1,0:T(8,128)(2,1)S(1)}, u32[]{:S(2)}, u32[]{:S(2)}) %collective-permute-start.1) | collective-permute-done | bytes 98336 | tf_op jit(solution)/shard_map/ppermute | solution.py:30
  22.6 6.5 %collective-permute-done.2.refs_3_ = bf16[64,768]{1,0:T(8,128)(2,1)S(1)} collective-permute-done((bf16[64,768]{1,0:T(8,128)(2,1)S(1)}, bf16[64,768]{1,0:T(8,128)(2,1)S(1)}, u32[]{:S(2)}, u32[]{:S(2)}) %collective-permute-start.2) | collective-permute-done | bytes 98336 | tf_op jit(solution)/shard_map/ppermute | solution.py:30
  29.8 3.0 %collective-permute-start.6 = (bf16[64,768]{1,0:T(8,128)(2,1)S(1)}, bf16[64,768]{1,0:T(8,128)(2,1)S(1)}, u32[]{:S(2)}, u32[]{:S(2)}) collective-permute-start(bf16[64,768]{1,0:T(8,128)(2,1)S(1)} %get-tuple-element.49.refs_0_.refs_13_), channel_id=1, source_target_pairs={{0,3},{1,2},{2,1},{3,0},{4,7},{5,6},{6,5},{7,4},{8,11},{9,10},{10,... | collective-permute-start | bytes 294920 | tf_op jit(solution)/shard_map/ppermute | solution.py:30
  32.8 1.7 %prep.1 = (bf16[2,1536,384]{2,1,0:T(8,128)(2,1)S(1)}, f32[3,2,3072]{2,1,0:T(2,128)S(1)}, f32[2,2,128]{2,1,0:T(2,128)S(1)}, f32[128,128]{1,0:T(8,128)S(1)}) custom-call(bf16[3,1536,384]{2,1,0:T(8,128)(2,1)} %bitcast.9, f32[3,2,3072]{2,1,0:T(2,128)} %bitcast.11, f32[2,2,128]{2,1,0:T(2,128)} %far_gain.1, s32[1]{0:T(128)S(6)} %copy.9.count_ref), custom_call_target="tpu_custom_call" | custom-call | tf_op jit(solution)/shard_map/prep/pallas_call | solution.py:303
  36.4 1.6 %collective-permute-start.14 = (bf16[64,768]{1,0:T(8,128)(2,1)S(1)}, bf16[64,768]{1,0:T(8,128)(2,1)S(1)}, u32[]{:S(2)}, u32[]{:S(2)}) collective-permute-start(bf16[64,768]{1,0:T(8,128)(2,1)S(1)} %get-tuple-element.52.refs_1_), channel_id=1, source_target_pairs={{0,4},{4,8},{8,12},{12,0},{1,5},{5,9},{9,13},{13,1},{2,6},{6,10},{... | collective-permute-start | bytes 294920 | tf_op jit(solution)/shard_map/ppermute | solution.py:26
  38.0 2.6 %collective-permute-start.15 = (bf16[64,768]{1,0:T(8,128)(2,1)S(1)}, bf16[64,768]{1,0:T(8,128)(2,1)S(1)}, u32[]{:S(2)}, u32[]{:S(2)}) collective-permute-start(bf16[64,768]{1,0:T(8,128)(2,1)S(1)} %get-tuple-element.52.refs_1_), channel_id=1, source_target_pairs={{0,8},{4,12},{8,0},{12,4},{1,9},{5,13},{9,1},{13,5},{2,10},{6,14},... | collective-permute-start | bytes 294920 | tf_op jit(solution)/shard_map/ppermute | solution.py:26
  40.6 1.5 %collective-permute-start.24 = (bf16[384,384]{1,0:T(8,128)(2,1)S(1)}, bf16[384,384]{1,0:T(8,128)(2,1)S(1)}, u32[]{:S(2)}, u32[]{:S(2)}) collective-permute-start(bf16[384,384]{1,0:T(8,128)(2,1)S(1)} %get-tuple-element.61), channel_id=1, source_target_pairs={{0,3},{1,2},{2,1},{3,0},{4,7},{5,6},{6,5},{7,4},{8,11},{9,10},{10,... | collective-permute-start | bytes 884744 | tf_op jit(solution)/shard_map/ppermute | solution.py:30
  42.9 2.1 %collective-permute-done.15.refs_3_ = bf16[64,768]{1,0:T(8,128)(2,1)S(1)} collective-permute-done((bf16[64,768]{1,0:T(8,128)(2,1)S(1)}, bf16[64,768]{1,0:T(8,128)(2,1)S(1)}, u32[]{:S(2)}, u32[]{:S(2)}) %collective-permute-start.15) | collective-permute-done | bytes 98336 | tf_op jit(solution)/shard_map/ppermute | solution.py:26
  45.8 1.3 %shard_map.83 = (bf16[64,768]{1,0:T(8,128)(2,1)S(1)}, bf16[4,64,768]{2,1,0:T(8,128)(2,1)S(1)}) custom-call(bf16[64,768]{1,0:T(8,128)(2,1)S(1)} %get-tuple-element.49.refs_0_.refs_13_, bf16[64,768]{1,0:T(8,128)(2,1)S(1)} %collective-permute-done.4.refs_1_, bf16[64,768]{1,0:T(8,128)(2,1)S(1)} %collective-permute-done.5.refs_2_, ...), custom_call_target="tpu_custom_call" | custom-call | tf_op jit(solution)/shard_map/pallas_call | solution.py:316
  47.1 2.5 %collective-permute-done.16.refs_4_ = bf16[64,768]{1,0:T(8,128)(2,1)S(1)} collective-permute-done((bf16[64,768]{1,0:T(8,128)(2,1)S(1)}, bf16[64,768]{1,0:T(8,128)(2,1)S(1)}, u32[]{:S(2)}, u32[]{:S(2)}) %collective-permute-start.16) | collective-permute-done | bytes 98336 | tf_op jit(solution)/shard_map/ppermute | solution.py:26
  52.0 1.5 %collective-permute-start.12 = (bf16[64,768]{1,0:T(8,128)(2,1)S(1)}, bf16[64,768]{1,0:T(8,128)(2,1)S(1)}, u32[]{:S(2)}, u32[]{:S(2)}) collective-permute-start(bf16[64,768]{1,0:T(8,128)(2,1)S(1)} %get-tuple-element.51.refs_2_), channel_id=1, source_target_pairs={{0,12},{4,0},{8,4},{12,8},{1,13},{5,1},{9,5},{13,9},{2,14},{6,2},{... | collective-permute-start | bytes 294920 | tf_op jit(solution)/shard_map/ppermute | solution.py:26
  53.5 2.3 %collective-permute-done.10.refs_4_ = bf16[64,768]{1,0:T(8,128)(2,1)S(1)} collective-permute-done((bf16[64,768]{1,0:T(8,128)(2,1)S(1)}, bf16[64,768]{1,0:T(8,128)(2,1)S(1)}, u32[]{:S(2)}, u32[]{:S(2)}) %collective-permute-start.10) | collective-permute-done | bytes 98336 | tf_op jit(solution)/shard_map/ppermute | solution.py:26
  55.9 2.1 %collective-permute-done.12.refs_5_ = bf16[64,768]{1,0:T(8,128)(2,1)S(1)} collective-permute-done((bf16[64,768]{1,0:T(8,128)(2,1)S(1)}, bf16[64,768]{1,0:T(8,128)(2,1)S(1)}, u32[]{:S(2)}, u32[]{:S(2)}) %collective-permute-start.12) | collective-permute-done | bytes 98336 | tf_op jit(solution)/shard_map/ppermute | solution.py:26
  58.0 4.3 %collective-permute-done.8.refs_3_ = bf16[64,768]{1,0:T(8,128)(2,1)S(1)} collective-permute-done((bf16[64,768]{1,0:T(8,128)(2,1)S(1)}, bf16[64,768]{1,0:T(8,128)(2,1)S(1)}, u32[]{:S(2)}, u32[]{:S(2)}) %collective-permute-start.8) | collective-permute-done | bytes 98336 | tf_op jit(solution)/shard_map/ppermute | solution.py:26
  67.5 1.7 %collective-permute-start.19 = (bf16[128,384]{1,0:T(8,128)(2,1)S(1)}, bf16[128,384]{1,0:T(8,128)(2,1)S(1)}, u32[]{:S(2)}, u32[]{:S(2)}) collective-permute-start(bf16[128,384]{1,0:T(8,128)(2,1)S(1)} %shard_map.87.refs_0_), channel_id=1, source_target_pairs={{0,2},{1,3},{2,0},{3,1},{4,6},{5,7},{6,4},{7,5},{8,10},{9,11},{10,... | collective-permute-start | bytes 294920 | tf_op jit(solution)/shard_map/ppermute | solution.py:30
  70.3 1.9 %collective-permute-done.18.refs_1_ = bf16[128,384]{1,0:T(8,128)(2,1)S(1)} collective-permute-done((bf16[128,384]{1,0:T(8,128)(2,1)S(1)}, bf16[128,384]{1,0:T(8,128)(2,1)S(1)}, u32[]{:S(2)}, u32[]{:S(2)}) %collective-permute-start.18) | collective-permute-done | bytes 98336 | tf_op jit(solution)/shard_map/ppermute | solution.py:30
  73.4 1.3 %collective-permute-done.20.refs_3_ = bf16[128,384]{1,0:T(8,128)(2,1)S(1)} collective-permute-done((bf16[128,384]{1,0:T(8,128)(2,1)S(1)}, bf16[128,384]{1,0:T(8,128)(2,1)S(1)}, u32[]{:S(2)}, u32[]{:S(2)}) %collective-permute-start.20) | collective-permute-done | bytes 98336 | tf_op jit(solution)/shard_map/ppermute | solution.py:30
  83.3 2.7 %collective-permute-start.34 = (bf16[64,768]{1,0:T(8,128)(2,1)S(1)}, bf16[64,768]{1,0:T(8,128)(2,1)S(1)}, u32[]{:S(2)}, u32[]{:S(2)}) collective-permute-start(bf16[64,768]{1,0:T(8,128)(2,1)S(1)} %get-tuple-element.65.refs_0_.refs_13_.refs_2_), channel_id=1, source_target_pairs={{0,3},{1,2},{2,1},{3,0},{4,7},{5,6},{6,5},{7,4},{8,11},{9,10},{10,... | collective-permute-start | bytes 294920 | tf_op jit(solution)/shard_map/ppermute | solution.py:30
  90.0 2.9 %collective-permute-start.44 = (bf16[64,768]{1,0:T(8,128)(2,1)S(1)}, bf16[64,768]{1,0:T(8,128)(2,1)S(1)}, u32[]{:S(2)}, u32[]{:S(2)}) collective-permute-start(bf16[64,768]{1,0:T(8,128)(2,1)S(1)} %get-tuple-element.68.refs_1_), channel_id=1, source_target_pairs={{0,12},{4,0},{8,4},{12,8},{1,13},{5,1},{9,5},{13,9},{2,14},{6,2},{... | collective-permute-start | bytes 294920 | tf_op jit(solution)/shard_map/ppermute | solution.py:26
  93.8 1.4 %collective-permute-start.52 = (bf16[384,384]{1,0:T(8,128)(2,1)S(1)}, bf16[384,384]{1,0:T(8,128)(2,1)S(1)}, u32[]{:S(2)}, u32[]{:S(2)}) collective-permute-start(bf16[384,384]{1,0:T(8,128)(2,1)S(1)} %get-tuple-element.77), channel_id=1, source_target_pairs={{0,3},{1,2},{2,1},{3,0},{4,7},{5,6},{6,5},{7,4},{8,11},{9,10},{10,... | collective-permute-start | bytes 884744 | tf_op jit(solution)/shard_map/ppermute | solution.py:30
  98.5 2.0 %collective-permute-start.38 = (bf16[64,768]{1,0:T(8,128)(2,1)S(1)}, bf16[64,768]{1,0:T(8,128)(2,1)S(1)}, u32[]{:S(2)}, u32[]{:S(2)}) collective-permute-start(bf16[64,768]{1,0:T(8,128)(2,1)S(1)} %get-tuple-element.67.refs_2_), channel_id=1, source_target_pairs={{0,8},{4,12},{8,0},{12,4},{1,9},{5,13},{9,1},{13,5},{2,10},{6,14},... | collective-permute-start | bytes 294920 | tf_op jit(solution)/shard_map/ppermute | solution.py:26
  100.5 2.5 %collective-permute-done.51.refs_6_ = bf16[384,384]{1,0:T(8,128)(2,1)S(1)} collective-permute-done((bf16[384,384]{1,0:T(8,128)(2,1)S(1)}, bf16[384,384]{1,0:T(8,128)(2,1)S(1)}, u32[]{:S(2)}, u32[]{:S(2)}) %collective-permute-start.51) | collective-permute-done | bytes 294944 | tf_op jit(solution)/shard_map/ppermute | solution.py:30
  103.2 2.2 %collective-permute-done.36.refs_3_ = bf16[64,768]{1,0:T(8,128)(2,1)S(1)} collective-permute-done((bf16[64,768]{1,0:T(8,128)(2,1)S(1)}, bf16[64,768]{1,0:T(8,128)(2,1)S(1)}, u32[]{:S(2)}, u32[]{:S(2)}) %collective-permute-start.36) | collective-permute-done | bytes 98336 | tf_op jit(solution)/shard_map/ppermute | solution.py:26
  105.4 3.7 %collective-permute-done.38.refs_4_ = bf16[64,768]{1,0:T(8,128)(2,1)S(1)} collective-permute-done((bf16[64,768]{1,0:T(8,128)(2,1)S(1)}, bf16[64,768]{1,0:T(8,128)(2,1)S(1)}, u32[]{:S(2)}, u32[]{:S(2)}) %collective-permute-start.38) | collective-permute-done | bytes 98336 | tf_op jit(solution)/shard_map/ppermute | solution.py:26
  114.3 1.7 %collective-permute-start.48 = (bf16[128,384]{1,0:T(8,128)(2,1)S(1)}, bf16[128,384]{1,0:T(8,128)(2,1)S(1)}, u32[]{:S(2)}, u32[]{:S(2)}) collective-permute-start(bf16[128,384]{1,0:T(8,128)(2,1)S(1)} %shard_map.95.refs_0_), channel_id=1, source_target_pairs={{0,3},{1,2},{2,1},{3,0},{4,7},{5,6},{6,5},{7,4},{8,11},{9,10},{10,... | collective-permute-start | bytes 294920 | tf_op jit(solution)/shard_map/ppermute | solution.py:30
  116.1 1.6 %collective-permute-done.46.refs_1_ = bf16[128,384]{1,0:T(8,128)(2,1)S(1)} collective-permute-done((bf16[128,384]{1,0:T(8,128)(2,1)S(1)}, bf16[128,384]{1,0:T(8,128)(2,1)S(1)}, u32[]{:S(2)}, u32[]{:S(2)}) %collective-permute-start.46) | collective-permute-done | bytes 98336 | tf_op jit(solution)/shard_map/ppermute | solution.py:30
  117.7 2.9 %collective-permute-done.47.refs_2_ = bf16[128,384]{1,0:T(8,128)(2,1)S(1)} collective-permute-done((bf16[128,384]{1,0:T(8,128)(2,1)S(1)}, bf16[128,384]{1,0:T(8,128)(2,1)S(1)}, u32[]{:S(2)}, u32[]{:S(2)}) %collective-permute-start.47) | collective-permute-done | bytes 98336 | tf_op jit(solution)/shard_map/ppermute | solution.py:30
  121.4 1.4 %collective-permute-done.56.refs_3_ = bf16[128,768]{1,0:T(8,128)(2,1)S(1)} collective-permute-done((bf16[128,768]{1,0:T(8,128)(2,1)S(1)}, bf16[128,768]{1,0:T(8,128)(2,1)S(1)}, u32[]{:S(2)}, u32[]{:S(2)}) %collective-permute-start.56) | collective-permute-done | bytes 196640 | tf_op jit(solution)/shard_map/ppermute | solution.py:34
  (109 shorter events, 40.9 us)
Async XLA Ops:
  0.0 29.8 %collective-permute-start.3 = (bf16[3,1536,384]{2,1,0:T(8,128)(2,1)}, bf16[3,1536,384]{2,1,0:T(8,128)(2,1)S(1)}, u32[]{:S(2)}, u32[]{:S(2)}) collective-permute-start(bf16[3,1536,384]{2,1,0:T(8,128)(2,1)} %bitcast.8), channel_id=1, source_target_pairs={{0,16},{16,0},{1,17},{17,1},{2,18},{18,2},{3,19},{19,3},{4,20},{20... | collective-permute-start | bytes 10616840 | tf_op jit(solution)/shard_map/ppermute | solution.py:34
  0.5 78.5 %collective-permute-start.31 = (bf16[3,1536,384]{2,1,0:T(8,128)(2,1)}, bf16[3,1536,384]{2,1,0:T(8,128)(2,1)S(1)}, u32[]{:S(2)}, u32[]{:S(2)}) collective-permute-start(bf16[3,1536,384]{2,1,0:T(8,128)(2,1)} %bitcast.4), channel_id=1, source_target_pairs={{0,16},{16,0},{1,17},{17,1},{2,18},{18,2},{3,19},{19,3},{4,20},{20... | collective-permute-start | bytes 10616840 | tf_op jit(solution)/shard_map/ppermute | solution.py:34
  0.5 12.8 %collective-permute-start.21 = (bf16[384,1536]{1,0:T(8,128)(2,1)}, bf16[384,1536]{1,0:T(8,128)(2,1)S(1)}, u32[]{:S(2)}, u32[]{:S(2)}) collective-permute-start(bf16[384,1536]{1,0:T(8,128)(2,1)} %near_ref.2), channel_id=1, source_target_pairs={{0,16},{16,0},{1,17},{17,1},{2,18},{18,2},{3,19},{19,3},{4,20},{20... | collective-permute-start | bytes 3538952 | tf_op jit(solution)/shard_map/ppermute | solution.py:34
  2.0 17.2 %collective-permute-start = (bf16[64,768]{1,0:T(8,128)(2,1)S(1)}, bf16[64,768]{1,0:T(8,128)(2,1)S(1)}, u32[]{:S(2)}, u32[]{:S(2)}) collective-permute-start(bf16[64,768]{1,0:T(8,128)(2,1)S(1)} %get-tuple-element.43.refs_0_.refs_12_), channel_id=1, source_target_pairs={{0,1},{1,0},{2,3},{3,2},{4,5},{5,4},{6,7},{7,6},{8,9},{9,8},{10,11... | collective-permute-start | bytes 294920 | tf_op jit(solution)/shard_map/ppermute | solution.py:30
  14.8 25.8 %collective-permute-start.22 = (bf16[384,384]{1,0:T(8,128)(2,1)S(1)}, bf16[384,384]{1,0:T(8,128)(2,1)S(1)}, u32[]{:S(2)}, u32[]{:S(2)}) collective-permute-start(bf16[384,384]{1,0:T(8,128)(2,1)S(1)} %get-tuple-element.59), channel_id=1, source_target_pairs={{0,1},{1,0},{2,3},{3,2},{4,5},{5,4},{6,7},{7,6},{8,9},{9,8},{10,11... | collective-permute-start | bytes 884744 | tf_op jit(solution)/shard_map/ppermute | solution.py:30
  19.2 9.9 %collective-permute-start.2 = (bf16[64,768]{1,0:T(8,128)(2,1)S(1)}, bf16[64,768]{1,0:T(8,128)(2,1)S(1)}, u32[]{:S(2)}, u32[]{:S(2)}) collective-permute-start(bf16[64,768]{1,0:T(8,128)(2,1)S(1)} %get-tuple-element.43.refs_0_.refs_12_), channel_id=1, source_target_pairs={{0,3},{1,2},{2,1},{3,0},{4,7},{5,6},{6,5},{7,4},{8,11},{9,10},{10,... | collective-permute-start | bytes 294920 | tf_op jit(solution)/shard_map/ppermute | solution.py:30
  22.3 13.5 %collective-permute-start.4 = (bf16[64,768]{1,0:T(8,128)(2,1)S(1)}, bf16[64,768]{1,0:T(8,128)(2,1)S(1)}, u32[]{:S(2)}, u32[]{:S(2)}) collective-permute-start(bf16[64,768]{1,0:T(8,128)(2,1)S(1)} %get-tuple-element.49.refs_0_.refs_13_), channel_id=1, source_target_pairs={{0,1},{1,0},{2,3},{3,2},{4,5},{5,4},{6,7},{7,6},{8,9},{9,8},{10,11... | collective-permute-start | bytes 294920 | tf_op jit(solution)/shard_map/ppermute | solution.py:30
  29.1 7.3 %collective-permute-start.5 = (bf16[64,768]{1,0:T(8,128)(2,1)S(1)}, bf16[64,768]{1,0:T(8,128)(2,1)S(1)}, u32[]{:S(2)}, u32[]{:S(2)}) collective-permute-start(bf16[64,768]{1,0:T(8,128)(2,1)S(1)} %get-tuple-element.49.refs_0_.refs_13_), channel_id=1, source_target_pairs={{0,2},{1,3},{2,0},{3,1},{4,6},{5,7},{6,4},{7,5},{8,10},{9,11},{10,... | collective-permute-start | bytes 294920 | tf_op jit(solution)/shard_map/ppermute | solution.py:30
  29.8 8.2 %collective-permute-start.6 = (bf16[64,768]{1,0:T(8,128)(2,1)S(1)}, bf16[64,768]{1,0:T(8,128)(2,1)S(1)}, u32[]{:S(2)}, u32[]{:S(2)}) collective-permute-start(bf16[64,768]{1,0:T(8,128)(2,1)S(1)} %get-tuple-element.49.refs_0_.refs_13_), channel_id=1, source_target_pairs={{0,3},{1,2},{2,1},{3,0},{4,7},{5,6},{6,5},{7,4},{8,11},{9,10},{10,... | collective-permute-start | bytes 294920 | tf_op jit(solution)/shard_map/ppermute | solution.py:30
  35.8 16.1 %collective-permute-start.23 = (bf16[384,384]{1,0:T(8,128)(2,1)S(1)}, bf16[384,384]{1,0:T(8,128)(2,1)S(1)}, u32[]{:S(2)}, u32[]{:S(2)}) collective-permute-start(bf16[384,384]{1,0:T(8,128)(2,1)S(1)} %get-tuple-element.60), channel_id=1, source_target_pairs={{0,2},{1,3},{2,0},{3,1},{4,6},{5,7},{6,4},{7,5},{8,10},{9,11},{10,... | collective-permute-start | bytes 884744 | tf_op jit(solution)/shard_map/ppermute | solution.py:30
  38.0 6.9 %collective-permute-start.15 = (bf16[64,768]{1,0:T(8,128)(2,1)S(1)}, bf16[64,768]{1,0:T(8,128)(2,1)S(1)}, u32[]{:S(2)}, u32[]{:S(2)}) collective-permute-start(bf16[64,768]{1,0:T(8,128)(2,1)S(1)} %get-tuple-element.52.refs_1_), channel_id=1, source_target_pairs={{0,8},{4,12},{8,0},{12,4},{1,9},{5,13},{9,1},{13,5},{2,10},{6,14},... | collective-permute-start | bytes 294920 | tf_op jit(solution)/shard_map/ppermute | solution.py:26
  40.6 11.4 %collective-permute-start.24 = (bf16[384,384]{1,0:T(8,128)(2,1)S(1)}, bf16[384,384]{1,0:T(8,128)(2,1)S(1)}, u32[]{:S(2)}, u32[]{:S(2)}) collective-permute-start(bf16[384,384]{1,0:T(8,128)(2,1)S(1)} %get-tuple-element.61), channel_id=1, source_target_pairs={{0,3},{1,2},{2,1},{3,0},{4,7},{5,6},{6,5},{7,4},{8,11},{9,10},{10,... | collective-permute-start | bytes 884744 | tf_op jit(solution)/shard_map/ppermute | solution.py:30
  42.9 44.5 %collective-permute-start.49 = (bf16[384,1536]{1,0:T(8,128)(2,1)S(1)}, bf16[384,1536]{1,0:T(8,128)(2,1)S(1)}, u32[]{:S(2)}, u32[]{:S(2)}) collective-permute-start(bf16[384,1536]{1,0:T(8,128)(2,1)S(1)} %copy-done.3), channel_id=1, source_target_pairs={{0,16},{16,0},{1,17},{17,1},{2,18},{18,2},{3,19},{19,3},{4,20},{20... | collective-permute-start | bytes 3538952 | tf_op jit(solution)/shard_map/ppermute | solution.py:34
  51.9 13.1 %collective-permute-start.17 = (bf16[256,768]{1,0:T(8,128)(2,1)S(1)}, bf16[256,768]{1,0:T(8,128)(2,1)S(1)}, u32[]{:S(2)}, u32[]{:S(2)}) collective-permute-start(bf16[256,768]{1,0:T(8,128)(2,1)S(1)} %get-tuple-element.53), channel_id=1, source_target_pairs={{0,16},{16,0},{1,17},{17,1},{2,18},{18,2},{3,19},{19,3},{4,20},{20... | collective-permute-start | bytes 1179656 | tf_op jit(solution)/shard_map/ppermute | solution.py:34
  76.7 6.6 %collective-permute-start.29 = (bf16[64,768]{1,0:T(8,128)(2,1)S(1)}, bf16[64,768]{1,0:T(8,128)(2,1)S(1)}, u32[]{:S(2)}, u32[]{:S(2)}) collective-permute-start(bf16[64,768]{1,0:T(8,128)(2,1)S(1)} %get-tuple-element.63.refs_0_.refs_12_.refs_1_), channel_id=1, source_target_pairs={{0,2},{1,3},{2,0},{3,1},{4,6},{5,7},{6,4},{7,5},{8,10},{9,11},{10,... | collective-permute-start | bytes 294920 | tf_op jit(solution)/shard_map/ppermute | solution.py:30
  77.9 8.1 %collective-permute-start.30 = (bf16[64,768]{1,0:T(8,128)(2,1)S(1)}, bf16[64,768]{1,0:T(8,128)(2,1)S(1)}, u32[]{:S(2)}, u32[]{:S(2)}) collective-permute-start(bf16[64,768]{1,0:T(8,128)(2,1)S(1)} %get-tuple-element.63.refs_0_.refs_12_.refs_1_), channel_id=1, source_target_pairs={{0,3},{1,2},{2,1},{3,0},{4,7},{5,6},{6,5},{7,4},{8,11},{9,10},{10,... | collective-permute-start | bytes 294920 | tf_op jit(solution)/shard_map/ppermute | solution.py:30
  79.0 9.9 %collective-permute-start.32 = (bf16[64,768]{1,0:T(8,128)(2,1)S(1)}, bf16[64,768]{1,0:T(8,128)(2,1)S(1)}, u32[]{:S(2)}, u32[]{:S(2)}) collective-permute-start(bf16[64,768]{1,0:T(8,128)(2,1)S(1)} %get-tuple-element.65.refs_0_.refs_13_.refs_2_), channel_id=1, source_target_pairs={{0,1},{1,0},{2,3},{3,2},{4,5},{5,4},{6,7},{7,6},{8,9},{9,8},{10,11... | collective-permute-start | bytes 294920 | tf_op jit(solution)/shard_map/ppermute | solution.py:30
  81.2 8.8 %collective-permute-start.33 = (bf16[64,768]{1,0:T(8,128)(2,1)S(1)}, bf16[64,768]{1,0:T(8,128)(2,1)S(1)}, u32[]{:S(2)}, u32[]{:S(2)}) collective-permute-start(bf16[64,768]{1,0:T(8,128)(2,1)S(1)} %get-tuple-element.65.refs_0_.refs_13_.refs_2_), channel_id=1, source_target_pairs={{0,2},{1,3},{2,0},{3,1},{4,6},{5,7},{6,4},{7,5},{8,10},{9,11},{10,... | collective-permute-start | bytes 294920 | tf_op jit(solution)/shard_map/ppermute | solution.py:30
  83.3 9.6 %collective-permute-start.34 = (bf16[64,768]{1,0:T(8,128)(2,1)S(1)}, bf16[64,768]{1,0:T(8,128)(2,1)S(1)}, u32[]{:S(2)}, u32[]{:S(2)}) collective-permute-start(bf16[64,768]{1,0:T(8,128)(2,1)S(1)} %get-tuple-element.65.refs_0_.refs_13_.refs_2_), channel_id=1, source_target_pairs={{0,3},{1,2},{2,1},{3,0},{4,7},{5,6},{6,5},{7,4},{8,11},{9,10},{10,... | collective-permute-start | bytes 294920 | tf_op jit(solution)/shard_map/ppermute | solution.py:30
  87.3 6.5 %collective-permute-start.42 = (bf16[64,768]{1,0:T(8,128)(2,1)S(1)}, bf16[64,768]{1,0:T(8,128)(2,1)S(1)}, u32[]{:S(2)}, u32[]{:S(2)}) collective-permute-start(bf16[64,768]{1,0:T(8,128)(2,1)S(1)} %get-tuple-element.68.refs_1_), channel_id=1, source_target_pairs={{0,4},{4,8},{8,12},{12,0},{1,5},{5,9},{9,13},{13,1},{2,6},{6,10},{... | collective-permute-start | bytes 294920 | tf_op jit(solution)/shard_map/ppermute | solution.py:26
  87.6 10.9 %collective-permute-start.50 = (bf16[384,384]{1,0:T(8,128)(2,1)S(1)}, bf16[384,384]{1,0:T(8,128)(2,1)S(1)}, u32[]{:S(2)}, u32[]{:S(2)}) collective-permute-start(bf16[384,384]{1,0:T(8,128)(2,1)S(1)} %get-tuple-element.75), channel_id=1, source_target_pairs={{0,1},{1,0},{2,3},{3,2},{4,5},{5,4},{6,7},{7,6},{8,9},{9,8},{10,11... | collective-permute-start | bytes 884744 | tf_op jit(solution)/shard_map/ppermute | solution.py:30
  88.9 8.3 %collective-permute-start.43 = (bf16[64,768]{1,0:T(8,128)(2,1)S(1)}, bf16[64,768]{1,0:T(8,128)(2,1)S(1)}, u32[]{:S(2)}, u32[]{:S(2)}) collective-permute-start(bf16[64,768]{1,0:T(8,128)(2,1)S(1)} %get-tuple-element.68.refs_1_), channel_id=1, source_target_pairs={{0,8},{4,12},{8,0},{12,4},{1,9},{5,13},{9,1},{13,5},{2,10},{6,14},... | collective-permute-start | bytes 294920 | tf_op jit(solution)/shard_map/ppermute | solution.py:26
  90.0 7.1 %collective-permute-start.44 = (bf16[64,768]{1,0:T(8,128)(2,1)S(1)}, bf16[64,768]{1,0:T(8,128)(2,1)S(1)}, u32[]{:S(2)}, u32[]{:S(2)}) collective-permute-start(bf16[64,768]{1,0:T(8,128)(2,1)S(1)} %get-tuple-element.68.refs_1_), channel_id=1, source_target_pairs={{0,12},{4,0},{8,4},{12,8},{1,13},{5,1},{9,5},{13,9},{2,14},{6,2},{... | collective-permute-start | bytes 294920 | tf_op jit(solution)/shard_map/ppermute | solution.py:26
  92.9 10.2 %collective-permute-start.51 = (bf16[384,384]{1,0:T(8,128)(2,1)S(1)}, bf16[384,384]{1,0:T(8,128)(2,1)S(1)}, u32[]{:S(2)}, u32[]{:S(2)}) collective-permute-start(bf16[384,384]{1,0:T(8,128)(2,1)S(1)} %get-tuple-element.76), channel_id=1, source_target_pairs={{0,2},{1,3},{2,0},{3,1},{4,6},{5,7},{6,4},{7,5},{8,10},{9,11},{10,... | collective-permute-start | bytes 884744 | tf_op jit(solution)/shard_map/ppermute | solution.py:30
  93.8 9.3 %collective-permute-start.52 = (bf16[384,384]{1,0:T(8,128)(2,1)S(1)}, bf16[384,384]{1,0:T(8,128)(2,1)S(1)}, u32[]{:S(2)}, u32[]{:S(2)}) collective-permute-start(bf16[384,384]{1,0:T(8,128)(2,1)S(1)} %get-tuple-element.77), channel_id=1, source_target_pairs={{0,3},{1,2},{2,1},{3,0},{4,7},{5,6},{6,5},{7,4},{8,11},{9,10},{10,... | collective-permute-start | bytes 884744 | tf_op jit(solution)/shard_map/ppermute | solution.py:30
  97.7 12.8 %collective-permute-start.45 = (bf16[256,768]{1,0:T(8,128)(2,1)S(1)}, bf16[256,768]{1,0:T(8,128)(2,1)S(1)}, u32[]{:S(2)}, u32[]{:S(2)}) collective-permute-start(bf16[256,768]{1,0:T(8,128)(2,1)S(1)} %get-tuple-element.69), channel_id=1, source_target_pairs={{0,16},{16,0},{1,17},{17,1},{2,18},{18,2},{3,19},{19,3},{4,20},{20... | collective-permute-start | bytes 1179656 | tf_op jit(solution)/shard_map/ppermute | solution.py:34
  97.7 7.6 %collective-permute-start.36 = (bf16[64,768]{1,0:T(8,128)(2,1)S(1)}, bf16[64,768]{1,0:T(8,128)(2,1)S(1)}, u32[]{:S(2)}, u32[]{:S(2)}) collective-permute-start(bf16[64,768]{1,0:T(8,128)(2,1)S(1)} %get-tuple-element.67.refs_2_), channel_id=1, source_target_pairs={{0,4},{4,8},{8,12},{12,0},{1,5},{5,9},{9,13},{13,1},{2,6},{6,10},{... | collective-permute-start | bytes 294920 | tf_op jit(solution)/shard_map/ppermute | solution.py:26
  98.5 10.6 %collective-permute-start.38 = (bf16[64,768]{1,0:T(8,128)(2,1)S(1)}, bf16[64,768]{1,0:T(8,128)(2,1)S(1)}, u32[]{:S(2)}, u32[]{:S(2)}) collective-permute-start(bf16[64,768]{1,0:T(8,128)(2,1)S(1)} %get-tuple-element.67.refs_2_), channel_id=1, source_target_pairs={{0,8},{4,12},{8,0},{12,4},{1,9},{5,13},{9,1},{13,5},{2,10},{6,14},... | collective-permute-start | bytes 294920 | tf_op jit(solution)/shard_map/ppermute | solution.py:26
  105.4 9.0 %collective-permute-start.53 = (bf16[384,384]{1,0:T(8,128)(2,1)S(1)}, bf16[384,384]{1,0:T(8,128)(2,1)S(1)}, u32[]{:S(2)}, u32[]{:S(2)}) collective-permute-start(bf16[384,384]{1,0:T(8,128)(2,1)S(1)} %collective-permute-done.50.refs_5_), channel_id=1, source_target_pairs={{0,16},{16,0},{1,17},{17,1},{2,18},{18,2},{3,19},{19,3},{4,20},{20... | collective-permute-start | bytes 884744 | tf_op jit(solution)/shard_map/ppermute | solution.py:34
  109.1 6.9 %collective-permute-start.54 = (bf16[384,384]{1,0:T(8,128)(2,1)S(1)}, bf16[384,384]{1,0:T(8,128)(2,1)S(1)}, u32[]{:S(2)}, u32[]{:S(2)}) collective-permute-start(bf16[384,384]{1,0:T(8,128)(2,1)S(1)} %collective-permute-done.51.refs_6_), channel_id=1, source_target_pairs={{0,16},{16,0},{1,17},{17,1},{2,18},{18,2},{3,19},{19,3},{4,20},{20... | collective-permute-start | bytes 884744 | tf_op jit(solution)/shard_map/ppermute | solution.py:34
  109.6 6.5 %collective-permute-start.55 = (bf16[384,384]{1,0:T(8,128)(2,1)S(1)}, bf16[384,384]{1,0:T(8,128)(2,1)S(1)}, u32[]{:S(2)}, u32[]{:S(2)}) collective-permute-start(bf16[384,384]{1,0:T(8,128)(2,1)S(1)} %collective-permute-done.52.refs_7_), channel_id=1, source_target_pairs={{0,16},{16,0},{1,17},{17,1},{2,18},{18,2},{3,19},{19,3},{4,20},{20... | collective-permute-start | bytes 884744 | tf_op jit(solution)/shard_map/ppermute | solution.py:34
  113.7 6.9 %collective-permute-start.47 = (bf16[128,384]{1,0:T(8,128)(2,1)S(1)}, bf16[128,384]{1,0:T(8,128)(2,1)S(1)}, u32[]{:S(2)}, u32[]{:S(2)}) collective-permute-start(bf16[128,384]{1,0:T(8,128)(2,1)S(1)} %shard_map.95.refs_0_), channel_id=1, source_target_pairs={{0,2},{1,3},{2,0},{3,1},{4,6},{5,7},{6,4},{7,5},{8,10},{9,11},{10,... | collective-permute-start | bytes 294920 | tf_op jit(solution)/shard_map/ppermute | solution.py:30
  (29 other events, 144.9 us)
